TPU v7x, 256 devices: a whole 4x4x8 slice. The times are simulated.
256 devices in a mesh: panel: 2 (over core), ang: 32 (over z, x), rad: 4 (over y).
Axes of the slice: x: 4, y: 4, z: 8, core: 2. Of those that a mesh axis runs over, the one named last changes fastest.
Arguments:
- density: float32 [2, 8, 512, 512], P('panel', 'rad', 'ang'), may hold values from 1 to 2
- momentum: float32 [2, 3, 8, 512, 512], P('panel', None, 'rad', 'ang'), may hold values from -2.5 to 2.5
- magnetic: float32 [2, 3, 8, 512, 512], P('panel', None, 'rad', 'ang'), may hold values from -2.5 to 2.5
- partner_device: int32 [2, 1024, 1], P('panel', 'ang'), may hold values from 0 to 31; in each aligned block of 32 rows (0 to 31, 32 to 63, ..., all dimensions but the last counted through in order) at most 2 rows name the same one
- partner_phi: int32 [2, 1024], P('panel', 'ang'), may hold values from 0 to 14
- partner_theta: int32 [2, 1024], P('panel', 'ang'), may hold values from 0 to 510
- partner_weight: float32 [2, 1024, 4], P('panel', 'ang'), may hold values from 0 to 1, as said below
- border_turn: float32 [2, 1024], P('panel', 'ang'), may hold values from -3.140625 to 3.140625
Outputs:
- density_next: float32 [2, 8, 512, 512], P('panel', 'rad', 'ang')
- momentum_next: float32 [2, 3, 8, 512, 512], P('panel', None, 'rad', 'ang')
- magnetic_next: float32 [2, 3, 8, 512, 512], P('panel', None, 'rad', 'ang')
Inputs may be any that keep to these rules, and one draw needn't show every extreme that they name: `partner_device`: within the 32 table rows of one device (aligned blocks), at most 2 rows name the same source device. `partner_weight`: each row's weights are (1-u)(1-v), (1-u)v, u(1-v), uv for some u, v in [0, 1].
All inputs are finite; a program needn't handle non-finite values.
Results may differ from a plain program's by a relative error of at most 0.00005.
Values sent between devices are 32-bit elements; how exact they have to be, the bound alone decides.
No kernel may reach another device: no remote copies, remote signals or barrier semaphores. Data moves between devices by JAX's collectives and lax.ppermute only.
A program may use at most 64 MiB of HBM per device.

v0:
```python
import math

import jax
import jax.numpy as jnp
from jax import lax
from jax.sharding import PartitionSpec as P

time_step = 0.15
sound_sq = 1.0
viscosity = 0.1
resistivity = 0.1
r_inner = 0.35


def swapped(block, axis, apart):
    count = lax.axis_size(axis)
    route = []
    for low in range(count):
        high = low | 1 << apart
        if high != low and high < count:
            route += [(low, high), (high, low)]
    return lax.ppermute(block, axis, route)


def padded(value, sides, width):
    for axis, dim in sides:
        size, length = (lax.axis_size(axis), value.shape[dim])
        up = [(i, (i + 1) % size) for i in range(size - 1)]
        down = [(j, i) for i, j in up]
        last = lax.slice_in_dim(value, length - width, length, axis=dim)
        first = lax.slice_in_dim(value, 0, width, axis=dim)
        before = lax.ppermute(last, axis, up)
        after = lax.ppermute(first, axis, down)
        value = jnp.concatenate([before, value, after], axis=dim)
    return value


def field_of(block, index):
    return block[..., index, :, :, :]


def fluxes(block, direction):
    mass_field = field_of(block, 0)
    moment = [field_of(block, 1 + component) for component in range(3)]
    magnet = [field_of(block, 4 + component) for component in range(3)]
    velocity = [moment[component] / mass_field for component in range(3)]
    pressure = sound_sq * mass_field + 0.5 * (
        magnet[0] * magnet[0] + magnet[1] * magnet[1] + magnet[2] * magnet[2]
    )
    pieces = [moment[direction]]
    for component in range(3):
        flux_term = moment[component] * velocity[direction] - magnet[component] * magnet[direction]
        if component == direction:
            flux_term = flux_term + pressure
        pieces.append(flux_term)
    for component in range(3):
        pieces.append(
            velocity[direction] * magnet[component] - magnet[direction] * velocity[component]
        )
    return jnp.stack(pieces, axis=-4)


def tendency(current, radial, polar, azimuth, half_t, half_p, sq_t, sq_p):
    flux_r = fluxes(radial, 0)
    flux_t = fluxes(polar, 1)
    flux_p = fluxes(azimuth, 2)
    divergence = (flux_r[..., 2:, :, :] - flux_r[..., :-2, :, :]) * 0.5
    divergence = divergence + (flux_t[..., 2:] - flux_t[..., :-2]) * half_t
    divergence = divergence + (flux_p[..., :, 2:, :] - flux_p[..., :, :-2, :]) * half_p
    laplace_sum = radial[..., 2:, :, :] - 2.0 * current + radial[..., :-2, :, :]
    laplace_sum = laplace_sum + (polar[..., 2:] - 2.0 * current + polar[..., :-2]) * sq_t
    laplace_sum = (
        laplace_sum + (azimuth[..., :, 2:, :] - 2.0 * current + azimuth[..., :, :-2, :]) * sq_p
    )
    mixing = jnp.array(
        [0.0, viscosity, viscosity, viscosity, resistivity, resistivity, resistivity], jnp.float32
    ).reshape(7, 1, 1, 1)
    return mixing * laplace_sum - divergence


def turn_frame(ghost, cosine, sine):
    pieces = [ghost[0], ghost[1]]
    pieces.append(cosine * ghost[2] + sine * ghost[3])
    pieces.append(cosine * ghost[3] - sine * ghost[2])
    pieces.append(ghost[4])
    pieces.append(cosine * ghost[5] + sine * ghost[6])
    pieces.append(cosine * ghost[6] - sine * ghost[5])
    return jnp.stack(pieces, axis=0)


def route_request(packed):
    crossed = swapped(packed, "panel", 0)
    return lax.all_to_all(crossed, "ang", split_axis=0, concat_axis=0, tiled=True)


def route_reply(answer):
    crossed = swapped(answer, "panel", 0)
    return lax.all_to_all(crossed, "ang", split_axis=1, concat_axis=1, tiled=True)


def body(
    density,
    momentum,
    magnetic,
    partner_device,
    partner_phi,
    partner_theta,
    partner_weight,
    border_turn,
):
    fields_now = jnp.concatenate([density, momentum[0], magnetic[0]], axis=0)
    fields, rows_r, rows_p, rows_t = fields_now.shape
    n_ang = lax.axis_size("ang")
    n_rad = lax.axis_size("rad")
    border = partner_phi.shape[1]
    capacity = max(2, 2 * border // n_ang)
    slot_count = n_ang * capacity
    stacked_rows = fields * rows_r
    highest = lax.Precision.HIGHEST
    level = lax.axis_index("rad") * rows_r + jnp.arange(rows_r, dtype=jnp.int32)
    radius = r_inner + (level.astype(jnp.float32) + 0.5) * ((1.0 - r_inner) / (rows_r * n_rad))
    colatitude = math.pi / 4 + (jnp.arange(rows_t).astype(jnp.float32) + 0.5) * (
        math.pi / 2 / rows_t
    )
    inv_radius = (1.0 / radius).reshape(rows_r, 1, 1)
    inv_both = inv_radius / jnp.sin(colatitude)
    half_t = 0.5 * inv_radius
    half_p = 0.5 * inv_both
    sq_t = inv_radius * inv_radius
    sq_p = inv_both * inv_both
    mirror = jnp.array([1.0, -1.0, -1.0, -1.0, 1.0, 1.0, 1.0], jnp.float32).reshape(7, 1, 1, 1)
    first_r = lax.axis_index("rad") == 0
    last_r = lax.axis_index("rad") == n_rad - 1
    first_p = lax.axis_index("ang") == 0
    last_p = lax.axis_index("ang") == n_ang - 1
    source_ang = partner_device[0, :, 0]
    one_hot = (source_ang[:, None] == jnp.arange(n_ang, dtype=jnp.int32)[None, :]).astype(jnp.int32)
    ranked = jnp.sum(one_hot * (jnp.cumsum(one_hot, axis=0) - 1), axis=1)
    target_slot = source_ang * capacity + ranked
    placing = (jnp.arange(slot_count, dtype=jnp.int32)[:, None] == target_slot[None, :]).astype(
        jnp.float32
    )
    base_cell = (partner_phi[0] * rows_t + partner_theta[0]).astype(jnp.float32)
    weights = partner_weight[0]
    payload = base_cell[:, None]
    packed = jnp.dot(placing, payload, precision=highest).reshape(n_ang, capacity, payload.shape[1])
    asked = route_request(packed)
    cell_index = (asked[:, :, 0].reshape(slot_count) + 0.5).astype(jnp.int32)
    offsets = jnp.array([0, 1, rows_t, rows_t + 1], jnp.int32)
    gather_index = (cell_index[:, None] + offsets[None, :]).reshape(slot_count * 4)
    cosine = jnp.cos(border_turn[0])
    sine = jnp.sin(border_turn[0])

    def overset(current):
        table = current.reshape(stacked_rows, rows_p * rows_t)
        corner = jnp.take(table, gather_index, axis=1).reshape(stacked_rows, slot_count, 4)
        returned = route_reply(corner.reshape(stacked_rows, n_ang, capacity, 4)).reshape(
            stacked_rows, slot_count, 4
        )
        picked = [jnp.dot(returned[:, :, index], placing, precision=highest) for index in range(4)]
        ghost = weights[:, 0] * picked[0] + weights[:, 1] * picked[1]
        ghost = ghost + weights[:, 2] * picked[2]
        ghost = ghost + weights[:, 3] * picked[3]
        ghost = turn_frame(ghost.reshape(fields, rows_r, border), cosine, sine)
        return (ghost[:, :, :rows_p], ghost[:, :, rows_p:])

    def evaluate(current):
        haloed = padded(current, (("ang", 2), ("rad", 1)), 1)
        lower_r = jnp.where(first_r, mirror * current[:, :1], haloed[:, :1, 1:-1])
        upper_r = jnp.where(last_r, mirror * current[:, -1:], haloed[:, -1:, 1:-1])
        lower_p = jnp.where(first_p, mirror * current[:, :, :1], haloed[:, 1:-1, :1])
        upper_p = jnp.where(last_p, mirror * current[:, :, -1:], haloed[:, 1:-1, -1:])
        radial = jnp.concatenate([lower_r, current, upper_r], axis=1)
        azimuth = jnp.concatenate([lower_p, current, upper_p], axis=2)
        lower_t, upper_t = overset(current)
        polar = jnp.concatenate([lower_t[..., None], current, upper_t[..., None]], axis=3)
        return tendency(current, radial, polar, azimuth, half_t, half_p, sq_t, sq_p)

    slope_one = evaluate(fields_now)
    slope_two = evaluate(fields_now + 0.5 * time_step * slope_one)
    slope_three = evaluate(fields_now + 0.5 * time_step * slope_two)
    slope_four = evaluate(fields_now + time_step * slope_three)
    updated = fields_now + time_step / 6.0 * (
        slope_one + 2.0 * slope_two + 2.0 * slope_three + slope_four
    )
    return (updated[0:1], updated[1:4][None], updated[4:7][None])


def solution(mesh):
    in_specs = (
        P("panel", "rad", "ang", None),
        P("panel", None, "rad", "ang", None),
        P("panel", None, "rad", "ang", None),
        P("panel", "ang", None),
        P("panel", "ang"),
        P("panel", "ang"),
        P("panel", "ang", None),
        P("panel", "ang"),
    )
    out_specs = (
        P("panel", "rad", "ang", None),
        P("panel", None, "rad", "ang", None),
        P("panel", None, "rad", "ang", None),
    )
    return jax.shard_map(body, mesh=mesh, in_specs=in_specs, out_specs=out_specs, check_vma=False)
```

profile of v0, /device:TPU:2, one launch (start us, length us, event | category | flops | bytes accessed | tf_op | source)
XLA Modules:
  0.0 199.3 jit_solution(3785506237722466291)
XLA Ops:
  1.8 4.3 %collective-permute-start.1 = (f32[7,2,1,512]{3,2,1,0:T(1,128)S(1)}, f32[7,2,1,512]{3,2,1,0:T(1,128)S(1)}, u32[]{:S(2)}, u32[]{:S(2)}) collective-permute-start(f32[7,2,1,512]{3,2,1,0:T(1,128)S(1)} %get-tuple-element.75), channel_id=1, source_target_pairs={{4,0},{8,4},{12,8},{16,12},{20,16},{24,20},{28,24},{32,28},{36,32}... | collective-permute-start | bytes 86024 | tf_op jit(solution)/shard_map/ppermute | solution.py:33
  13.2 13.2 %all-to-all-start = ((f32[32,2,1]{1,2,0:T(1,128)}), f32[32,2,1]{1,2,0:T(1,128)S(1)}, u32[]{:S(2)}, u32[]{:S(2)}) async-start(f32[32,2,1]{1,2,0:T(1,128)} %copy.59), calls=%async_computation | async-start | bytes 32768 | tf_op jit(solution)/shard_map/all_to_all | solution.py:93
  27.5 2.7 %copy.60 = f32[14,8192]{0,1:T(8,128)} copy(f32[14,8192]{1,0:T(8,128)S(1)} %bitcast.210) | data formatting | bytes 917504 | tf_op jit(solution)/shard_map/reshape | solution.py:155
  30.2 4.7 %all-to-all-done = f32[32,2,1]{1,2,0:T(1,128)S(1)} async-done(((f32[32,2,1]{1,2,0:T(1,128)}), f32[32,2,1]{1,2,0:T(1,128)S(1)}, u32[]{:S(2)}, u32[]{:S(2)}) %all-to-all-start) | async-done | bytes 288 | tf_op jit(solution)/shard_map/all_to_all | solution.py:93
  35.3 2.9 %gather_fusion = f32[256,14]{1,0:T(8,128)S(1)} fusion(f32[14,8192]{0,1:T(8,128)} %copy.60, s32[1024]{0:T(1024)S(1)} %pad_clamp_fusion), kind=kCustom, calls=%fused_computation.clone | custom fusion | bytes 29696 | tf_op jit(solution)/shard_map/jit(_take)/gather | solution.py:156
  39.9 5.1 %all-to-all-start.1 = ((f32[14,32,2,4]{0,3,2,1:T(4,128)}), f32[14,32,2,4]{0,3,2,1:T(4,128)S(1)}, u32[]{:S(2)}, u32[]{:S(2)}) async-start(f32[14,32,2,4]{0,3,2,1:T(4,128)} %collective-permute-done.5), calls=%async_computation.1 | async-start | bytes 262144 | tf_op jit(solution)/shard_map/all_to_all | solution.py:98
  46.4 4.2 %collective-permute-start.3 = (f32[7,1,18,512]{3,2,1,0:T(8,128)}, f32[7,1,18,512]{3,2,1,0:T(8,128)}, u32[]{:S(2)}, u32[]{:S(2)}) collective-permute-start(f32[7,1,18,512]{3,2,1,0:T(8,128)} %get-tuple-element.40), channel_id=1, source_target_pairs={{0,1},{1,2},{2,3},{4,5},{5,6},{6,7},{8,9},{9,10},{10,11},{12,13},{... | collective-permute-start | bytes 774152 | tf_op jit(solution)/shard_map/ppermute | solution.py:32
  57.4 4.6 %collective-permute-done.2 = f32[7,1,18,512]{3,2,1,0:T(8,128)} collective-permute-done((f32[7,1,18,512]{3,2,1,0:T(8,128)S(1)}, f32[7,1,18,512]{3,2,1,0:T(8,128)}, u32[]{:S(2)}, u32[]{:S(2)}) %collective-permute-start.2) | collective-permute-done | bytes 258080 | tf_op jit(solution)/shard_map/ppermute | solution.py:33
  64.4 2.5 %collective-permute-start.7 = (f32[7,2,1,512]{3,2,1,0:T(1,128)S(1)}, f32[7,2,1,512]{3,2,1,0:T(1,128)S(1)}, u32[]{:S(2)}, u32[]{:S(2)}) collective-permute-start(f32[7,2,1,512]{3,2,1,0:T(1,128)S(1)} %get-tuple-element.71), channel_id=1, source_target_pairs={{4,0},{8,4},{12,8},{16,12},{20,16},{24,20},{28,24},{32,28},{36,32}... | collective-permute-start | bytes 86024 | tf_op jit(solution)/shard_map/ppermute | solution.py:33
  67.0 3.3 %collective-permute-start.6 = (f32[7,2,1,512]{3,2,1,0:T(1,128)S(1)}, f32[7,2,1,512]{3,2,1,0:T(1,128)S(1)}, u32[]{:S(2)}, u32[]{:S(2)}) collective-permute-start(f32[7,2,1,512]{3,2,1,0:T(1,128)S(1)} %get-tuple-element.70), channel_id=1, source_target_pairs={{0,4},{4,8},{8,12},{12,16},{16,20},{20,24},{24,28},{28,32},{32,36}... | collective-permute-start | bytes 86024 | tf_op jit(solution)/shard_map/ppermute | solution.py:32
  70.7 2.7 %copy.65 = f32[14,8192]{0,1:T(8,128)} copy(f32[14,8192]{1,0:T(8,128)S(1)} %bitcast.211) | data formatting | bytes 917504 | tf_op jit(solution)/shard_map/reshape | solution.py:155
  73.3 2.9 %gather_fusion.1 = f32[256,14]{1,0:T(8,128)S(1)} fusion(f32[14,8192]{0,1:T(8,128)} %copy.65, s32[1024]{0:T(1024)S(1)} %pad_clamp_fusion), kind=kCustom, calls=%fused_computation.1.clone | custom fusion | bytes 29696 | tf_op jit(solution)/shard_map/jit(_take)/gather | solution.py:156
  77.9 11.7 %all-to-all-start.2 = ((f32[14,32,2,4]{0,3,2,1:T(4,128)}), f32[14,32,2,4]{0,3,2,1:T(4,128)S(1)}, u32[]{:S(2)}, u32[]{:S(2)}) async-start(f32[14,32,2,4]{0,3,2,1:T(4,128)} %collective-permute-done.10), calls=%async_computation.2 | async-start | bytes 262144 | tf_op jit(solution)/shard_map/all_to_all | solution.py:98
  91.2 3.5 %collective-permute-start.9 = (f32[7,1,18,512]{3,2,1,0:T(8,128)}, f32[7,1,18,512]{3,2,1,0:T(8,128)}, u32[]{:S(2)}, u32[]{:S(2)}) collective-permute-start(f32[7,1,18,512]{3,2,1,0:T(8,128)} %get-tuple-element.38), channel_id=1, source_target_pairs={{0,1},{1,2},{2,3},{4,5},{5,6},{6,7},{8,9},{9,10},{10,11},{12,13},{... | collective-permute-start | bytes 774152 | tf_op jit(solution)/shard_map/ppermute | solution.py:32
  96.0 2.8 %all-to-all-done.2 = f32[14,32,2,4]{0,3,2,1:T(4,128)S(1)} async-done(((f32[14,32,2,4]{0,3,2,1:T(4,128)}), f32[14,32,2,4]{0,3,2,1:T(4,128)S(1)}, u32[]{:S(2)}, u32[]{:S(2)}) %all-to-all-start.2) | async-done | bytes 14368 | tf_op jit(solution)/shard_map/all_to_all | solution.py:98
  101.3 4.8 %collective-permute-done.8 = f32[7,1,18,512]{3,2,1,0:T(8,128)} collective-permute-done((f32[7,1,18,512]{3,2,1,0:T(8,128)}, f32[7,1,18,512]{3,2,1,0:T(8,128)}, u32[]{:S(2)}, u32[]{:S(2)}) %collective-permute-start.8) | collective-permute-done | bytes 258080 | tf_op jit(solution)/shard_map/ppermute | solution.py:33
  109.9 2.4 %collective-permute-start.12 = (f32[7,2,1,512]{3,2,1,0:T(1,128)S(1)}, f32[7,2,1,512]{3,2,1,0:T(1,128)S(1)}, u32[]{:S(2)}, u32[]{:S(2)}) collective-permute-start(f32[7,2,1,512]{3,2,1,0:T(1,128)S(1)} %get-tuple-element.67), channel_id=1, source_target_pairs={{4,0},{8,4},{12,8},{16,12},{20,16},{24,20},{28,24},{32,28},{36,32}... | collective-permute-start | bytes 86024 | tf_op jit(solution)/shard_map/ppermute | solution.py:33
  112.3 3.6 %collective-permute-start.11 = (f32[7,2,1,512]{3,2,1,0:T(1,128)S(1)}, f32[7,2,1,512]{3,2,1,0:T(1,128)S(1)}, u32[]{:S(2)}, u32[]{:S(2)}) collective-permute-start(f32[7,2,1,512]{3,2,1,0:T(1,128)S(1)} %get-tuple-element.66), channel_id=1, source_target_pairs={{0,4},{4,8},{8,12},{12,16},{16,20},{20,24},{24,28},{28,32},{32,36}... | collective-permute-start | bytes 86024 | tf_op jit(solution)/shard_map/ppermute | solution.py:32
  116.3 2.7 %copy.70 = f32[14,8192]{0,1:T(8,128)} copy(f32[14,8192]{1,0:T(8,128)S(1)} %bitcast.212) | data formatting | bytes 917504 | tf_op jit(solution)/shard_map/reshape | solution.py:155
  118.9 2.9 %gather_fusion.2 = f32[256,14]{1,0:T(8,128)S(1)} fusion(f32[14,8192]{0,1:T(8,128)} %copy.70, s32[1024]{0:T(1024)S(1)} %pad_clamp_fusion), kind=kCustom, calls=%fused_computation.2.clone | custom fusion | bytes 29696 | tf_op jit(solution)/shard_map/jit(_take)/gather | solution.py:156
  123.5 11.6 %all-to-all-start.3 = ((f32[14,32,2,4]{0,3,2,1:T(4,128)}), f32[14,32,2,4]{0,3,2,1:T(4,128)S(1)}, u32[]{:S(2)}, u32[]{:S(2)}) async-start(f32[14,32,2,4]{0,3,2,1:T(4,128)} %collective-permute-done.15), calls=%async_computation.3 | async-start | bytes 262144 | tf_op jit(solution)/shard_map/all_to_all | solution.py:98
  137.5 3.2 %collective-permute-start.14 = (f32[7,1,18,512]{3,2,1,0:T(8,128)}, f32[7,1,18,512]{3,2,1,0:T(8,128)}, u32[]{:S(2)}, u32[]{:S(2)}) collective-permute-start(f32[7,1,18,512]{3,2,1,0:T(8,128)} %get-tuple-element.36), channel_id=1, source_target_pairs={{0,1},{1,2},{2,3},{4,5},{5,6},{6,7},{8,9},{9,10},{10,11},{12,13},{... | collective-permute-start | bytes 774152 | tf_op jit(solution)/shard_map/ppermute | solution.py:32
  141.9 2.3 %all-to-all-done.3 = f32[14,32,2,4]{0,3,2,1:T(4,128)S(1)} async-done(((f32[14,32,2,4]{0,3,2,1:T(4,128)}), f32[14,32,2,4]{0,3,2,1:T(4,128)S(1)}, u32[]{:S(2)}, u32[]{:S(2)}) %all-to-all-start.3) | async-done | bytes 14368 | tf_op jit(solution)/shard_map/all_to_all | solution.py:98
  147.3 4.6 %collective-permute-done.13 = f32[7,1,18,512]{3,2,1,0:T(8,128)} collective-permute-done((f32[7,1,18,512]{3,2,1,0:T(8,128)S(1)}, f32[7,1,18,512]{3,2,1,0:T(8,128)}, u32[]{:S(2)}, u32[]{:S(2)}) %collective-permute-start.13) | collective-permute-done | bytes 258080 | tf_op jit(solution)/shard_map/ppermute | solution.py:33
  154.3 2.4 %collective-permute-start.17 = (f32[7,2,1,512]{3,2,1,0:T(1,128)S(1)}, f32[7,2,1,512]{3,2,1,0:T(1,128)S(1)}, u32[]{:S(2)}, u32[]{:S(2)}) collective-permute-start(f32[7,2,1,512]{3,2,1,0:T(1,128)S(1)} %get-tuple-element.63), channel_id=1, source_target_pairs={{4,0},{8,4},{12,8},{16,12},{20,16},{24,20},{28,24},{32,28},{36,32}... | collective-permute-start | bytes 86024 | tf_op jit(solution)/shard_map/ppermute | solution.py:33
  156.7 3.4 %collective-permute-start.16 = (f32[7,2,1,512]{3,2,1,0:T(1,128)S(1)}, f32[7,2,1,512]{3,2,1,0:T(1,128)S(1)}, u32[]{:S(2)}, u32[]{:S(2)}) collective-permute-start(f32[7,2,1,512]{3,2,1,0:T(1,128)S(1)} %get-tuple-element.62), channel_id=1, source_target_pairs={{0,4},{4,8},{8,12},{12,16},{16,20},{20,24},{24,28},{28,32},{32,36}... | collective-permute-start | bytes 86024 | tf_op jit(solution)/shard_map/ppermute | solution.py:32
  160.5 2.7 %copy.75 = f32[14,8192]{0,1:T(8,128)} copy(f32[14,8192]{1,0:T(8,128)S(1)} %bitcast.213) | data formatting | bytes 917504 | tf_op jit(solution)/shard_map/reshape | solution.py:155
  163.2 2.9 %gather_fusion.3 = f32[256,14]{1,0:T(8,128)S(1)} fusion(f32[14,8192]{0,1:T(8,128)} %copy.75, s32[1024]{0:T(1024)S(1)} %pad_clamp_fusion), kind=kCustom, calls=%fused_computation.3.clone | custom fusion | bytes 29696 | tf_op jit(solution)/shard_map/jit(_take)/gather | solution.py:156
  167.8 11.6 %all-to-all-start.4 = ((f32[14,32,2,4]{0,3,2,1:T(4,128)}), f32[14,32,2,4]{0,3,2,1:T(4,128)S(1)}, u32[]{:S(2)}, u32[]{:S(2)}) async-start(f32[14,32,2,4]{0,3,2,1:T(4,128)} %collective-permute-done.20), calls=%async_computation.4 | async-start | bytes 262144 | tf_op jit(solution)/shard_map/all_to_all | solution.py:98
  181.7 2.2 %collective-permute-start.19 = (f32[7,1,18,512]{3,2,1,0:T(8,128)}, f32[7,1,18,512]{3,2,1,0:T(8,128)}, u32[]{:S(2)}, u32[]{:S(2)}) collective-permute-start(f32[7,1,18,512]{3,2,1,0:T(8,128)} %get-tuple-element.34), channel_id=1, source_target_pairs={{0,1},{1,2},{2,3},{4,5},{5,6},{6,7},{8,9},{9,10},{10,11},{12,13},{... | collective-permute-start | bytes 774152 | tf_op jit(solution)/shard_map/ppermute | solution.py:32
  185.2 3.2 %all-to-all-done.4 = f32[14,32,2,4]{0,3,2,1:T(4,128)S(1)} async-done(((f32[14,32,2,4]{0,3,2,1:T(4,128)}), f32[14,32,2,4]{0,3,2,1:T(4,128)S(1)}, u32[]{:S(2)}, u32[]{:S(2)}) %all-to-all-start.4) | async-done | bytes 14368 | tf_op jit(solution)/shard_map/all_to_all | solution.py:98
  190.7 4.6 %collective-permute-done.18 = f32[7,1,18,512]{3,2,1,0:T(8,128)} collective-permute-done((f32[7,1,18,512]{3,2,1,0:T(8,128)S(1)}, f32[7,1,18,512]{3,2,1,0:T(8,128)}, u32[]{:S(2)}, u32[]{:S(2)}) %collective-permute-start.18) | collective-permute-done | bytes 258080 | tf_op jit(solution)/shard_map/ppermute | solution.py:33
  (262 shorter events, 55.0 us)
Async XLA Ops:
  0.6 34.4 %copy-start.10 = (s32[4]{0:T(128)S(1)}, s32[4]{0:T(128)}, u32[]{:S(2)}) copy-start(s32[4]{0:T(128)} %constant.27.clone) | copy-start | bytes 52
  0.6 44.3 %copy-start.8 = (f32[7]{0:T(128)S(1)}, f32[7]{0:T(128)}, u32[]{:S(2)}) copy-start(f32[7]{0:T(128)} %constant.26.clone) | copy-start | bytes 88
  1.7 43.4 %copy-start = (f32[1,3,2,16,512]{4,3,2,1,0:T(8,128)S(1)}, f32[1,3,2,16,512]{4,3,2,1,0:T(8,128)}, u32[]{:S(2)}) copy-start(f32[1,3,2,16,512]{4,3,2,1,0:T(8,128)} %param.18) | copy-start | bytes 589828
  1.7 43.4 %copy-start.1 = (f32[1,3,2,16,512]{4,3,2,1,0:T(8,128)S(1)}, f32[1,3,2,16,512]{4,3,2,1,0:T(8,128)}, u32[]{:S(2)}) copy-start(f32[1,3,2,16,512]{4,3,2,1,0:T(8,128)} %param.17) | copy-start | bytes 589828
  1.8 43.4 %copy-start.2 = (f32[1,2,16,512]{3,2,1,0:T(8,128)S(1)}, f32[1,2,16,512]{3,2,1,0:T(8,128)}, u32[]{:S(2)}) copy-start(f32[1,2,16,512]{3,2,1,0:T(8,128)} %param.16) | copy-start | bytes 196612
  1.8 43.1 %collective-permute-start.1 = (f32[7,2,1,512]{3,2,1,0:T(1,128)S(1)}, f32[7,2,1,512]{3,2,1,0:T(1,128)S(1)}, u32[]{:S(2)}, u32[]{:S(2)}) collective-permute-start(f32[7,2,1,512]{3,2,1,0:T(1,128)S(1)} %get-tuple-element.75), channel_id=1, source_target_pairs={{4,0},{8,4},{12,8},{16,12},{20,16},{24,20},{28,24},{32,28},{36,32}... | collective-permute-start | bytes 86024 | tf_op jit(solution)/shard_map/ppermute | solution.py:33
  6.1 38.8 %collective-permute-start = (f32[7,2,1,512]{3,2,1,0:T(1,128)S(1)}, f32[7,2,1,512]{3,2,1,0:T(1,128)S(1)}, u32[]{:S(2)}, u32[]{:S(2)}) collective-permute-start(f32[7,2,1,512]{3,2,1,0:T(1,128)S(1)} %get-tuple-element.74), channel_id=1, source_target_pairs={{0,4},{4,8},{8,12},{12,16},{16,20},{20,24},{24,28},{28,32},{32,36}... | collective-permute-start | bytes 86024 | tf_op jit(solution)/shard_map/ppermute | solution.py:32
  11.2 1.2 collective-permute-start.4
  13.2 21.7 %all-to-all-start = ((f32[32,2,1]{1,2,0:T(1,128)}), f32[32,2,1]{1,2,0:T(1,128)S(1)}, u32[]{:S(2)}, u32[]{:S(2)}) async-start(f32[32,2,1]{1,2,0:T(1,128)} %copy.59), calls=%async_computation | async-start | bytes 32768 | tf_op jit(solution)/shard_map/all_to_all | solution.py:93
  38.3 1.6 collective-permute-start.5
  39.9 14.2 %all-to-all-start.1 = ((f32[14,32,2,4]{0,3,2,1:T(4,128)}), f32[14,32,2,4]{0,3,2,1:T(4,128)S(1)}, u32[]{:S(2)}, u32[]{:S(2)}) async-start(f32[14,32,2,4]{0,3,2,1:T(4,128)} %collective-permute-done.5), calls=%async_computation.1 | async-start | bytes 262144 | tf_op jit(solution)/shard_map/all_to_all | solution.py:98
  46.4 11.0 %collective-permute-start.3 = (f32[7,1,18,512]{3,2,1,0:T(8,128)}, f32[7,1,18,512]{3,2,1,0:T(8,128)}, u32[]{:S(2)}, u32[]{:S(2)}) collective-permute-start(f32[7,1,18,512]{3,2,1,0:T(8,128)} %get-tuple-element.40), channel_id=1, source_target_pairs={{0,1},{1,2},{2,3},{4,5},{5,6},{6,7},{8,9},{9,10},{10,11},{12,13},{... | collective-permute-start | bytes 774152 | tf_op jit(solution)/shard_map/ppermute | solution.py:32
  50.6 11.4 %collective-permute-start.2 = (f32[7,1,18,512]{3,2,1,0:T(8,128)S(1)}, f32[7,1,18,512]{3,2,1,0:T(8,128)}, u32[]{:S(2)}, u32[]{:S(2)}) collective-permute-start(f32[7,1,18,512]{3,2,1,0:T(8,128)S(1)} %get-tuple-element.41), channel_id=1, source_target_pairs={{1,0},{2,1},{3,2},{5,4},{6,5},{7,6},{9,8},{10,9},{11,10},{13,12},{... | collective-permute-start | bytes 774152 | tf_op jit(solution)/shard_map/ppermute | solution.py:33
  64.4 25.2 %collective-permute-start.7 = (f32[7,2,1,512]{3,2,1,0:T(1,128)S(1)}, f32[7,2,1,512]{3,2,1,0:T(1,128)S(1)}, u32[]{:S(2)}, u32[]{:S(2)}) collective-permute-start(f32[7,2,1,512]{3,2,1,0:T(1,128)S(1)} %get-tuple-element.71), channel_id=1, source_target_pairs={{4,0},{8,4},{12,8},{16,12},{20,16},{24,20},{28,24},{32,28},{36,32}... | collective-permute-start | bytes 86024 | tf_op jit(solution)/shard_map/ppermute | solution.py:33
  67.0 22.7 %collective-permute-start.6 = (f32[7,2,1,512]{3,2,1,0:T(1,128)S(1)}, f32[7,2,1,512]{3,2,1,0:T(1,128)S(1)}, u32[]{:S(2)}, u32[]{:S(2)}) collective-permute-start(f32[7,2,1,512]{3,2,1,0:T(1,128)S(1)} %get-tuple-element.70), channel_id=1, source_target_pairs={{0,4},{4,8},{8,12},{12,16},{16,20},{20,24},{24,28},{28,32},{32,36}... | collective-permute-start | bytes 86024 | tf_op jit(solution)/shard_map/ppermute | solution.py:32
  76.3 1.6 collective-permute-start.10
  77.9 20.8 %all-to-all-start.2 = ((f32[14,32,2,4]{0,3,2,1:T(4,128)}), f32[14,32,2,4]{0,3,2,1:T(4,128)S(1)}, u32[]{:S(2)}, u32[]{:S(2)}) async-start(f32[14,32,2,4]{0,3,2,1:T(4,128)} %collective-permute-done.10), calls=%async_computation.2 | async-start | bytes 262144 | tf_op jit(solution)/shard_map/all_to_all | solution.py:98
  91.1 16.3 %copy-start.3 = (f32[7,2,18,512]{3,2,1,0:T(8,128)}, f32[7,2,18,512]{3,2,1,0:T(8,128)S(1)}, u32[]{:S(2)}) copy-start(f32[7,2,18,512]{3,2,1,0:T(8,128)S(1)} %constant_dynamic-update-slice_fusion.49) | copy-start | bytes 1548292
  91.2 10.1 %collective-permute-start.9 = (f32[7,1,18,512]{3,2,1,0:T(8,128)}, f32[7,1,18,512]{3,2,1,0:T(8,128)}, u32[]{:S(2)}, u32[]{:S(2)}) collective-permute-start(f32[7,1,18,512]{3,2,1,0:T(8,128)} %get-tuple-element.38), channel_id=1, source_target_pairs={{0,1},{1,2},{2,3},{4,5},{5,6},{6,7},{8,9},{9,10},{10,11},{12,13},{... | collective-permute-start | bytes 774152 | tf_op jit(solution)/shard_map/ppermute | solution.py:32
  94.7 11.5 %collective-permute-start.8 = (f32[7,1,18,512]{3,2,1,0:T(8,128)}, f32[7,1,18,512]{3,2,1,0:T(8,128)}, u32[]{:S(2)}, u32[]{:S(2)}) collective-permute-start(f32[7,1,18,512]{3,2,1,0:T(8,128)} %get-tuple-element.39), channel_id=1, source_target_pairs={{1,0},{2,1},{3,2},{5,4},{6,5},{7,6},{9,8},{10,9},{11,10},{13,12},{... | collective-permute-start | bytes 774152 | tf_op jit(solution)/shard_map/ppermute | solution.py:33
  109.9 25.3 %collective-permute-start.12 = (f32[7,2,1,512]{3,2,1,0:T(1,128)S(1)}, f32[7,2,1,512]{3,2,1,0:T(1,128)S(1)}, u32[]{:S(2)}, u32[]{:S(2)}) collective-permute-start(f32[7,2,1,512]{3,2,1,0:T(1,128)S(1)} %get-tuple-element.67), channel_id=1, source_target_pairs={{4,0},{8,4},{12,8},{16,12},{20,16},{24,20},{28,24},{32,28},{36,32}... | collective-permute-start | bytes 86024 | tf_op jit(solution)/shard_map/ppermute | solution.py:33
  112.3 22.9 %collective-permute-start.11 = (f32[7,2,1,512]{3,2,1,0:T(1,128)S(1)}, f32[7,2,1,512]{3,2,1,0:T(1,128)S(1)}, u32[]{:S(2)}, u32[]{:S(2)}) collective-permute-start(f32[7,2,1,512]{3,2,1,0:T(1,128)S(1)} %get-tuple-element.66), channel_id=1, source_target_pairs={{0,4},{4,8},{8,12},{12,16},{16,20},{20,24},{24,28},{28,32},{32,36}... | collective-permute-start | bytes 86024 | tf_op jit(solution)/shard_map/ppermute | solution.py:32
  122.0 1.6 collective-permute-start.15
  123.5 20.7 %all-to-all-start.3 = ((f32[14,32,2,4]{0,3,2,1:T(4,128)}), f32[14,32,2,4]{0,3,2,1:T(4,128)S(1)}, u32[]{:S(2)}, u32[]{:S(2)}) async-start(f32[14,32,2,4]{0,3,2,1:T(4,128)} %collective-permute-done.15), calls=%async_computation.3 | async-start | bytes 262144 | tf_op jit(solution)/shard_map/all_to_all | solution.py:98
  137.5 9.8 %collective-permute-start.14 = (f32[7,1,18,512]{3,2,1,0:T(8,128)}, f32[7,1,18,512]{3,2,1,0:T(8,128)}, u32[]{:S(2)}, u32[]{:S(2)}) collective-permute-start(f32[7,1,18,512]{3,2,1,0:T(8,128)} %get-tuple-element.36), channel_id=1, source_target_pairs={{0,1},{1,2},{2,3},{4,5},{5,6},{6,7},{8,9},{9,10},{10,11},{12,13},{... | collective-permute-start | bytes 774152 | tf_op jit(solution)/shard_map/ppermute | solution.py:32
  140.7 11.3 %collective-permute-start.13 = (f32[7,1,18,512]{3,2,1,0:T(8,128)S(1)}, f32[7,1,18,512]{3,2,1,0:T(8,128)}, u32[]{:S(2)}, u32[]{:S(2)}) collective-permute-start(f32[7,1,18,512]{3,2,1,0:T(8,128)S(1)} %get-tuple-element.37), channel_id=1, source_target_pairs={{1,0},{2,1},{3,2},{5,4},{6,5},{7,6},{9,8},{10,9},{11,10},{13,12},{... | collective-permute-start | bytes 774152 | tf_op jit(solution)/shard_map/ppermute | solution.py:33
  154.3 25.1 %collective-permute-start.17 = (f32[7,2,1,512]{3,2,1,0:T(1,128)S(1)}, f32[7,2,1,512]{3,2,1,0:T(1,128)S(1)}, u32[]{:S(2)}, u32[]{:S(2)}) collective-permute-start(f32[7,2,1,512]{3,2,1,0:T(1,128)S(1)} %get-tuple-element.63), channel_id=1, source_target_pairs={{4,0},{8,4},{12,8},{16,12},{20,16},{24,20},{28,24},{32,28},{36,32}... | collective-permute-start | bytes 86024 | tf_op jit(solution)/shard_map/ppermute | solution.py:33
  156.7 22.7 %collective-permute-start.16 = (f32[7,2,1,512]{3,2,1,0:T(1,128)S(1)}, f32[7,2,1,512]{3,2,1,0:T(1,128)S(1)}, u32[]{:S(2)}, u32[]{:S(2)}) collective-permute-start(f32[7,2,1,512]{3,2,1,0:T(1,128)S(1)} %get-tuple-element.62), channel_id=1, source_target_pairs={{0,4},{4,8},{8,12},{12,16},{16,20},{20,24},{24,28},{28,32},{32,36}... | collective-permute-start | bytes 86024 | tf_op jit(solution)/shard_map/ppermute | solution.py:32
  166.2 1.6 collective-permute-start.20
  167.8 20.7 %all-to-all-start.4 = ((f32[14,32,2,4]{0,3,2,1:T(4,128)}), f32[14,32,2,4]{0,3,2,1:T(4,128)S(1)}, u32[]{:S(2)}, u32[]{:S(2)}) async-start(f32[14,32,2,4]{0,3,2,1:T(4,128)} %collective-permute-done.20), calls=%async_computation.4 | async-start | bytes 262144 | tf_op jit(solution)/shard_map/all_to_all | solution.py:98
  181.7 8.9 %collective-permute-start.19 = (f32[7,1,18,512]{3,2,1,0:T(8,128)}, f32[7,1,18,512]{3,2,1,0:T(8,128)}, u32[]{:S(2)}, u32[]{:S(2)}) collective-permute-start(f32[7,1,18,512]{3,2,1,0:T(8,128)} %get-tuple-element.34), channel_id=1, source_target_pairs={{0,1},{1,2},{2,3},{4,5},{5,6},{6,7},{8,9},{9,10},{10,11},{12,13},{... | collective-permute-start | bytes 774152 | tf_op jit(solution)/shard_map/ppermute | solution.py:32
  183.9 11.4 %collective-permute-start.18 = (f32[7,1,18,512]{3,2,1,0:T(8,128)S(1)}, f32[7,1,18,512]{3,2,1,0:T(8,128)}, u32[]{:S(2)}, u32[]{:S(2)}) collective-permute-start(f32[7,1,18,512]{3,2,1,0:T(8,128)S(1)} %get-tuple-element.35), channel_id=1, source_target_pairs={{1,0},{2,1},{3,2},{5,4},{6,5},{7,6},{9,8},{10,9},{11,10},{13,12},{... | collective-permute-start | bytes 774152 | tf_op jit(solution)/shard_map/ppermute | solution.py:33
  (5 other events, 23.7 us)
where the time goes:
time: 200 us; the launch traced here: 199 us
  starting transfers between devices  95.8 us (48%)
  waiting for transfers between devices  43.7 us (22%)
  local copies, waits for them, and re-layouts  35.1 us (18%)
  other arithmetic  18.7 us (9%)
  matrix products  4.04 us (2%)
    all_to_all x4, starting transfers between devices, route_reply(): lax.all_to_all(crossed, 'ang', split_axis=1, concat_axis=1, tiled=True)  40 us
    ppermute x8, starting transfers between devices, padded(): before = lax.ppermute(last, axis, up)  25.4 us
    ppermute x8, waiting for transfers between devices, padded(): after = lax.ppermute(first, axis, down)  18.7 us
    ppermute x8, starting transfers between devices, padded(): after = lax.ppermute(first, axis, down)  16.8 us
    all_to_all x1, starting transfers between devices, route_request(): lax.all_to_all(crossed, 'ang', split_axis=0, concat_axis=0, tiled=True)  13.2 us
    gather x4, local copies, waits for them, and re-layouts, overset(): jnp.take(table, gather_index, axis=1).reshape(stacked_rows, slot_count, 4)  11.6 us
    reshape x4, local copies, waits for them, and re-layouts, overset(): table = current.reshape(stacked_rows, rows_p * rows_t)  10.7 us
    all_to_all x4, waiting for transfers between devices, route_reply(): lax.all_to_all(crossed, 'ang', split_axis=1, concat_axis=1, tiled=True)  10.4 us
  transfers between devices with their start and end apart: 26, of which 18 were waited for; matrix products, arithmetic and copies ran while one was open for 21% of the time, Pallas kernels for 0%

commit v1 on v0

v1 whole, which is shorter than its diff:
```python
import math

import jax
import jax.numpy as jnp
import numpy as np
from jax import lax
from jax.experimental import pallas as pl
from jax.experimental.pallas import tpu as pltpu
from jax.sharding import PartitionSpec as P

time_step = 0.15
diffusion = 0.1
r_inner = 0.35
NF = 7
MIRROR = (1.0, -1.0, -1.0, -1.0, 1.0, 1.0, 1.0)
INTERPRET = False
SLOT = 16
HIGHEST = lax.Precision.HIGHEST


def iota(shape, dim):
    return lax.broadcasted_iota(jnp.int32, shape, dim)


def derived(cells):
    inverse = 1.0 / cells[0]
    speed = [cells[1 + c] * inverse for c in range(3)]
    pressure = cells[0] + 0.5 * (
        cells[4] * cells[4] + cells[5] * cells[5] + cells[6] * cells[6]
    )
    return speed, pressure


def flux_along(cells, speed, pressure, d):
    moment, magnet = cells[1:4], cells[4:7]
    out = [moment[d]]
    for c in range(3):
        term = moment[c] * speed[d] - magnet[c] * magnet[d]
        out.append(term + pressure if c == d else term)
    for c in range(3):
        out.append(None if c == d else speed[d] * magnet[c] - magnet[d] * speed[c])
    return out


def upper_part(flux, cell, half, spread):
    if cell is None:
        return half * flux
    if flux is None:
        return -(spread * cell)
    return half * flux - spread * cell


def lower_part(flux, cell, half, spread):
    if cell is None:
        return half * flux
    if flux is None:
        return spread * cell
    return half * flux + spread * cell


def place(rad, n_rad, level, rows_r):
    value = None
    for at in range(n_rad):
        radius = r_inner + (at * rows_r + level + 0.5) * ((1.0 - r_inner) / (rows_r * n_rad))
        item = jnp.float32(1.0 / radius)
        value = item if value is None else jnp.where(rad == at, item, value)
    return value


def answer_into(msg_ref, low, high, corner, rowmask):
    rows_p = rowmask.shape[0]
    parts = []
    for level in (low, high):
        product = jnp.dot(level, corner, precision=HIGHEST, preferred_element_type=jnp.float32)
        picked = product.reshape(NF, rows_p, 128) * rowmask[None]
        parts.append(jnp.sum(picked, axis=1))
        parts.append(jnp.zeros((1, 128), jnp.float32))
    both = jnp.concatenate(parts, axis=0)
    both = both + pltpu.roll(both, 64, axis=1)
    turned = both.T
    lanes = jnp.concatenate([turned, jnp.zeros((128, 128 - SLOT), jnp.float32)], axis=1)
    lane = iota((32, 128), 1)
    message = jnp.where(lane < SLOT, lanes[0:32], pltpu.roll(lanes[32:64], SLOT, axis=1))
    msg_ref[...] = message.reshape(msg_ref.shape)


def send_rows(first_ref, last_ref, level, f, value):
    first_ref[f, level : level + 1, :] = value[0:1, :]
    last_ref[f, level : level + 1, :] = value[value.shape[0] - 1 :, :]


def open_kernel(
    density, momentum, magnetic, device, phi, theta, weight, turn, cos_in, sin_in,
    low_ref, high_ref, first_ref, last_ref, ask_ref, table_ref,
):
    for level, ref in ((0, low_ref), (1, high_ref)):
        for f in range(NF):
            if f == 0:
                value = density[0, level]
            elif f < 4:
                value = momentum[0, f - 1, level]
            else:
                value = magnetic[0, f - 4, level]
            ref[f] = value
            send_rows(first_ref, last_ref, level, f, value)
    rows = device.shape[1]
    one, two = iota((rows, rows), 0), iota((rows, rows), 1)
    eye = one == two
    dev_col = device[0]
    dev_row = jnp.sum(jnp.where(eye, jnp.broadcast_to(dev_col, (rows, rows)), 0), axis=0, keepdims=True)
    same = dev_col == dev_row
    rank_row = jnp.sum(jnp.where(same & (one < two), 1, 0), axis=0, keepdims=True)
    rank_col = jnp.sum(jnp.where(same & (two < one), 1, 0), axis=1, keepdims=True)

    def column(row):
        return jnp.sum(jnp.where(eye, jnp.broadcast_to(row, (rows, rows)), 0.0), axis=1, keepdims=True)

    phi_col = column(phi[...].astype(jnp.float32))
    theta_col = column(theta[...].astype(jnp.float32))
    weights = weight[0]
    lane = iota((rows, 128), 1)
    items = [phi_col, theta_col] + [weights[:, c : c + 1] for c in range(4)]
    record = jnp.zeros((rows, 128), jnp.float32)
    for at, item in enumerate(items):
        record = jnp.where(lane == at, item, record)
    asked = jnp.zeros((rows, 128), jnp.float32)
    for slot in range(2):
        placing = jnp.where((one == dev_row) & (rank_row == slot), 1.0, 0.0)
        moved = record if slot == 0 else pltpu.roll(record, 8, axis=1)
        asked = asked + jnp.dot(placing, moved, precision=HIGHEST, preferred_element_type=jnp.float32)
    ask_ref[...] = asked.reshape(ask_ref.shape)
    picks = jnp.where(((lane & 31) == dev_col) & ((lane >> 5) == rank_col) & (lane < 64), 1.0, 0.0)
    cosine = column(cos_in[...])
    sine = column(sin_in[...])
    picks = jnp.where(lane == 64, cosine, picks)
    table_ref[...] = jnp.where(lane == 65, sine, picks)


def asked_kernel(asked_ref, low_ref, high_ref, corner_ref, mask_ref, msg_ref):
    asked = asked_ref[...].reshape(32, 128)
    lane, sub = iota((32, 128), 1), iota((32, 128), 0)

    def row_of(at):
        total = jnp.zeros((32, 128), jnp.float32)
        for part in range(4):
            slot = part & 1
            col = asked[:, slot * 8 + at[part >> 1] : slot * 8 + at[part >> 1] + 1]
            total = jnp.where(lane == sub + 32 * part, col, total)
        return jnp.sum(total, axis=0, keepdims=True)

    phi_row = row_of((0, 0)).astype(jnp.int32)
    theta_row = row_of((1, 1)).astype(jnp.int32)
    near = row_of((2, 4))
    far = row_of((3, 5))
    cell = iota((corner_ref.shape[0], 128), 0)
    corner = jnp.where(cell == theta_row, near, jnp.where(cell == theta_row + 1, far, 0.0))
    corner_ref[...] = corner
    rows_p = mask_ref.shape[0]
    wanted = phi_row + jnp.where(iota((1, 128), 1) < 64, 0, 1)
    mask = jnp.where(iota((rows_p, 128), 0) == wanted, 1.0, 0.0)
    mask_ref[...] = mask
    rows_t = low_ref.shape[2]
    low = low_ref[...].reshape(NF * rows_p, rows_t)
    high = high_ref[...].reshape(NF * rows_p, rows_t)
    answer_into(msg_ref, low, high, corner, mask)


def stage_kernel(stage, n_rad, n_ang, *refs):
    last = stage == 4
    (flags, sines, low0, high0, below, above, before, after, reply, table) = refs[:10]
    refs = refs[10:]
    if stage == 1:
        low, high = low0, high0
    else:
        low, high, acc_low, acc_high = refs[:4]
        refs = refs[4:]
    if last:
        density_out, momentum_out, magnetic_out = refs[:3]
        refs = refs[3:]
    else:
        corner, rowmask = refs[:2]
        low_out, high_out, acc_low_out, acc_high_out, first_out, last_out, msg_out = refs[2:9]
        refs = refs[9:]
    slope, up, down = refs
    rad, ang = flags[0], flags[1]
    rows_p, rows_t = low.shape[1:]
    invs = [place(rad, n_rad, level, 2) for level in range(2)]

    got = reply[...].reshape(32, 128)
    picks = table[...]
    ghost = jnp.dot(picks[:, 0:32], got, precision=HIGHEST, preferred_element_type=jnp.float32)
    second = jnp.dot(picks[:, 32:64], got, precision=HIGHEST, preferred_element_type=jnp.float32)
    ghost = ghost + pltpu.roll(second, 128 - SLOT, axis=1)
    cosine, sine = picks[:, 64:65], picks[:, 65:66]
    lane = iota((32, 128), 1) & 7
    is_t = (lane == 2) | (lane == 5)
    is_p = (lane == 3) | (lane == 6)
    turned_t = cosine * ghost + sine * pltpu.roll(ghost, 127, axis=1)
    turned_p = cosine * ghost - sine * pltpu.roll(ghost, 1, axis=1)
    ghost = jnp.where(is_t, turned_t, jnp.where(is_p, turned_p, ghost))

    sine_row = sines[...]
    rim = []
    for f in range(NF):
        own = [low[f, 0:1, :], high[f, 0:1, :], low[f, rows_p - 1 :, :], high[f, rows_p - 1 :, :]]
        own = [MIRROR[f] * item for item in own]
        start = jnp.where(ang == 0, jnp.concatenate(own[:2], axis=0), before[f])
        end = jnp.where(ang == n_ang - 1, jnp.concatenate(own[2:], axis=0), after[f])
        rim.append(jnp.concatenate([start, end, start, end], axis=0))
    rim_row = iota((8, rows_t), 0) & 1
    rim_inv = jnp.where(rim_row == 0, invs[0], invs[1]) * sine_row
    speed, pressure = derived(rim)
    flux = flux_along(rim, speed, pressure, 2)
    rim_half, rim_spread = 0.5 * rim_inv, diffusion * rim_inv * rim_inv
    rim_low = [lower_part(flux[f], rim[f] if f else None, rim_half, rim_spread) for f in range(NF)]
    rim_high = [upper_part(flux[f], rim[f] if f else None, rim_half, rim_spread) for f in range(NF)]

    half_row = iota((8, 128), 1) < 64
    for tile in range(rows_p // 8):
        rows = slice(8 * tile, 8 * tile + 8)
        for level in range(2):
            mine, other = (low, high) if level == 0 else (high, low)
            far, wall = (below, rad == 0) if level == 0 else (above, rad == n_rad - 1)
            cells = [mine[f, rows, :] for f in range(NF)]
            sums = []
            outer = [jnp.where(wall, MIRROR[f] * cells[f], far[f, rows, :]) for f in range(NF)]
            speed, pressure = derived(outer)
            flux = flux_along(outer, speed, pressure, 0)
            part = lower_part if level == 0 else upper_part
            for f in range(NF):
                sums.append(part(flux[f], outer[f] if f else None, 0.5, diffusion))
            inner = [other[f, rows, :] for f in range(NF)]
            speed, pressure = derived(inner)
            flux = flux_along(inner, speed, pressure, 0)
            part = upper_part if level == 0 else lower_part
            for f in range(NF):
                item = part(flux[f], inner[f] if f else None, 0.5, diffusion)
                sums[f] = sums[f] - item if level == 0 else item - sums[f]
            speed, pressure = derived(cells)
            inv = invs[level]
            inv_sine = inv * sine_row
            half, spread = 0.5 * inv_sine, diffusion * inv_sine * inv_sine
            flux = flux_along(cells, speed, pressure, 2)
            for f in range(NF):
                cell = cells[f] if f else None
                down[level, f, rows, :] = lower_part(flux[f], cell, half, spread)
                up[level, f, rows, :] = upper_part(flux[f], cell, half, spread)
            flux = flux_along(cells, speed, pressure, 1)
            rim_cells = []
            for f in range(NF):
                at = 8 * level + f
                lower = ghost[8 * tile : 8 * tile + 8, at : at + 1]
                upper = ghost[16 + 8 * tile : 24 + 8 * tile, at : at + 1]
                rim_cells.append(jnp.where(half_row, upper, lower))
            rim_speed, rim_pressure = derived(rim_cells)
            rim_flux = flux_along(rim_cells, rim_speed, rim_pressure, 1)
            half_t, spread_t = 0.5 * inv, diffusion * inv * inv
            centre = 2.0 * diffusion * (1.0 + inv * inv) + 2.0 * spread
            for f in range(NF):
                full = jnp.concatenate([cells[f], rim_cells[f]], axis=1) if f else None
                whole = None
                if flux[f] is not None:
                    whole = jnp.concatenate([flux[f], rim_flux[f]], axis=1)
                give_up = lower_part(whole, full, half_t, spread_t)
                give_down = upper_part(whole, full, half_t, spread_t)
                width = rows_t + 128
                total = sums[f] + pltpu.roll(give_up, 1, axis=1)[:, :rows_t]
                total = total - pltpu.roll(give_down, width - 1, axis=1)[:, :rows_t]
                if f:
                    total = total - centre * cells[f]
                slope[level, f, rows, :] = total

    row = iota((rows_p, rows_t), 0)
    for level in range(2):
        start, now = (low0, low) if level == 0 else (high0, high)
        for f in range(NF):
            lower = pltpu.roll(down[level, f], 1, axis=0)
            lower = jnp.where(row == 0, rim_low[f][level : level + 1, :], lower)
            upper = pltpu.roll(up[level, f], rows_p - 1, axis=0)
            upper = jnp.where(row == rows_p - 1, rim_high[f][2 + level : 3 + level, :], upper)
            k = slope[level, f] + lower - upper
            if last:
                acc = acc_low if level == 0 else acc_high
                value = start[f] + (time_step / 6.0) * (acc[f] + k)
                if f == 0:
                    density_out[0, level] = value
                elif f < 4:
                    momentum_out[0, f - 1, level] = value
                else:
                    magnetic_out[0, f - 4, level] = value
                continue
            acc_out = acc_low_out if level == 0 else acc_high_out
            if stage == 1:
                acc_out[f] = k
            else:
                acc_out[f] = (acc_low if level == 0 else acc_high)[f] + 2.0 * k
            step = time_step if stage == 3 else 0.5 * time_step
            value = start[f] + step * k
            (low_out if level == 0 else high_out)[f] = value
            send_rows(first_out, last_out, level, f, value)
    if not last:
        new_low = low_out[...].reshape(NF * rows_p, rows_t)
        new_high = high_out[...].reshape(NF * rows_p, rows_t)
        answer_into(msg_out, new_low, new_high, corner[...], rowmask[...])


def body(
    density, momentum, magnetic, partner_device, partner_phi, partner_theta, partner_weight, border_turn
):
    _, rows_r, rows_p, rows_t = density.shape
    n_ang, n_rad = lax.axis_size("ang"), lax.axis_size("rad")
    f32 = jnp.float32
    vmem = pl.BlockSpec(memory_space=pltpu.VMEM)
    smem = pl.BlockSpec(memory_space=pltpu.SMEM)

    def shape(*dims):
        return jax.ShapeDtypeStruct(dims, f32)

    def call(kernel, ins, outs, scratch=(), name=None, scalars=0):
        return pl.pallas_call(
            kernel,
            out_shape=outs,
            in_specs=[smem] * scalars + [vmem] * (len(ins) - scalars),
            out_specs=[vmem] * len(outs),
            scratch_shapes=list(scratch),
            interpret=INTERPRET,
            name=name,
        )(*ins)

    level = shape(NF, rows_p, rows_t)
    edge = shape(NF, 2, rows_t)
    message = shape(32, 1, 128)

    def shifted(value, axis, by):
        size = lax.axis_size(axis)
        return lax.ppermute(value, axis, [(i, (i + by) % size) for i in range(size)])

    def crossed(value):
        swap = lax.ppermute(value, "panel", [(0, 1), (1, 0)])
        return lax.all_to_all(swap, "ang", split_axis=0, concat_axis=0, tiled=True)

    def halos(low, high, first, final):
        return (
            shifted(high, "rad", 1),
            shifted(low, "rad", -1),
            shifted(final, "ang", 1),
            shifted(first, "ang", -1),
        )

    flags = jnp.stack([lax.axis_index("rad"), lax.axis_index("ang")]).astype(jnp.int32)
    theta = math.pi / 4 + (np.arange(rows_t) + 0.5) * (math.pi / 2 / rows_t)
    sines = jnp.asarray((1.0 / np.sin(theta)).astype(np.float32)).reshape(1, rows_t)

    low0, high0, first, final, ask, table = call(
        open_kernel,
        [
            density, momentum, magnetic, partner_device, partner_phi, partner_theta, partner_weight,
            border_turn, jnp.cos(border_turn), jnp.sin(border_turn),
        ],
        [level, level, edge, edge, message, shape(32, 128)],
        name="open",
    )
    around = halos(low0, high0, first, final)
    corner, rowmask, answer = call(
        asked_kernel,
        [crossed(ask), low0, high0],
        [shape(rows_t, 128), shape(rows_p, 128), message],
        name="asked",
    )
    low, high, sums = low0, high0, []
    scratch = [pltpu.VMEM((2, NF, rows_p, rows_t), f32) for _ in range(3)]
    for stage in range(1, 5):
        ins = [flags, sines, low0, high0, *around, crossed(answer), table]
        if stage > 1:
            ins += [low, high, *sums]
        if stage < 4:
            ins += [corner, rowmask]
            outs = [level, level, level, level, edge, edge, message]
        else:
            outs = [
                shape(1, rows_r, rows_p, rows_t),
                shape(1, 3, rows_r, rows_p, rows_t),
                shape(1, 3, rows_r, rows_p, rows_t),
            ]

        def kernel(*refs, stage=stage):
            stage_kernel(stage, n_rad, n_ang, *refs)

        result = call(kernel, ins, outs, scratch, name=f"stage{stage}", scalars=1)
        if stage == 4:
            return tuple(result)
        low, high, acc_low, acc_high, first, final, answer = result
        sums = [acc_low, acc_high]
        around = halos(low, high, first, final)


def solution(mesh):
    in_specs = (
        P("panel", "rad", "ang", None),
        P("panel", None, "rad", "ang", None),
        P("panel", None, "rad", "ang", None),
        P("panel", "ang", None),
        P("panel", "ang"),
        P("panel", "ang"),
        P("panel", "ang", None),
        P("panel", "ang"),
    )
    out_specs = (
        P("panel", "rad", "ang", None),
        P("panel", None, "rad", "ang", None),
        P("panel", None, "rad", "ang", None),
    )
    return jax.shard_map(body, mesh=mesh, in_specs=in_specs, out_specs=out_specs, check_vma=False)
```

time: 200 us -> 134 us (0.67)
  starting transfers between devices: 95.8 us -> 51.7 us
  local copies, waits for them, and re-layouts: 35.1 us -> 5.63 us
  Pallas kernels: 0 us -> 20.8 us
  blocking collectives: 0 us -> 20.1 us
  other arithmetic: 18.7 us -> 0.64 us
  waiting for transfers between devices: 43.7 us -> 33.7 us
  matrix products: 4.04 us -> 0 us
    all_to_all x5 -> x4, starting transfers between devices: 53.2 us -> 30.3 us  [crossed(): return lax.all_to_all(swap, 'ang', split_axis=0, concat_axis=0, tiled=True)]
    ppermute x21, starting transfers between devices: 42.6 us -> 21.4 us  [the longest x16 21.4 us: shifted(): lax.ppermute(value, axis, [(i, (i + by) % size) for i in range(size)])]
    pallas_call x0 -> x6, Pallas kernels: none -> 20.8 us  [call(): pl.pallas_call(kernel, out_shape=outs, in_specs=[smem] * scalars + [vmem]...]
    all_to_all x0 -> x1, blocking collectives: none -> 20.1 us  [crossed(): return lax.all_to_all(swap, 'ang', split_axis=0, concat_axis=0, tiled=True)]
    ppermute x21, waiting for transfers between devices: 28.5 us -> 15.9 us  [the longest x16 9.98 us: shifted(): lax.ppermute(value, axis, [(i, (i + by) % size) for i in range(size)])]
    gather x4 -> x0, local copies, waits for them, and re-layouts: 11.6 us -> none  [overset(): jnp.take(table, gather_index, axis=1).reshape(stacked_rows, slot_count, 4)]
    reshape x4 -> x0, local copies, waits for them, and re-layouts: 10.7 us -> none  [overset(): table = current.reshape(stacked_rows, rows_p * rows_t)]
    select_n x13 -> x0, other arithmetic: 5.65 us -> none  [the longest x4 4.77 us: evaluate(): lower_r = jnp.where(first_r, mirror * current[:, :1], haloed[:, :1, 1:-1])]
  transfers between devices with their start and end apart: 26 -> 25, of which waited for: 18 -> 14; matrix products, arithmetic and copies ran while one was open for 21% -> 0% of each run, Pallas kernels for 0% -> 2%
where the time goes in v1:
time: 134 us; the launch traced here: 133 us
  starting transfers between devices  51.7 us (39%)
  waiting for transfers between devices  33.7 us (25%)
  Pallas kernels  20.8 us (16%)
  blocking collectives  20.1 us (15%)
  local copies, waits for them, and re-layouts  5.63 us (4%)
    all_to_all x4, starting transfers between devices, crossed(): return lax.all_to_all(swap, 'ang', split_axis=0, concat_axis=0, tiled=True)  30.3 us
    ppermute x16, starting transfers between devices, shifted(): lax.ppermute(value, axis, [(i, (i + by) % size) for i in range(size)])  21.4 us
    pallas_call x6, Pallas kernels, call(): pl.pallas_call(kernel, out_shape=outs, in_specs=[smem] * scalars + [vmem]...  20.8 us
    all_to_all x1, blocking collectives, crossed(): return lax.all_to_all(swap, 'ang', split_axis=0, concat_axis=0, tiled=True)  20.1 us
    all_to_all x4, waiting for transfers between devices, crossed(): return lax.all_to_all(swap, 'ang', split_axis=0, concat_axis=0, tiled=True)  17.8 us
    ppermute x16, waiting for transfers between devices, shifted(): lax.ppermute(value, axis, [(i, (i + by) % size) for i in range(size)])  9.98 us
    ppermute x5, waiting for transfers between devices, crossed(): swap = lax.ppermute(value, 'panel', [(0, 1), (1, 0)])  5.96 us
    unnamed x56, local copies, waits for them, and re-layouts  4.33 us
  transfers between devices with their start and end apart: 25, of which 14 were waited for; matrix products, arithmetic and copies ran while one was open for 0% of the time, Pallas kernels for 2%

profile of v1, /device:TPU:2, one launch (start us, length us, event | category | flops | bytes accessed | tf_op | source)
XLA Modules:
  0.0 133.5 jit_solution(18164072120465819791)
XLA Ops:
  0.6 1.3 fusion
  3.3 2.2 %open.1 = (f32[7,16,512]{2,1,0:T(8,128)}, f32[7,16,512]{2,1,0:T(8,128)}, f32[7,2,512]{2,1,0:T(2,128)}, f32[7,2,512]{2,1,0:T(2,128)}, f32[32,1,128]{2,1,0:T(1,128)}, /*index=5*/f32[32,128]{1,0:T(8,128)}) custom-call(f32[1,2,16,512]{3,2,1,0:T(8,128)} %density.1, f32[1,3,2,16,512]{4,3,2,1,0:T(8,128)} %momentum.1, f32[1,3,2,16,512]{4,3,2,1,0:T(8,128)} %magnetic.1, ...), custom_call_target="tpu_custom_call" | custom-call | tf_op jit(solution)/shard_map/open/pallas_call | solution.py:320
  5.5 3.1 %collective-permute-start.1 = (f32[7,16,512]{2,1,0:T(8,128)}, f32[7,16,512]{2,1,0:T(8,128)S(1)}, u32[]{:S(2)}, u32[]{:S(2)}) collective-permute-start(f32[7,16,512]{2,1,0:T(8,128)} %get-tuple-element.33.low_ref.refs_2_), channel_id=1, source_target_pairs={{0,3},{1,0},{2,1},{3,2},{4,7},{5,4},{6,5},{7,6},{8,11},{9,8},{10,9... | collective-permute-start | bytes 688136 | tf_op jit(solution)/shard_map/ppermute | solution.py:336
  8.6 1.4 %collective-permute-done.4 = f32[32,1,128]{2,1,0:T(1,128)S(1)} collective-permute-done((f32[32,1,128]{2,1,0:T(1,128)}, f32[32,1,128]{2,1,0:T(1,128)S(1)}, u32[]{:S(2)}, u32[]{:S(2)}) %collective-permute-start.4) | collective-permute-done | bytes 16416 | tf_op jit(solution)/shard_map/ppermute | solution.py:339
  10.0 20.1 %all_to_all.25.asked_ref = f32[32,1,128]{2,1,0:T(1,128)} all-to-all(f32[32,1,128]{2,1,0:T(1,128)S(1)} %collective-permute-done.4), channel_id=1, replica_groups=mesh['panel'=2,'ang'=32,'rad'=4] {'ang'}, dimensions={0} | all-to-all | bytes 32768 | tf_op jit(solution)/shard_map/all_to_all | solution.py:340
  30.1 3.0 %asked.1 = (f32[512,128]{1,0:T(8,128)}, f32[16,128]{1,0:T(8,128)}, f32[32,1,128]{2,1,0:T(1,128)}) custom-call(f32[32,1,128]{2,1,0:T(1,128)} %all_to_all.25.asked_ref, f32[7,16,512]{2,1,0:T(8,128)} %get-tuple-element.33.low_ref.refs_2_, f32[7,16,512]{2,1,0:T(8,128)} %get-tuple-element.34.high_ref.refs_3_), custom_call_target="tpu_custom_call" | custom-call | tf_op jit(solution)/shard_map/asked/pallas_call | solution.py:320
  33.7 1.4 %collective-permute-start.3 = (f32[7,2,512]{2,1,0:T(2,128)S(1)}, f32[7,2,512]{2,1,0:T(2,128)S(1)}, u32[]{:S(2)}, u32[]{:S(2)}) collective-permute-start(f32[7,2,512]{2,1,0:T(2,128)S(1)} %copy-done.22), channel_id=1, source_target_pairs={{0,124},{4,0},{8,4},{12,8},{16,12},{20,16},{24,20},{28,24},{32,28}... | collective-permute-start | bytes 86024 | tf_op jit(solution)/shard_map/ppermute | solution.py:336
  35.1 8.3 %all-to-all-start.1 = ((f32[32,1,128]{2,1,0:T(1,128)}), f32[32,1,128]{2,1,0:T(1,128)S(1)}, u32[]{:S(2)}, u32[]{:S(2)}) async-start(f32[32,1,128]{2,1,0:T(1,128)} %collective-permute-done.5), calls=%async_computation.1 | async-start | bytes 32768 | tf_op jit(solution)/shard_map/all_to_all | solution.py:340
  44.0 8.0 %all-to-all-done.1.refs_8_ = f32[32,1,128]{2,1,0:T(1,128)S(1)} async-done(((f32[32,1,128]{2,1,0:T(1,128)}), f32[32,1,128]{2,1,0:T(1,128)S(1)}, u32[]{:S(2)}, u32[]{:S(2)}) %all-to-all-start.1) | async-done | bytes 16416 | tf_op jit(solution)/shard_map/all_to_all | solution.py:340
  52.8 3.9 %stage1.1 = (f32[7,16,512]{2,1,0:T(8,128)}, f32[7,16,512]{2,1,0:T(8,128)}, f32[7,16,512]{2,1,0:T(8,128)}, f32[7,16,512]{2,1,0:T(8,128)}, f32[7,2,512]{2,1,0:T(2,...) custom-call(s32[2]{0:T(128)} %pad_add_fusion.refs_0_, f32[1,512]{1,0:T(1,128)} %constant.20.refs_1_, ...), custom_call_target="tpu_custom_call" | custom-call | tf_op jit(solution)/shard_map/stage1/pallas_call | solution.py:320
  57.3 2.7 %collective-permute-start.7 = (f32[7,16,512]{2,1,0:T(8,128)}, f32[7,16,512]{2,1,0:T(8,128)S(1)}, u32[]{:S(2)}, u32[]{:S(2)}) collective-permute-start(f32[7,16,512]{2,1,0:T(8,128)} %get-tuple-element.43.refs_10_), channel_id=1, source_target_pairs={{0,3},{1,0},{2,1},{3,2},{4,7},{5,4},{6,5},{7,6},{8,11},{9,8},{10,9... | collective-permute-start | bytes 688136 | tf_op jit(solution)/shard_map/ppermute | solution.py:336
  60.0 1.5 %collective-permute-done.10 = f32[32,1,128]{2,1,0:T(1,128)} collective-permute-done((f32[32,1,128]{2,1,0:T(1,128)}, f32[32,1,128]{2,1,0:T(1,128)}, u32[]{:S(2)}, u32[]{:S(2)}) %collective-permute-start.10) | collective-permute-done | bytes 16416 | tf_op jit(solution)/shard_map/ppermute | solution.py:339
  61.6 4.8 %all-to-all-start.2 = ((f32[32,1,128]{2,1,0:T(1,128)}), f32[32,1,128]{2,1,0:T(1,128)S(1)}, u32[]{:S(2)}, u32[]{:S(2)}) async-start(f32[32,1,128]{2,1,0:T(1,128)} %collective-permute-done.10), calls=%async_computation.2 | async-start | bytes 32768 | tf_op jit(solution)/shard_map/all_to_all | solution.py:340
  66.3 1.5 %collective-permute-start.8 = (f32[7,2,512]{2,1,0:T(2,128)}, f32[7,2,512]{2,1,0:T(2,128)S(1)}, u32[]{:S(2)}, u32[]{:S(2)}) collective-permute-start(f32[7,2,512]{2,1,0:T(2,128)} %get-tuple-element.44), channel_id=1, source_target_pairs={{0,4},{4,8},{8,12},{12,16},{16,20},{20,24},{24,28},{28,32},{32,36}... | collective-permute-start | bytes 86024 | tf_op jit(solution)/shard_map/ppermute | solution.py:336
  68.4 2.1 %collective-permute-done.8.refs_6_ = f32[7,2,512]{2,1,0:T(2,128)S(1)} collective-permute-done((f32[7,2,512]{2,1,0:T(2,128)}, f32[7,2,512]{2,1,0:T(2,128)S(1)}, u32[]{:S(2)}, u32[]{:S(2)}) %collective-permute-start.8) | collective-permute-done | bytes 28704 | tf_op jit(solution)/shard_map/ppermute | solution.py:336
  70.5 1.3 collective-permute-done.9.refs_7_
  71.8 3.4 %all-to-all-done.2.refs_8_ = f32[32,1,128]{2,1,0:T(1,128)S(1)} async-done(((f32[32,1,128]{2,1,0:T(1,128)}), f32[32,1,128]{2,1,0:T(1,128)S(1)}, u32[]{:S(2)}, u32[]{:S(2)}) %all-to-all-start.2) | async-done | bytes 16416 | tf_op jit(solution)/shard_map/all_to_all | solution.py:340
  75.9 4.2 %stage2.1 = (f32[7,16,512]{2,1,0:T(8,128)}, f32[7,16,512]{2,1,0:T(8,128)}, f32[7,16,512]{2,1,0:T(8,128)}, f32[7,16,512]{2,1,0:T(8,128)}, f32[7,2,512]{2,1,0:T(2,...) custom-call(s32[2]{0:T(128)} %pad_add_fusion.refs_0_, f32[1,512]{1,0:T(1,128)} %constant.20.refs_1_, ...), custom_call_target="tpu_custom_call" | custom-call | tf_op jit(solution)/shard_map/stage2/pallas_call | solution.py:320
  80.2 3.2 %collective-permute-start.12 = (f32[7,16,512]{2,1,0:T(8,128)}, f32[7,16,512]{2,1,0:T(8,128)S(1)}, u32[]{:S(2)}, u32[]{:S(2)}) collective-permute-start(f32[7,16,512]{2,1,0:T(8,128)} %get-tuple-element.50.refs_10_), channel_id=1, source_target_pairs={{0,3},{1,0},{2,1},{3,2},{4,7},{5,4},{6,5},{7,6},{8,11},{9,8},{10,9... | collective-permute-start | bytes 688136 | tf_op jit(solution)/shard_map/ppermute | solution.py:336
  83.4 1.5 %collective-permute-done.15 = f32[32,1,128]{2,1,0:T(1,128)} collective-permute-done((f32[32,1,128]{2,1,0:T(1,128)}, f32[32,1,128]{2,1,0:T(1,128)}, u32[]{:S(2)}, u32[]{:S(2)}) %collective-permute-start.15) | collective-permute-done | bytes 16416 | tf_op jit(solution)/shard_map/ppermute | solution.py:339
  85.0 8.6 %all-to-all-start.3 = ((f32[32,1,128]{2,1,0:T(1,128)}), f32[32,1,128]{2,1,0:T(1,128)S(1)}, u32[]{:S(2)}, u32[]{:S(2)}) async-start(f32[32,1,128]{2,1,0:T(1,128)} %collective-permute-done.15), calls=%async_computation.3 | async-start | bytes 32768 | tf_op jit(solution)/shard_map/all_to_all | solution.py:340
  93.6 1.5 %collective-permute-start.13 = (f32[7,2,512]{2,1,0:T(2,128)}, f32[7,2,512]{2,1,0:T(2,128)S(1)}, u32[]{:S(2)}, u32[]{:S(2)}) collective-permute-start(f32[7,2,512]{2,1,0:T(2,128)} %get-tuple-element.51), channel_id=1, source_target_pairs={{0,4},{4,8},{8,12},{12,16},{16,20},{20,24},{24,28},{28,32},{32,36}... | collective-permute-start | bytes 86024 | tf_op jit(solution)/shard_map/ppermute | solution.py:336
  95.7 2.1 %collective-permute-done.13.refs_6_ = f32[7,2,512]{2,1,0:T(2,128)S(1)} collective-permute-done((f32[7,2,512]{2,1,0:T(2,128)}, f32[7,2,512]{2,1,0:T(2,128)S(1)}, u32[]{:S(2)}, u32[]{:S(2)}) %collective-permute-start.13) | collective-permute-done | bytes 28704 | tf_op jit(solution)/shard_map/ppermute | solution.py:336
  99.0 3.2 %all-to-all-done.3.refs_8_ = f32[32,1,128]{2,1,0:T(1,128)S(1)} async-done(((f32[32,1,128]{2,1,0:T(1,128)}), f32[32,1,128]{2,1,0:T(1,128)S(1)}, u32[]{:S(2)}, u32[]{:S(2)}) %all-to-all-start.3) | async-done | bytes 16416 | tf_op jit(solution)/shard_map/all_to_all | solution.py:340
  103.0 4.2 %stage3.1 = (f32[7,16,512]{2,1,0:T(8,128)}, f32[7,16,512]{2,1,0:T(8,128)}, f32[7,16,512]{2,1,0:T(8,128)}, f32[7,16,512]{2,1,0:T(8,128)}, f32[7,2,512]{2,1,0:T(2,...) custom-call(s32[2]{0:T(128)} %pad_add_fusion.refs_0_, f32[1,512]{1,0:T(1,128)} %constant.20.refs_1_, ...), custom_call_target="tpu_custom_call" | custom-call | tf_op jit(solution)/shard_map/stage3/pallas_call | solution.py:320
  107.3 3.2 %collective-permute-start.17 = (f32[7,16,512]{2,1,0:T(8,128)}, f32[7,16,512]{2,1,0:T(8,128)S(1)}, u32[]{:S(2)}, u32[]{:S(2)}) collective-permute-start(f32[7,16,512]{2,1,0:T(8,128)} %get-tuple-element.57.refs_10_), channel_id=1, source_target_pairs={{0,3},{1,0},{2,1},{3,2},{4,7},{5,4},{6,5},{7,6},{8,11},{9,8},{10,9... | collective-permute-start | bytes 688136 | tf_op jit(solution)/shard_map/ppermute | solution.py:336
  110.5 1.5 %collective-permute-done.20 = f32[32,1,128]{2,1,0:T(1,128)} collective-permute-done((f32[32,1,128]{2,1,0:T(1,128)}, f32[32,1,128]{2,1,0:T(1,128)}, u32[]{:S(2)}, u32[]{:S(2)}) %collective-permute-start.20) | collective-permute-done | bytes 16416 | tf_op jit(solution)/shard_map/ppermute | solution.py:339
  112.1 8.7 %all-to-all-start.4 = ((f32[32,1,128]{2,1,0:T(1,128)}), f32[32,1,128]{2,1,0:T(1,128)S(1)}, u32[]{:S(2)}, u32[]{:S(2)}) async-start(f32[32,1,128]{2,1,0:T(1,128)} %collective-permute-done.20), calls=%async_computation.4 | async-start | bytes 32768 | tf_op jit(solution)/shard_map/all_to_all | solution.py:340
  120.7 1.5 %collective-permute-start.18 = (f32[7,2,512]{2,1,0:T(2,128)}, f32[7,2,512]{2,1,0:T(2,128)S(1)}, u32[]{:S(2)}, u32[]{:S(2)}) collective-permute-start(f32[7,2,512]{2,1,0:T(2,128)} %get-tuple-element.58), channel_id=1, source_target_pairs={{0,4},{4,8},{8,12},{12,16},{16,20},{20,24},{24,28},{28,32},{32,36}... | collective-permute-start | bytes 86024 | tf_op jit(solution)/shard_map/ppermute | solution.py:336
  122.9 2.1 %collective-permute-done.18.refs_6_ = f32[7,2,512]{2,1,0:T(2,128)S(1)} collective-permute-done((f32[7,2,512]{2,1,0:T(2,128)}, f32[7,2,512]{2,1,0:T(2,128)S(1)}, u32[]{:S(2)}, u32[]{:S(2)}) %collective-permute-start.18) | collective-permute-done | bytes 28704 | tf_op jit(solution)/shard_map/ppermute | solution.py:336
  126.2 3.2 %all-to-all-done.4.refs_8_ = f32[32,1,128]{2,1,0:T(1,128)S(1)} async-done(((f32[32,1,128]{2,1,0:T(1,128)}), f32[32,1,128]{2,1,0:T(1,128)S(1)}, u32[]{:S(2)}, u32[]{:S(2)}) %all-to-all-start.4) | async-done | bytes 16416 | tf_op jit(solution)/shard_map/all_to_all | solution.py:340
  130.2 3.3 %stage4.1 = (f32[1,2,16,512]{3,2,1,0:T(8,128)}, f32[1,3,2,16,512]{4,3,2,1,0:T(8,128)}, f32[1,3,2,16,512]{4,3,2,1,0:T(8,128)}) custom-call(s32[2]{0:T(128)} %pad_add_fusion.refs_0_, f32[1,512]{1,0:T(1,128)} %constant.20.refs_1_, f32[7,16,512]{2,1,0:T(8,128)} %get-tuple-element.33.low_ref.refs_2_, f32[7,16,512]{2,1,0:T(8,128)} %get-tuple-element.34.high_ref.refs_3_, ...), custom_call_target="tpu_custom_call" | custom-call | tf_op jit(solution)/shard_map/stage4/pallas_call | solution.py:320
  (83 shorter events, 10.6 us)
Async XLA Ops:
  5.5 46.5 %collective-permute-start.1 = (f32[7,16,512]{2,1,0:T(8,128)}, f32[7,16,512]{2,1,0:T(8,128)S(1)}, u32[]{:S(2)}, u32[]{:S(2)}) collective-permute-start(f32[7,16,512]{2,1,0:T(8,128)} %get-tuple-element.33.low_ref.refs_2_), channel_id=1, source_target_pairs={{0,3},{1,0},{2,1},{3,2},{4,7},{5,4},{6,5},{7,6},{8,11},{9,8},{10,9... | collective-permute-start | bytes 688136 | tf_op jit(solution)/shard_map/ppermute | solution.py:336
  8.6 43.5 %collective-permute-start = (f32[7,16,512]{2,1,0:T(8,128)}, f32[7,16,512]{2,1,0:T(8,128)S(1)}, u32[]{:S(2)}, u32[]{:S(2)}) collective-permute-start(f32[7,16,512]{2,1,0:T(8,128)} %get-tuple-element.34.high_ref.refs_3_), channel_id=1, source_target_pairs={{0,1},{1,2},{2,3},{3,0},{4,5},{5,6},{6,7},{7,4},{8,9},{9,10},{10,1... | collective-permute-start | bytes 688136 | tf_op jit(solution)/shard_map/ppermute | solution.py:336
  8.6 1.4 %collective-permute-start.4 = (f32[32,1,128]{2,1,0:T(1,128)}, f32[32,1,128]{2,1,0:T(1,128)S(1)}, u32[]{:S(2)}, u32[]{:S(2)}) collective-permute-start(f32[32,1,128]{2,1,0:T(1,128)} %get-tuple-element.37), channel_id=1, source_target_pairs={{0,128},{128,0},{1,129},{129,1},{2,130},{130,2},{3,131},{131,3},{4... | collective-permute-start | bytes 49160 | tf_op jit(solution)/shard_map/ppermute | solution.py:339
  33.1 2.0 %collective-permute-start.5 = (f32[32,1,128]{2,1,0:T(1,128)}, f32[32,1,128]{2,1,0:T(1,128)}, u32[]{:S(2)}, u32[]{:S(2)}) collective-permute-start(f32[32,1,128]{2,1,0:T(1,128)} %get-tuple-element.38), channel_id=1, source_target_pairs={{0,128},{128,0},{1,129},{129,1},{2,130},{130,2},{3,131},{131,3},{4... | collective-permute-start | bytes 49160 | tf_op jit(solution)/shard_map/ppermute | solution.py:339
  33.1 10.9 %collective-permute-start.2 = (f32[7,2,512]{2,1,0:T(2,128)S(1)}, f32[7,2,512]{2,1,0:T(2,128)S(1)}, u32[]{:S(2)}, u32[]{:S(2)}) collective-permute-start(f32[7,2,512]{2,1,0:T(2,128)S(1)} %copy-done.23), channel_id=1, source_target_pairs={{0,4},{4,8},{8,12},{12,16},{16,20},{20,24},{24,28},{28,32},{32,36}... | collective-permute-start | bytes 86024 | tf_op jit(solution)/shard_map/ppermute | solution.py:336
  33.7 10.3 %collective-permute-start.3 = (f32[7,2,512]{2,1,0:T(2,128)S(1)}, f32[7,2,512]{2,1,0:T(2,128)S(1)}, u32[]{:S(2)}, u32[]{:S(2)}) collective-permute-start(f32[7,2,512]{2,1,0:T(2,128)S(1)} %copy-done.22), channel_id=1, source_target_pairs={{0,124},{4,0},{8,4},{12,8},{16,12},{20,16},{24,20},{28,24},{32,28}... | collective-permute-start | bytes 86024 | tf_op jit(solution)/shard_map/ppermute | solution.py:336
  35.1 16.9 %all-to-all-start.1 = ((f32[32,1,128]{2,1,0:T(1,128)}), f32[32,1,128]{2,1,0:T(1,128)S(1)}, u32[]{:S(2)}, u32[]{:S(2)}) async-start(f32[32,1,128]{2,1,0:T(1,128)} %collective-permute-done.5), calls=%async_computation.1 | async-start | bytes 32768 | tf_op jit(solution)/shard_map/all_to_all | solution.py:340
  44.0 8.0 %copy-start.18 = (f32[7,2,512]{2,1,0:T(2,128)}, f32[7,2,512]{2,1,0:T(2,128)S(1)}, u32[]{:S(2)}) copy-start(f32[7,2,512]{2,1,0:T(2,128)S(1)} %collective-permute-done.2.refs_6_) | copy-start | bytes 86020
  44.0 8.0 %copy-start.19 = (f32[7,2,512]{2,1,0:T(2,128)}, f32[7,2,512]{2,1,0:T(2,128)S(1)}, u32[]{:S(2)}) copy-start(f32[7,2,512]{2,1,0:T(2,128)S(1)} %collective-permute-done.3.refs_7_) | copy-start | bytes 86020
  56.7 11.2 %copy-start.26 = (f32[7,2,512]{2,1,0:T(2,128)S(1)}, f32[7,2,512]{2,1,0:T(2,128)}, u32[]{:S(2)}) copy-start(f32[7,2,512]{2,1,0:T(2,128)} %get-tuple-element.45) | copy-start | bytes 86020
  56.7 18.5 %collective-permute-start.6 = (f32[7,16,512]{2,1,0:T(8,128)}, f32[7,16,512]{2,1,0:T(8,128)S(1)}, u32[]{:S(2)}, u32[]{:S(2)}) collective-permute-start(f32[7,16,512]{2,1,0:T(8,128)} %get-tuple-element.42.refs_11_), channel_id=1, source_target_pairs={{0,1},{1,2},{2,3},{3,0},{4,5},{5,6},{6,7},{7,4},{8,9},{9,10},{10,1... | collective-permute-start | bytes 688136 | tf_op jit(solution)/shard_map/ppermute | solution.py:336
  57.3 17.8 %collective-permute-start.7 = (f32[7,16,512]{2,1,0:T(8,128)}, f32[7,16,512]{2,1,0:T(8,128)S(1)}, u32[]{:S(2)}, u32[]{:S(2)}) collective-permute-start(f32[7,16,512]{2,1,0:T(8,128)} %get-tuple-element.43.refs_10_), channel_id=1, source_target_pairs={{0,3},{1,0},{2,1},{3,2},{4,7},{5,4},{6,5},{7,6},{8,11},{9,8},{10,9... | collective-permute-start | bytes 688136 | tf_op jit(solution)/shard_map/ppermute | solution.py:336
  60.0 1.5 %collective-permute-start.10 = (f32[32,1,128]{2,1,0:T(1,128)}, f32[32,1,128]{2,1,0:T(1,128)}, u32[]{:S(2)}, u32[]{:S(2)}) collective-permute-start(f32[32,1,128]{2,1,0:T(1,128)} %get-tuple-element.46), channel_id=1, source_target_pairs={{0,128},{128,0},{1,129},{129,1},{2,130},{130,2},{3,131},{131,3},{4... | collective-permute-start | bytes 49160 | tf_op jit(solution)/shard_map/ppermute | solution.py:339
  61.6 13.6 %all-to-all-start.2 = ((f32[32,1,128]{2,1,0:T(1,128)}), f32[32,1,128]{2,1,0:T(1,128)S(1)}, u32[]{:S(2)}, u32[]{:S(2)}) async-start(f32[32,1,128]{2,1,0:T(1,128)} %collective-permute-done.10), calls=%async_computation.2 | async-start | bytes 32768 | tf_op jit(solution)/shard_map/all_to_all | solution.py:340
  66.3 4.2 %collective-permute-start.8 = (f32[7,2,512]{2,1,0:T(2,128)}, f32[7,2,512]{2,1,0:T(2,128)S(1)}, u32[]{:S(2)}, u32[]{:S(2)}) collective-permute-start(f32[7,2,512]{2,1,0:T(2,128)} %get-tuple-element.44), channel_id=1, source_target_pairs={{0,4},{4,8},{8,12},{12,16},{16,20},{20,24},{24,28},{28,32},{32,36}... | collective-permute-start | bytes 86024 | tf_op jit(solution)/shard_map/ppermute | solution.py:336
  67.9 3.9 %collective-permute-start.9 = (f32[7,2,512]{2,1,0:T(2,128)S(1)}, f32[7,2,512]{2,1,0:T(2,128)S(1)}, u32[]{:S(2)}, u32[]{:S(2)}) collective-permute-start(f32[7,2,512]{2,1,0:T(2,128)S(1)} %copy-done.26), channel_id=1, source_target_pairs={{0,124},{4,0},{8,4},{12,8},{16,12},{20,16},{24,20},{28,24},{32,28}... | collective-permute-start | bytes 86024 | tf_op jit(solution)/shard_map/ppermute | solution.py:336
  70.5 4.6 %copy-start.14 = (f32[7,2,512]{2,1,0:T(2,128)}, f32[7,2,512]{2,1,0:T(2,128)S(1)}, u32[]{:S(2)}) copy-start(f32[7,2,512]{2,1,0:T(2,128)S(1)} %collective-permute-done.8.refs_6_) | copy-start | bytes 86020
  80.1 15.0 %copy-start.25 = (f32[7,2,512]{2,1,0:T(2,128)S(1)}, f32[7,2,512]{2,1,0:T(2,128)}, u32[]{:S(2)}) copy-start(f32[7,2,512]{2,1,0:T(2,128)} %get-tuple-element.52) | copy-start | bytes 86020
  80.1 22.1 %collective-permute-start.11 = (f32[7,16,512]{2,1,0:T(8,128)}, f32[7,16,512]{2,1,0:T(8,128)S(1)}, u32[]{:S(2)}, u32[]{:S(2)}) collective-permute-start(f32[7,16,512]{2,1,0:T(8,128)} %get-tuple-element.49.refs_11_), channel_id=1, source_target_pairs={{0,1},{1,2},{2,3},{3,0},{4,5},{5,6},{6,7},{7,4},{8,9},{9,10},{10,1... | collective-permute-start | bytes 688136 | tf_op jit(solution)/shard_map/ppermute | solution.py:336
  80.2 22.0 %collective-permute-start.12 = (f32[7,16,512]{2,1,0:T(8,128)}, f32[7,16,512]{2,1,0:T(8,128)S(1)}, u32[]{:S(2)}, u32[]{:S(2)}) collective-permute-start(f32[7,16,512]{2,1,0:T(8,128)} %get-tuple-element.50.refs_10_), channel_id=1, source_target_pairs={{0,3},{1,0},{2,1},{3,2},{4,7},{5,4},{6,5},{7,6},{8,11},{9,8},{10,9... | collective-permute-start | bytes 688136 | tf_op jit(solution)/shard_map/ppermute | solution.py:336
  83.4 1.5 %collective-permute-start.15 = (f32[32,1,128]{2,1,0:T(1,128)}, f32[32,1,128]{2,1,0:T(1,128)}, u32[]{:S(2)}, u32[]{:S(2)}) collective-permute-start(f32[32,1,128]{2,1,0:T(1,128)} %get-tuple-element.53), channel_id=1, source_target_pairs={{0,128},{128,0},{1,129},{129,1},{2,130},{130,2},{3,131},{131,3},{4... | collective-permute-start | bytes 49160 | tf_op jit(solution)/shard_map/ppermute | solution.py:339
  85.0 17.3 %all-to-all-start.3 = ((f32[32,1,128]{2,1,0:T(1,128)}), f32[32,1,128]{2,1,0:T(1,128)S(1)}, u32[]{:S(2)}, u32[]{:S(2)}) async-start(f32[32,1,128]{2,1,0:T(1,128)} %collective-permute-done.15), calls=%async_computation.3 | async-start | bytes 32768 | tf_op jit(solution)/shard_map/all_to_all | solution.py:340
  93.6 4.2 %collective-permute-start.13 = (f32[7,2,512]{2,1,0:T(2,128)}, f32[7,2,512]{2,1,0:T(2,128)S(1)}, u32[]{:S(2)}, u32[]{:S(2)}) collective-permute-start(f32[7,2,512]{2,1,0:T(2,128)} %get-tuple-element.51), channel_id=1, source_target_pairs={{0,4},{4,8},{8,12},{12,16},{16,20},{20,24},{24,28},{28,32},{32,36}... | collective-permute-start | bytes 86024 | tf_op jit(solution)/shard_map/ppermute | solution.py:336
  95.1 3.9 %collective-permute-start.14 = (f32[7,2,512]{2,1,0:T(2,128)S(1)}, f32[7,2,512]{2,1,0:T(2,128)S(1)}, u32[]{:S(2)}, u32[]{:S(2)}) collective-permute-start(f32[7,2,512]{2,1,0:T(2,128)S(1)} %copy-done.25), channel_id=1, source_target_pairs={{0,124},{4,0},{8,4},{12,8},{16,12},{20,16},{24,20},{28,24},{32,28}... | collective-permute-start | bytes 86024 | tf_op jit(solution)/shard_map/ppermute | solution.py:336
  97.8 4.5 %copy-start.12 = (f32[7,2,512]{2,1,0:T(2,128)}, f32[7,2,512]{2,1,0:T(2,128)S(1)}, u32[]{:S(2)}) copy-start(f32[7,2,512]{2,1,0:T(2,128)S(1)} %collective-permute-done.13.refs_6_) | copy-start | bytes 86020
  107.2 15.1 %copy-start.24 = (f32[7,2,512]{2,1,0:T(2,128)S(1)}, f32[7,2,512]{2,1,0:T(2,128)}, u32[]{:S(2)}) copy-start(f32[7,2,512]{2,1,0:T(2,128)} %get-tuple-element.59) | copy-start | bytes 86020
  107.2 22.2 %collective-permute-start.16 = (f32[7,16,512]{2,1,0:T(8,128)}, f32[7,16,512]{2,1,0:T(8,128)S(1)}, u32[]{:S(2)}, u32[]{:S(2)}) collective-permute-start(f32[7,16,512]{2,1,0:T(8,128)} %get-tuple-element.56.refs_11_), channel_id=1, source_target_pairs={{0,1},{1,2},{2,3},{3,0},{4,5},{5,6},{6,7},{7,4},{8,9},{9,10},{10,1... | collective-permute-start | bytes 688136 | tf_op jit(solution)/shard_map/ppermute | solution.py:336
  107.3 22.1 %collective-permute-start.17 = (f32[7,16,512]{2,1,0:T(8,128)}, f32[7,16,512]{2,1,0:T(8,128)S(1)}, u32[]{:S(2)}, u32[]{:S(2)}) collective-permute-start(f32[7,16,512]{2,1,0:T(8,128)} %get-tuple-element.57.refs_10_), channel_id=1, source_target_pairs={{0,3},{1,0},{2,1},{3,2},{4,7},{5,4},{6,5},{7,6},{8,11},{9,8},{10,9... | collective-permute-start | bytes 688136 | tf_op jit(solution)/shard_map/ppermute | solution.py:336
  110.5 1.5 %collective-permute-start.20 = (f32[32,1,128]{2,1,0:T(1,128)}, f32[32,1,128]{2,1,0:T(1,128)}, u32[]{:S(2)}, u32[]{:S(2)}) collective-permute-start(f32[32,1,128]{2,1,0:T(1,128)} %get-tuple-element.60), channel_id=1, source_target_pairs={{0,128},{128,0},{1,129},{129,1},{2,130},{130,2},{3,131},{131,3},{4... | collective-permute-start | bytes 49160 | tf_op jit(solution)/shard_map/ppermute | solution.py:339
  112.1 17.3 %all-to-all-start.4 = ((f32[32,1,128]{2,1,0:T(1,128)}), f32[32,1,128]{2,1,0:T(1,128)S(1)}, u32[]{:S(2)}, u32[]{:S(2)}) async-start(f32[32,1,128]{2,1,0:T(1,128)} %collective-permute-done.20), calls=%async_computation.4 | async-start | bytes 32768 | tf_op jit(solution)/shard_map/all_to_all | solution.py:340
  120.7 4.2 %collective-permute-start.18 = (f32[7,2,512]{2,1,0:T(2,128)}, f32[7,2,512]{2,1,0:T(2,128)S(1)}, u32[]{:S(2)}, u32[]{:S(2)}) collective-permute-start(f32[7,2,512]{2,1,0:T(2,128)} %get-tuple-element.58), channel_id=1, source_target_pairs={{0,4},{4,8},{8,12},{12,16},{16,20},{20,24},{24,28},{28,32},{32,36}... | collective-permute-start | bytes 86024 | tf_op jit(solution)/shard_map/ppermute | solution.py:336
  122.3 3.9 %collective-permute-start.19 = (f32[7,2,512]{2,1,0:T(2,128)S(1)}, f32[7,2,512]{2,1,0:T(2,128)S(1)}, u32[]{:S(2)}, u32[]{:S(2)}) collective-permute-start(f32[7,2,512]{2,1,0:T(2,128)S(1)} %copy-done.24), channel_id=1, source_target_pairs={{0,124},{4,0},{8,4},{12,8},{16,12},{20,16},{24,20},{28,24},{32,28}... | collective-permute-start | bytes 86024 | tf_op jit(solution)/shard_map/ppermute | solution.py:336
  (20 other events, 31.2 us)

commit v2 on v1

--- a/solution.py
+++ b/solution.py
@@ -90,7 +90,7 @@
 
 
 def open_kernel(
-    density, momentum, magnetic, device, phi, theta, weight, turn, cos_in, sin_in,
+    density, momentum, magnetic, device, phi, theta, weight, turn,
     low_ref, high_ref, first_ref, last_ref, ask_ref, table_ref,
 ):
     for level, ref in ((0, low_ref), (1, high_ref)):
@@ -103,11 +103,11 @@
                 value = magnetic[0, f - 4, level]
             ref[f] = value
             send_rows(first_ref, last_ref, level, f, value)
-    rows = device.shape[1]
+    rows = device.shape[2]
     one, two = iota((rows, rows), 0), iota((rows, rows), 1)
     eye = one == two
-    dev_col = device[0]
-    dev_row = jnp.sum(jnp.where(eye, jnp.broadcast_to(dev_col, (rows, rows)), 0), axis=0, keepdims=True)
+    dev_row = device[0]
+    dev_col = jnp.sum(jnp.where(eye, jnp.broadcast_to(dev_row, (rows, rows)), 0), axis=1, keepdims=True)
     same = dev_col == dev_row
     rank_row = jnp.sum(jnp.where(same & (one < two), 1, 0), axis=0, keepdims=True)
     rank_col = jnp.sum(jnp.where(same & (two < one), 1, 0), axis=1, keepdims=True)
@@ -119,7 +119,7 @@
     theta_col = column(theta[...].astype(jnp.float32))
     weights = weight[0]
     lane = iota((rows, 128), 1)
-    items = [phi_col, theta_col] + [weights[:, c : c + 1] for c in range(4)]
+    items = [phi_col, theta_col] + [column(weights[c : c + 1, :]) for c in range(4)]
     record = jnp.zeros((rows, 128), jnp.float32)
     for at, item in enumerate(items):
         record = jnp.where(lane == at, item, record)
@@ -130,8 +130,8 @@
         asked = asked + jnp.dot(placing, moved, precision=HIGHEST, preferred_element_type=jnp.float32)
     ask_ref[...] = asked.reshape(ask_ref.shape)
     picks = jnp.where(((lane & 31) == dev_col) & ((lane >> 5) == rank_col) & (lane < 64), 1.0, 0.0)
-    cosine = column(cos_in[...])
-    sine = column(sin_in[...])
+    cosine = column(jnp.cos(turn[...]))
+    sine = column(jnp.sin(turn[...]))
     picks = jnp.where(lane == 64, cosine, picks)
     table_ref[...] = jnp.where(lane == 65, sine, picks)
 
@@ -167,8 +167,8 @@
 
 def stage_kernel(stage, n_rad, n_ang, *refs):
     last = stage == 4
-    (flags, sines, low0, high0, below, above, before, after, reply, table) = refs[:10]
-    refs = refs[10:]
+    (sines, low0, high0, below, above, before, after, reply, table) = refs[:9]
+    refs = refs[9:]
     if stage == 1:
         low, high = low0, high0
     else:
@@ -182,7 +182,7 @@
         low_out, high_out, acc_low_out, acc_high_out, first_out, last_out, msg_out = refs[2:9]
         refs = refs[9:]
     slope, up, down = refs
-    rad, ang = flags[0], flags[1]
+    rad, ang = lax.axis_index("rad"), lax.axis_index("ang")
     rows_p, rows_t = low.shape[1:]
     invs = [place(rad, n_rad, level, 2) for level in range(2)]
 
@@ -272,7 +272,7 @@
 
     row = iota((rows_p, rows_t), 0)
     for level in range(2):
-        start, now = (low0, low) if level == 0 else (high0, high)
+        start, _ = (low0, low) if level == 0 else (high0, high)
         for f in range(NF):
             lower = pltpu.roll(down[level, f], 1, axis=0)
             lower = jnp.where(row == 0, rim_low[f][level : level + 1, :], lower)
@@ -311,21 +311,23 @@
     n_ang, n_rad = lax.axis_size("ang"), lax.axis_size("rad")
     f32 = jnp.float32
     vmem = pl.BlockSpec(memory_space=pltpu.VMEM)
-    smem = pl.BlockSpec(memory_space=pltpu.SMEM)
-
-    def shape(*dims):
-        return jax.ShapeDtypeStruct(dims, f32)
-
-    def call(kernel, ins, outs, scratch=(), name=None, scalars=0):
+
+    def shape(*dims, final=False):
+        return jax.ShapeDtypeStruct(dims, f32) if final or INTERPRET else pltpu.VMEM(dims, f32)
+
+    def held(value):
+        return value if INTERPRET else pltpu.with_memory_space_constraint(value, pltpu.VMEM)
+
+    def call(kernel, ins, outs, scratch=(), plain=0):
         return pl.pallas_call(
             kernel,
             out_shape=outs,
-            in_specs=[smem] * scalars + [vmem] * (len(ins) - scalars),
+            in_specs=[vmem] * len(ins),
             out_specs=[vmem] * len(outs),
             scratch_shapes=list(scratch),
             interpret=INTERPRET,
-            name=name,
-        )(*ins)
+            compiler_params=pltpu.CompilerParams(vmem_limit_bytes=None if plain > 1 else 12 << 20),
+        )(*[item if at < plain else held(item) for at, item in enumerate(ins)])
 
     level = shape(NF, rows_p, rows_t)
     edge = shape(NF, 2, rows_t)
@@ -333,44 +335,39 @@
 
     def shifted(value, axis, by):
         size = lax.axis_size(axis)
-        return lax.ppermute(value, axis, [(i, (i + by) % size) for i in range(size)])
+        return held(lax.ppermute(value, axis, [(i, (i + by) % size) for i in range(size)]))
 
     def crossed(value):
-        swap = lax.ppermute(value, "panel", [(0, 1), (1, 0)])
-        return lax.all_to_all(swap, "ang", split_axis=0, concat_axis=0, tiled=True)
+        swap = held(lax.ppermute(value, "panel", [(0, 1), (1, 0)]))
+        return held(lax.all_to_all(swap, "ang", split_axis=0, concat_axis=0, tiled=True))
 
     def halos(low, high, first, final):
-        return (
-            shifted(high, "rad", 1),
-            shifted(low, "rad", -1),
-            shifted(final, "ang", 1),
-            shifted(first, "ang", -1),
-        )
-
-    flags = jnp.stack([lax.axis_index("rad"), lax.axis_index("ang")]).astype(jnp.int32)
+        items = ((high, "rad", 1), (low, "rad", -1), (final, "ang", 1), (first, "ang", -1))
+        out = []
+        for item in items:
+            out.append(shifted(*item))
+        return out
+
     theta = math.pi / 4 + (np.arange(rows_t) + 0.5) * (math.pi / 2 / rows_t)
     sines = jnp.asarray((1.0 / np.sin(theta)).astype(np.float32)).reshape(1, rows_t)
 
     low0, high0, first, final, ask, table = call(
         open_kernel,
         [
-            density, momentum, magnetic, partner_device, partner_phi, partner_theta, partner_weight,
-            border_turn, jnp.cos(border_turn), jnp.sin(border_turn),
+            density, momentum, magnetic, jnp.swapaxes(partner_device, 1, 2), partner_phi, partner_theta,
+            jnp.swapaxes(partner_weight, 1, 2), border_turn,
         ],
         [level, level, edge, edge, message, shape(32, 128)],
-        name="open",
+        plain=8,
     )
     around = halos(low0, high0, first, final)
     corner, rowmask, answer = call(
-        asked_kernel,
-        [crossed(ask), low0, high0],
-        [shape(rows_t, 128), shape(rows_p, 128), message],
-        name="asked",
+        asked_kernel, [crossed(ask), low0, high0], [shape(rows_t, 128), shape(rows_p, 128), message]
     )
     low, high, sums = low0, high0, []
     scratch = [pltpu.VMEM((2, NF, rows_p, rows_t), f32) for _ in range(3)]
     for stage in range(1, 5):
-        ins = [flags, sines, low0, high0, *around, crossed(answer), table]
+        ins = [sines, low0, high0, *around, crossed(answer), table]
         if stage > 1:
             ins += [low, high, *sums]
         if stage < 4:
@@ -378,15 +375,15 @@
             outs = [level, level, level, level, edge, edge, message]
         else:
             outs = [
-                shape(1, rows_r, rows_p, rows_t),
-                shape(1, 3, rows_r, rows_p, rows_t),
-                shape(1, 3, rows_r, rows_p, rows_t),
+                shape(1, rows_r, rows_p, rows_t, final=True),
+                shape(1, 3, rows_r, rows_p, rows_t, final=True),
+                shape(1, 3, rows_r, rows_p, rows_t, final=True),
             ]
 
         def kernel(*refs, stage=stage):
             stage_kernel(stage, n_rad, n_ang, *refs)
 
-        result = call(kernel, ins, outs, scratch, name=f"stage{stage}", scalars=1)
+        result = call(kernel, ins, outs, scratch, plain=1)
         if stage == 4:
             return tuple(result)
         low, high, acc_low, acc_high, first, final, answer = result

time: 134 us -> 118 us (0.88)
  Pallas kernels: 20.8 us -> 10.3 us
  local copies, waits for them, and re-layouts: 5.63 us -> 0.68 us
  waiting for transfers between devices: 33.7 us -> 32.3 us
    pallas_call x6, Pallas kernels: 20.8 us -> 10.3 us  [call(): pl.pallas_call(kernel, out_shape=outs, in_specs=[vmem] * len(ins), out_sp...]
    all_to_all x4, waiting for transfers between devices: 17.8 us -> 12.6 us  [crossed(): lax.all_to_all(swap, 'ang', split_axis=0, concat_axis=0, tiled=True)]
    unnamed x56 -> x2, local copies, waits for them, and re-layouts: 4.33 us -> 0.68 us
    ppermute x16, waiting for transfers between devices: 9.98 us -> 13.3 us  [shifted(): lax.ppermute(value, axis, [(i, (i + by) % size) for i in range(size)])]
  transfers between devices with their start and end apart: 25 -> 25, of which waited for: 14 -> 17; matrix products, arithmetic and copies ran while one was open for 0% -> 0% of each run, Pallas kernels for 2% -> 1%
where the time goes in v2:
time: 118 us; the launch traced here: 117 us
  starting transfers between devices  52.8 us (45%)
  waiting for transfers between devices  32.3 us (27%)
  blocking collectives  20 us (17%)
  Pallas kernels  10.3 us (9%)
    all_to_all x4, starting transfers between devices, crossed(): lax.all_to_all(swap, 'ang', split_axis=0, concat_axis=0, tiled=True)  31.2 us
    ppermute x16, starting transfers between devices, shifted(): lax.ppermute(value, axis, [(i, (i + by) % size) for i in range(size)])  21.5 us
    all_to_all x1, blocking collectives, crossed(): lax.all_to_all(swap, 'ang', split_axis=0, concat_axis=0, tiled=True)  20 us
    ppermute x16, waiting for transfers between devices, shifted(): lax.ppermute(value, axis, [(i, (i + by) % size) for i in range(size)])  13.3 us
    all_to_all x4, waiting for transfers between devices, crossed(): lax.all_to_all(swap, 'ang', split_axis=0, concat_axis=0, tiled=True)  12.6 us
    pallas_call x6, Pallas kernels, call(): pl.pallas_call(kernel, out_shape=outs, in_specs=[vmem] * len(ins), out_sp...  10.3 us
    ppermute x5, waiting for transfers between devices, crossed(): swap = held(lax.ppermute(value, 'panel', [(0, 1), (1, 0)]))  6.42 us
  transfers between devices with their start and end apart: 25, of which 17 were waited for; matrix products, arithmetic and copies ran while one was open for 0% of the time, Pallas kernels for 1%

profile of v2, /device:TPU:2, one launch (start us, length us, event | category | flops | bytes accessed | tf_op | source)
XLA Modules:
  0.0 116.8 jit_solution(15613674505373740800)
XLA Ops:
  0.6 1.5 %shard_map.112 = (f32[7,16,512]{2,1,0:T(8,128)S(1)}, f32[7,16,512]{2,1,0:T(8,128)S(1)}, f32[7,2,512]{2,1,0:T(2,128)S(1)}, f32[7,2,512]{2,1,0:T(2,128)S(1)}, f32[...) custom-call(f32[1,2,16,512]{3,2,1,0:T(8,128)} %density.1, f32[1,3,2,16,512]{4,3,2,1,0:T(8,128)} %momentum.1, ...), custom_call_target="tpu_custom_call" | custom-call | tf_op jit(solution)/shard_map/pallas_call | solution.py:322
  2.1 3.1 %collective-permute-start.1 = (f32[7,16,512]{2,1,0:T(8,128)S(1)}, f32[7,16,512]{2,1,0:T(8,128)S(1)}, u32[]{:S(2)}, u32[]{:S(2)}) collective-permute-start(f32[7,16,512]{2,1,0:T(8,128)S(1)} %get-tuple-element.33.low_ref.refs_1_), channel_id=1, source_target_pairs={{0,3},{1,0},{2,1},{3,2},{4,7},{5,4},{6,5},{7,6},{8,11},{9,8},{10,9... | collective-permute-start | bytes 688136 | tf_op jit(solution)/shard_map/ppermute | solution.py:338
  6.4 20.0 %all_to_all.25.asked_ref = f32[32,1,128]{2,1,0:T(1,128)S(1)} all-to-all(f32[32,1,128]{2,1,0:T(1,128)S(1)} %collective-permute-done.4), channel_id=1, replica_groups=mesh['panel'=2,'ang'=32,'rad'=4] {'ang'}, dimensions={0} | all-to-all | bytes 32768 | tf_op jit(solution)/shard_map/all_to_all | solution.py:342
  26.4 1.3 %shard_map.113 = (f32[512,128]{1,0:T(8,128)S(1)}, f32[16,128]{1,0:T(8,128)S(1)}, f32[32,1,128]{2,1,0:T(1,128)S(1)}) custom-call(f32[32,1,128]{2,1,0:T(1,128)S(1)} %all_to_all.25.asked_ref, f32[7,16,512]{2,1,0:T(8,128)S(1)} %get-tuple-element.33.low_ref.refs_1_, f32[7,16,512]{2,1,0:T(8,128)S(1)} %get-tuple-element.34.high_ref.refs_2_), custom_call_target="tpu_custom_call" | custom-call | tf_op jit(solution)/shard_map/pallas_call | solution.py:322
  29.1 4.9 %all-to-all-start.1 = ((f32[32,1,128]{2,1,0:T(1,128)}), f32[32,1,128]{2,1,0:T(1,128)S(1)}, u32[]{:S(2)}, u32[]{:S(2)}) async-start(f32[32,1,128]{2,1,0:T(1,128)} %collective-permute-done.5), calls=%async_computation.1 | async-start | bytes 32768 | tf_op jit(solution)/shard_map/all_to_all | solution.py:342
  34.0 1.5 %collective-permute-start.2 = (f32[7,2,512]{2,1,0:T(2,128)S(1)}, f32[7,2,512]{2,1,0:T(2,128)S(1)}, u32[]{:S(2)}, u32[]{:S(2)}) collective-permute-start(f32[7,2,512]{2,1,0:T(2,128)S(1)} %get-tuple-element.35), channel_id=1, source_target_pairs={{0,4},{4,8},{8,12},{12,16},{16,20},{20,24},{24,28},{28,32},{32,36}... | collective-permute-start | bytes 86024 | tf_op jit(solution)/shard_map/ppermute | solution.py:338
  36.1 1.8 %collective-permute-done.2.refs_5_ = f32[7,2,512]{2,1,0:T(2,128)S(1)} collective-permute-done((f32[7,2,512]{2,1,0:T(2,128)S(1)}, f32[7,2,512]{2,1,0:T(2,128)S(1)}, u32[]{:S(2)}, u32[]{:S(2)}) %collective-permute-start.2) | collective-permute-done | bytes 28704 | tf_op jit(solution)/shard_map/ppermute | solution.py:338
  38.0 1.5 %collective-permute-done.3.refs_6_ = f32[7,2,512]{2,1,0:T(2,128)S(1)} collective-permute-done((f32[7,2,512]{2,1,0:T(2,128)S(1)}, f32[7,2,512]{2,1,0:T(2,128)S(1)}, u32[]{:S(2)}, u32[]{:S(2)}) %collective-permute-start.3) | collective-permute-done | bytes 28704 | tf_op jit(solution)/shard_map/ppermute | solution.py:338
  39.4 3.2 %all-to-all-done.1.refs_7_ = f32[32,1,128]{2,1,0:T(1,128)S(1)} async-done(((f32[32,1,128]{2,1,0:T(1,128)}), f32[32,1,128]{2,1,0:T(1,128)S(1)}, u32[]{:S(2)}, u32[]{:S(2)}) %all-to-all-start.1) | async-done | bytes 16416 | tf_op jit(solution)/shard_map/all_to_all | solution.py:342
  43.4 1.9 %shard_map.114 = (f32[7,16,512]{2,1,0:T(8,128)S(1)}, f32[7,16,512]{2,1,0:T(8,128)S(1)}, f32[7,16,512]{2,1,0:T(8,128)S(1)}, f32[7,16,512]{2,1,0:T(8,128)S(1)}, f3...) custom-call(f32[1,512]{1,0:T(1,128)S(1)} %copy-done, ...), custom_call_target="tpu_custom_call" | custom-call | tf_op jit(solution)/shard_map/pallas_call | solution.py:322
  45.9 2.7 %collective-permute-start.7 = (f32[7,16,512]{2,1,0:T(8,128)S(1)}, f32[7,16,512]{2,1,0:T(8,128)S(1)}, u32[]{:S(2)}, u32[]{:S(2)}) collective-permute-start(f32[7,16,512]{2,1,0:T(8,128)S(1)} %get-tuple-element.43.refs_9_), channel_id=1, source_target_pairs={{0,3},{1,0},{2,1},{3,2},{4,7},{5,4},{6,5},{7,6},{8,11},{9,8},{10,9... | collective-permute-start | bytes 688136 | tf_op jit(solution)/shard_map/ppermute | solution.py:338
  50.0 8.8 %all-to-all-start.2 = ((f32[32,1,128]{2,1,0:T(1,128)}), f32[32,1,128]{2,1,0:T(1,128)S(1)}, u32[]{:S(2)}, u32[]{:S(2)}) async-start(f32[32,1,128]{2,1,0:T(1,128)} %collective-permute-done.10), calls=%async_computation.2 | async-start | bytes 32768 | tf_op jit(solution)/shard_map/all_to_all | solution.py:342
  58.7 1.5 %collective-permute-start.8 = (f32[7,2,512]{2,1,0:T(2,128)S(1)}, f32[7,2,512]{2,1,0:T(2,128)S(1)}, u32[]{:S(2)}, u32[]{:S(2)}) collective-permute-start(f32[7,2,512]{2,1,0:T(2,128)S(1)} %get-tuple-element.44), channel_id=1, source_target_pairs={{0,4},{4,8},{8,12},{12,16},{16,20},{20,24},{24,28},{28,32},{32,36}... | collective-permute-start | bytes 86024 | tf_op jit(solution)/shard_map/ppermute | solution.py:338
  60.8 1.9 %collective-permute-done.8.refs_5_ = f32[7,2,512]{2,1,0:T(2,128)S(1)} collective-permute-done((f32[7,2,512]{2,1,0:T(2,128)S(1)}, f32[7,2,512]{2,1,0:T(2,128)S(1)}, u32[]{:S(2)}, u32[]{:S(2)}) %collective-permute-start.8) | collective-permute-done | bytes 28704 | tf_op jit(solution)/shard_map/ppermute | solution.py:338
  62.7 1.5 %collective-permute-done.9.refs_6_ = f32[7,2,512]{2,1,0:T(2,128)S(1)} collective-permute-done((f32[7,2,512]{2,1,0:T(2,128)S(1)}, f32[7,2,512]{2,1,0:T(2,128)S(1)}, u32[]{:S(2)}, u32[]{:S(2)}) %collective-permute-start.9) | collective-permute-done | bytes 28704 | tf_op jit(solution)/shard_map/ppermute | solution.py:338
  64.2 3.1 %all-to-all-done.2.refs_7_ = f32[32,1,128]{2,1,0:T(1,128)S(1)} async-done(((f32[32,1,128]{2,1,0:T(1,128)}), f32[32,1,128]{2,1,0:T(1,128)S(1)}, u32[]{:S(2)}, u32[]{:S(2)}) %all-to-all-start.2) | async-done | bytes 16416 | tf_op jit(solution)/shard_map/all_to_all | solution.py:342
  67.3 1.9 %shard_map.115 = (f32[7,16,512]{2,1,0:T(8,128)S(1)}, f32[7,16,512]{2,1,0:T(8,128)S(1)}, f32[7,16,512]{2,1,0:T(8,128)S(1)}, f32[7,16,512]{2,1,0:T(8,128)S(1)}, f3...) custom-call(f32[1,512]{1,0:T(1,128)S(1)} %copy-done, ...), custom_call_target="tpu_custom_call" | custom-call | tf_op jit(solution)/shard_map/pallas_call | solution.py:322
  69.3 3.2 %collective-permute-start.12 = (f32[7,16,512]{2,1,0:T(8,128)S(1)}, f32[7,16,512]{2,1,0:T(8,128)S(1)}, u32[]{:S(2)}, u32[]{:S(2)}) collective-permute-start(f32[7,16,512]{2,1,0:T(8,128)S(1)} %get-tuple-element.50.refs_9_), channel_id=1, source_target_pairs={{0,3},{1,0},{2,1},{3,2},{4,7},{5,4},{6,5},{7,6},{8,11},{9,8},{10,9... | collective-permute-start | bytes 688136 | tf_op jit(solution)/shard_map/ppermute | solution.py:338
  72.6 1.3 %collective-permute-done.15 = f32[32,1,128]{2,1,0:T(1,128)} collective-permute-done((f32[32,1,128]{2,1,0:T(1,128)S(1)}, f32[32,1,128]{2,1,0:T(1,128)}, u32[]{:S(2)}, u32[]{:S(2)}) %collective-permute-start.15) | collective-permute-done | bytes 16416 | tf_op jit(solution)/shard_map/ppermute | solution.py:341
  73.9 8.8 %all-to-all-start.3 = ((f32[32,1,128]{2,1,0:T(1,128)}), f32[32,1,128]{2,1,0:T(1,128)S(1)}, u32[]{:S(2)}, u32[]{:S(2)}) async-start(f32[32,1,128]{2,1,0:T(1,128)} %collective-permute-done.15), calls=%async_computation.3 | async-start | bytes 32768 | tf_op jit(solution)/shard_map/all_to_all | solution.py:342
  82.6 1.5 %collective-permute-start.13 = (f32[7,2,512]{2,1,0:T(2,128)S(1)}, f32[7,2,512]{2,1,0:T(2,128)S(1)}, u32[]{:S(2)}, u32[]{:S(2)}) collective-permute-start(f32[7,2,512]{2,1,0:T(2,128)S(1)} %get-tuple-element.51), channel_id=1, source_target_pairs={{0,4},{4,8},{8,12},{12,16},{16,20},{20,24},{24,28},{28,32},{32,36}... | collective-permute-start | bytes 86024 | tf_op jit(solution)/shard_map/ppermute | solution.py:338
  84.7 1.9 %collective-permute-done.13.refs_5_ = f32[7,2,512]{2,1,0:T(2,128)S(1)} collective-permute-done((f32[7,2,512]{2,1,0:T(2,128)S(1)}, f32[7,2,512]{2,1,0:T(2,128)S(1)}, u32[]{:S(2)}, u32[]{:S(2)}) %collective-permute-start.13) | collective-permute-done | bytes 28704 | tf_op jit(solution)/shard_map/ppermute | solution.py:338
  86.6 1.5 %collective-permute-done.14.refs_6_ = f32[7,2,512]{2,1,0:T(2,128)S(1)} collective-permute-done((f32[7,2,512]{2,1,0:T(2,128)S(1)}, f32[7,2,512]{2,1,0:T(2,128)S(1)}, u32[]{:S(2)}, u32[]{:S(2)}) %collective-permute-start.14) | collective-permute-done | bytes 28704 | tf_op jit(solution)/shard_map/ppermute | solution.py:338
  88.1 3.1 %all-to-all-done.3.refs_7_ = f32[32,1,128]{2,1,0:T(1,128)S(1)} async-done(((f32[32,1,128]{2,1,0:T(1,128)}), f32[32,1,128]{2,1,0:T(1,128)S(1)}, u32[]{:S(2)}, u32[]{:S(2)}) %all-to-all-start.3) | async-done | bytes 16416 | tf_op jit(solution)/shard_map/all_to_all | solution.py:342
  91.2 1.9 %shard_map.116 = (f32[7,16,512]{2,1,0:T(8,128)S(1)}, f32[7,16,512]{2,1,0:T(8,128)S(1)}, f32[7,16,512]{2,1,0:T(8,128)S(1)}, f32[7,16,512]{2,1,0:T(8,128)S(1)}, f3...) custom-call(f32[1,512]{1,0:T(1,128)S(1)} %copy-done, ...), custom_call_target="tpu_custom_call" | custom-call | tf_op jit(solution)/shard_map/pallas_call | solution.py:322
  93.2 3.2 %collective-permute-start.17 = (f32[7,16,512]{2,1,0:T(8,128)S(1)}, f32[7,16,512]{2,1,0:T(8,128)S(1)}, u32[]{:S(2)}, u32[]{:S(2)}) collective-permute-start(f32[7,16,512]{2,1,0:T(8,128)S(1)} %get-tuple-element.57.refs_9_), channel_id=1, source_target_pairs={{0,3},{1,0},{2,1},{3,2},{4,7},{5,4},{6,5},{7,6},{8,11},{9,8},{10,9... | collective-permute-start | bytes 688136 | tf_op jit(solution)/shard_map/ppermute | solution.py:338
  97.8 8.8 %all-to-all-start.4 = ((f32[32,1,128]{2,1,0:T(1,128)}), f32[32,1,128]{2,1,0:T(1,128)S(1)}, u32[]{:S(2)}, u32[]{:S(2)}) async-start(f32[32,1,128]{2,1,0:T(1,128)} %collective-permute-done.20), calls=%async_computation.4 | async-start | bytes 32768 | tf_op jit(solution)/shard_map/all_to_all | solution.py:342
  106.6 1.5 %collective-permute-start.18 = (f32[7,2,512]{2,1,0:T(2,128)S(1)}, f32[7,2,512]{2,1,0:T(2,128)S(1)}, u32[]{:S(2)}, u32[]{:S(2)}) collective-permute-start(f32[7,2,512]{2,1,0:T(2,128)S(1)} %get-tuple-element.58), channel_id=1, source_target_pairs={{0,4},{4,8},{8,12},{12,16},{16,20},{20,24},{24,28},{28,32},{32,36}... | collective-permute-start | bytes 86024 | tf_op jit(solution)/shard_map/ppermute | solution.py:338
  108.7 1.9 %collective-permute-done.18.refs_5_ = f32[7,2,512]{2,1,0:T(2,128)S(1)} collective-permute-done((f32[7,2,512]{2,1,0:T(2,128)S(1)}, f32[7,2,512]{2,1,0:T(2,128)S(1)}, u32[]{:S(2)}, u32[]{:S(2)}) %collective-permute-start.18) | collective-permute-done | bytes 28704 | tf_op jit(solution)/shard_map/ppermute | solution.py:338
  110.5 1.5 %collective-permute-done.19.refs_6_ = f32[7,2,512]{2,1,0:T(2,128)S(1)} collective-permute-done((f32[7,2,512]{2,1,0:T(2,128)S(1)}, f32[7,2,512]{2,1,0:T(2,128)S(1)}, u32[]{:S(2)}, u32[]{:S(2)}) %collective-permute-start.19) | collective-permute-done | bytes 28704 | tf_op jit(solution)/shard_map/ppermute | solution.py:338
  112.0 3.1 %all-to-all-done.4.refs_7_ = f32[32,1,128]{2,1,0:T(1,128)S(1)} async-done(((f32[32,1,128]{2,1,0:T(1,128)}), f32[32,1,128]{2,1,0:T(1,128)S(1)}, u32[]{:S(2)}, u32[]{:S(2)}) %all-to-all-start.4) | async-done | bytes 16416 | tf_op jit(solution)/shard_map/all_to_all | solution.py:342
  115.1 1.7 %shard_map.117 = (f32[1,2,16,512]{3,2,1,0:T(8,128)}, f32[1,3,2,16,512]{4,3,2,1,0:T(8,128)}, f32[1,3,2,16,512]{4,3,2,1,0:T(8,128)}) custom-call(f32[1,512]{1,0:T(1,128)S(1)} %copy-done, f32[7,16,512]{2,1,0:T(8,128)S(1)} %get-tuple-element.33.low_ref.refs_1_, f32[7,16,512]{2,1,0:T(8,128)S(1)} %get-tuple-element.34.high_ref.refs_2_, ...), custom_call_target="tpu_custom_call" | custom-call | tf_op jit(solution)/shard_map/pallas_call | solution.py:322
  (27 shorter events, 9.0 us)
Async XLA Ops:
  2.1 40.6 %collective-permute-start.1 = (f32[7,16,512]{2,1,0:T(8,128)S(1)}, f32[7,16,512]{2,1,0:T(8,128)S(1)}, u32[]{:S(2)}, u32[]{:S(2)}) collective-permute-start(f32[7,16,512]{2,1,0:T(8,128)S(1)} %get-tuple-element.33.low_ref.refs_1_), channel_id=1, source_target_pairs={{0,3},{1,0},{2,1},{3,2},{4,7},{5,4},{6,5},{7,6},{8,11},{9,8},{10,9... | collective-permute-start | bytes 688136 | tf_op jit(solution)/shard_map/ppermute | solution.py:338
  5.2 37.5 %collective-permute-start = (f32[7,16,512]{2,1,0:T(8,128)S(1)}, f32[7,16,512]{2,1,0:T(8,128)S(1)}, u32[]{:S(2)}, u32[]{:S(2)}) collective-permute-start(f32[7,16,512]{2,1,0:T(8,128)S(1)} %get-tuple-element.34.high_ref.refs_2_), channel_id=1, source_target_pairs={{0,1},{1,2},{2,3},{3,0},{4,5},{5,6},{6,7},{7,4},{8,9},{9,10},{10,1... | collective-permute-start | bytes 688136 | tf_op jit(solution)/shard_map/ppermute | solution.py:338
  5.2 1.2 %collective-permute-start.4 = (f32[32,1,128]{2,1,0:T(1,128)S(1)}, f32[32,1,128]{2,1,0:T(1,128)S(1)}, u32[]{:S(2)}, u32[]{:S(2)}) collective-permute-start(f32[32,1,128]{2,1,0:T(1,128)S(1)} %get-tuple-element.37), channel_id=1, source_target_pairs={{0,128},{128,0},{1,129},{129,1},{2,130},{130,2},{3,131},{131,3},{4... | collective-permute-start | bytes 49160 | tf_op jit(solution)/shard_map/ppermute | solution.py:341
  27.7 1.4 %collective-permute-start.5 = (f32[32,1,128]{2,1,0:T(1,128)S(1)}, f32[32,1,128]{2,1,0:T(1,128)}, u32[]{:S(2)}, u32[]{:S(2)}) collective-permute-start(f32[32,1,128]{2,1,0:T(1,128)S(1)} %get-tuple-element.38), channel_id=1, source_target_pairs={{0,128},{128,0},{1,129},{129,1},{2,130},{130,2},{3,131},{131,3},{4... | collective-permute-start | bytes 49160 | tf_op jit(solution)/shard_map/ppermute | solution.py:341
  29.1 13.6 %all-to-all-start.1 = ((f32[32,1,128]{2,1,0:T(1,128)}), f32[32,1,128]{2,1,0:T(1,128)S(1)}, u32[]{:S(2)}, u32[]{:S(2)}) async-start(f32[32,1,128]{2,1,0:T(1,128)} %collective-permute-done.5), calls=%async_computation.1 | async-start | bytes 32768 | tf_op jit(solution)/shard_map/all_to_all | solution.py:342
  34.0 4.0 %collective-permute-start.2 = (f32[7,2,512]{2,1,0:T(2,128)S(1)}, f32[7,2,512]{2,1,0:T(2,128)S(1)}, u32[]{:S(2)}, u32[]{:S(2)}) collective-permute-start(f32[7,2,512]{2,1,0:T(2,128)S(1)} %get-tuple-element.35), channel_id=1, source_target_pairs={{0,4},{4,8},{8,12},{12,16},{16,20},{20,24},{24,28},{28,32},{32,36}... | collective-permute-start | bytes 86024 | tf_op jit(solution)/shard_map/ppermute | solution.py:338
  35.6 3.9 %collective-permute-start.3 = (f32[7,2,512]{2,1,0:T(2,128)S(1)}, f32[7,2,512]{2,1,0:T(2,128)S(1)}, u32[]{:S(2)}, u32[]{:S(2)}) collective-permute-start(f32[7,2,512]{2,1,0:T(2,128)S(1)} %get-tuple-element.36), channel_id=1, source_target_pairs={{0,124},{4,0},{8,4},{12,8},{16,12},{20,16},{24,20},{28,24},{32,28}... | collective-permute-start | bytes 86024 | tf_op jit(solution)/shard_map/ppermute | solution.py:338
  42.7 0.7 copy-start
  45.3 22.0 %collective-permute-start.6 = (f32[7,16,512]{2,1,0:T(8,128)S(1)}, f32[7,16,512]{2,1,0:T(8,128)S(1)}, u32[]{:S(2)}, u32[]{:S(2)}) collective-permute-start(f32[7,16,512]{2,1,0:T(8,128)S(1)} %get-tuple-element.42.refs_10_), channel_id=1, source_target_pairs={{0,1},{1,2},{2,3},{3,0},{4,5},{5,6},{6,7},{7,4},{8,9},{9,10},{10,1... | collective-permute-start | bytes 688136 | tf_op jit(solution)/shard_map/ppermute | solution.py:338
  45.9 21.4 %collective-permute-start.7 = (f32[7,16,512]{2,1,0:T(8,128)S(1)}, f32[7,16,512]{2,1,0:T(8,128)S(1)}, u32[]{:S(2)}, u32[]{:S(2)}) collective-permute-start(f32[7,16,512]{2,1,0:T(8,128)S(1)} %get-tuple-element.43.refs_9_), channel_id=1, source_target_pairs={{0,3},{1,0},{2,1},{3,2},{4,7},{5,4},{6,5},{7,6},{8,11},{9,8},{10,9... | collective-permute-start | bytes 688136 | tf_op jit(solution)/shard_map/ppermute | solution.py:338
  48.7 1.3 %collective-permute-start.10 = (f32[32,1,128]{2,1,0:T(1,128)S(1)}, f32[32,1,128]{2,1,0:T(1,128)}, u32[]{:S(2)}, u32[]{:S(2)}) collective-permute-start(f32[32,1,128]{2,1,0:T(1,128)S(1)} %get-tuple-element.46), channel_id=1, source_target_pairs={{0,128},{128,0},{1,129},{129,1},{2,130},{130,2},{3,131},{131,3},{4... | collective-permute-start | bytes 49160 | tf_op jit(solution)/shard_map/ppermute | solution.py:341
  50.0 17.3 %all-to-all-start.2 = ((f32[32,1,128]{2,1,0:T(1,128)}), f32[32,1,128]{2,1,0:T(1,128)S(1)}, u32[]{:S(2)}, u32[]{:S(2)}) async-start(f32[32,1,128]{2,1,0:T(1,128)} %collective-permute-done.10), calls=%async_computation.2 | async-start | bytes 32768 | tf_op jit(solution)/shard_map/all_to_all | solution.py:342
  58.7 4.0 %collective-permute-start.8 = (f32[7,2,512]{2,1,0:T(2,128)S(1)}, f32[7,2,512]{2,1,0:T(2,128)S(1)}, u32[]{:S(2)}, u32[]{:S(2)}) collective-permute-start(f32[7,2,512]{2,1,0:T(2,128)S(1)} %get-tuple-element.44), channel_id=1, source_target_pairs={{0,4},{4,8},{8,12},{12,16},{16,20},{20,24},{24,28},{28,32},{32,36}... | collective-permute-start | bytes 86024 | tf_op jit(solution)/shard_map/ppermute | solution.py:338
  60.3 3.9 %collective-permute-start.9 = (f32[7,2,512]{2,1,0:T(2,128)S(1)}, f32[7,2,512]{2,1,0:T(2,128)S(1)}, u32[]{:S(2)}, u32[]{:S(2)}) collective-permute-start(f32[7,2,512]{2,1,0:T(2,128)S(1)} %get-tuple-element.45), channel_id=1, source_target_pairs={{0,124},{4,0},{8,4},{12,8},{16,12},{20,16},{24,20},{28,24},{32,28}... | collective-permute-start | bytes 86024 | tf_op jit(solution)/shard_map/ppermute | solution.py:338
  69.2 22.0 %collective-permute-start.11 = (f32[7,16,512]{2,1,0:T(8,128)S(1)}, f32[7,16,512]{2,1,0:T(8,128)S(1)}, u32[]{:S(2)}, u32[]{:S(2)}) collective-permute-start(f32[7,16,512]{2,1,0:T(8,128)S(1)} %get-tuple-element.49.refs_10_), channel_id=1, source_target_pairs={{0,1},{1,2},{2,3},{3,0},{4,5},{5,6},{6,7},{7,4},{8,9},{9,10},{10,1... | collective-permute-start | bytes 688136 | tf_op jit(solution)/shard_map/ppermute | solution.py:338
  69.3 21.9 %collective-permute-start.12 = (f32[7,16,512]{2,1,0:T(8,128)S(1)}, f32[7,16,512]{2,1,0:T(8,128)S(1)}, u32[]{:S(2)}, u32[]{:S(2)}) collective-permute-start(f32[7,16,512]{2,1,0:T(8,128)S(1)} %get-tuple-element.50.refs_9_), channel_id=1, source_target_pairs={{0,3},{1,0},{2,1},{3,2},{4,7},{5,4},{6,5},{7,6},{8,11},{9,8},{10,9... | collective-permute-start | bytes 688136 | tf_op jit(solution)/shard_map/ppermute | solution.py:338
  72.6 1.3 %collective-permute-start.15 = (f32[32,1,128]{2,1,0:T(1,128)S(1)}, f32[32,1,128]{2,1,0:T(1,128)}, u32[]{:S(2)}, u32[]{:S(2)}) collective-permute-start(f32[32,1,128]{2,1,0:T(1,128)S(1)} %get-tuple-element.53), channel_id=1, source_target_pairs={{0,128},{128,0},{1,129},{129,1},{2,130},{130,2},{3,131},{131,3},{4... | collective-permute-start | bytes 49160 | tf_op jit(solution)/shard_map/ppermute | solution.py:341
  73.9 17.3 %all-to-all-start.3 = ((f32[32,1,128]{2,1,0:T(1,128)}), f32[32,1,128]{2,1,0:T(1,128)S(1)}, u32[]{:S(2)}, u32[]{:S(2)}) async-start(f32[32,1,128]{2,1,0:T(1,128)} %collective-permute-done.15), calls=%async_computation.3 | async-start | bytes 32768 | tf_op jit(solution)/shard_map/all_to_all | solution.py:342
  82.6 4.0 %collective-permute-start.13 = (f32[7,2,512]{2,1,0:T(2,128)S(1)}, f32[7,2,512]{2,1,0:T(2,128)S(1)}, u32[]{:S(2)}, u32[]{:S(2)}) collective-permute-start(f32[7,2,512]{2,1,0:T(2,128)S(1)} %get-tuple-element.51), channel_id=1, source_target_pairs={{0,4},{4,8},{8,12},{12,16},{16,20},{20,24},{24,28},{28,32},{32,36}... | collective-permute-start | bytes 86024 | tf_op jit(solution)/shard_map/ppermute | solution.py:338
  84.2 3.9 %collective-permute-start.14 = (f32[7,2,512]{2,1,0:T(2,128)S(1)}, f32[7,2,512]{2,1,0:T(2,128)S(1)}, u32[]{:S(2)}, u32[]{:S(2)}) collective-permute-start(f32[7,2,512]{2,1,0:T(2,128)S(1)} %get-tuple-element.52), channel_id=1, source_target_pairs={{0,124},{4,0},{8,4},{12,8},{16,12},{20,16},{24,20},{28,24},{32,28}... | collective-permute-start | bytes 86024 | tf_op jit(solution)/shard_map/ppermute | solution.py:338
  93.1 22.0 %collective-permute-start.16 = (f32[7,16,512]{2,1,0:T(8,128)S(1)}, f32[7,16,512]{2,1,0:T(8,128)S(1)}, u32[]{:S(2)}, u32[]{:S(2)}) collective-permute-start(f32[7,16,512]{2,1,0:T(8,128)S(1)} %get-tuple-element.56.refs_10_), channel_id=1, source_target_pairs={{0,1},{1,2},{2,3},{3,0},{4,5},{5,6},{6,7},{7,4},{8,9},{9,10},{10,1... | collective-permute-start | bytes 688136 | tf_op jit(solution)/shard_map/ppermute | solution.py:338
  93.2 21.9 %collective-permute-start.17 = (f32[7,16,512]{2,1,0:T(8,128)S(1)}, f32[7,16,512]{2,1,0:T(8,128)S(1)}, u32[]{:S(2)}, u32[]{:S(2)}) collective-permute-start(f32[7,16,512]{2,1,0:T(8,128)S(1)} %get-tuple-element.57.refs_9_), channel_id=1, source_target_pairs={{0,3},{1,0},{2,1},{3,2},{4,7},{5,4},{6,5},{7,6},{8,11},{9,8},{10,9... | collective-permute-start | bytes 688136 | tf_op jit(solution)/shard_map/ppermute | solution.py:338
  96.5 1.3 %collective-permute-start.20 = (f32[32,1,128]{2,1,0:T(1,128)S(1)}, f32[32,1,128]{2,1,0:T(1,128)}, u32[]{:S(2)}, u32[]{:S(2)}) collective-permute-start(f32[32,1,128]{2,1,0:T(1,128)S(1)} %get-tuple-element.60), channel_id=1, source_target_pairs={{0,128},{128,0},{1,129},{129,1},{2,130},{130,2},{3,131},{131,3},{4... | collective-permute-start | bytes 49160 | tf_op jit(solution)/shard_map/ppermute | solution.py:341
  97.8 17.3 %all-to-all-start.4 = ((f32[32,1,128]{2,1,0:T(1,128)}), f32[32,1,128]{2,1,0:T(1,128)S(1)}, u32[]{:S(2)}, u32[]{:S(2)}) async-start(f32[32,1,128]{2,1,0:T(1,128)} %collective-permute-done.20), calls=%async_computation.4 | async-start | bytes 32768 | tf_op jit(solution)/shard_map/all_to_all | solution.py:342
  106.6 4.0 %collective-permute-start.18 = (f32[7,2,512]{2,1,0:T(2,128)S(1)}, f32[7,2,512]{2,1,0:T(2,128)S(1)}, u32[]{:S(2)}, u32[]{:S(2)}) collective-permute-start(f32[7,2,512]{2,1,0:T(2,128)S(1)} %get-tuple-element.58), channel_id=1, source_target_pairs={{0,4},{4,8},{8,12},{12,16},{16,20},{20,24},{24,28},{28,32},{32,36}... | collective-permute-start | bytes 86024 | tf_op jit(solution)/shard_map/ppermute | solution.py:338
  108.1 3.9 %collective-permute-start.19 = (f32[7,2,512]{2,1,0:T(2,128)S(1)}, f32[7,2,512]{2,1,0:T(2,128)S(1)}, u32[]{:S(2)}, u32[]{:S(2)}) collective-permute-start(f32[7,2,512]{2,1,0:T(2,128)S(1)} %get-tuple-element.59), channel_id=1, source_target_pairs={{0,124},{4,0},{8,4},{12,8},{16,12},{20,16},{24,20},{28,24},{32,28}... | collective-permute-start | bytes 86024 | tf_op jit(solution)/shard_map/ppermute | solution.py:338

commit v3 on v2

--- a/solution.py
+++ b/solution.py
@@ -90,9 +90,10 @@
 
 
 def open_kernel(
-    density, momentum, magnetic, device, phi, theta, weight, turn,
-    low_ref, high_ref, first_ref, last_ref, ask_ref, table_ref,
+    density, momentum, magnetic, device, phi, theta, weight, turn, sines,
+    low_ref, high_ref, first_ref, last_ref, ask_ref, table_ref, sines_ref,
 ):
+    sines_ref[...] = sines[...]
     for level, ref in ((0, low_ref), (1, high_ref)):
         for f in range(NF):
             if f == 0:
@@ -165,10 +166,25 @@
     answer_into(msg_ref, low, high, corner, mask)
 
 
+def ghost_kernel(reply, table, out_ref):
+    got = reply[...].reshape(32, 128)
+    picks = table[...]
+    ghost = jnp.dot(picks[:, 0:32], got, precision=HIGHEST, preferred_element_type=jnp.float32)
+    second = jnp.dot(picks[:, 32:64], got, precision=HIGHEST, preferred_element_type=jnp.float32)
+    ghost = ghost + pltpu.roll(second, 128 - SLOT, axis=1)
+    cosine, sine = picks[:, 64:65], picks[:, 65:66]
+    lane = iota((32, 128), 1) & 7
+    is_t = (lane == 2) | (lane == 5)
+    is_p = (lane == 3) | (lane == 6)
+    turned_t = cosine * ghost + sine * pltpu.roll(ghost, 127, axis=1)
+    turned_p = cosine * ghost - sine * pltpu.roll(ghost, 1, axis=1)
+    out_ref[...] = jnp.where(is_t, turned_t, jnp.where(is_p, turned_p, ghost))
+
+
 def stage_kernel(stage, n_rad, n_ang, *refs):
     last = stage == 4
-    (sines, low0, high0, below, above, before, after, reply, table) = refs[:9]
-    refs = refs[9:]
+    (sines, low0, high0, below, above, before, after, ghosts) = refs[:8]
+    refs = refs[8:]
     if stage == 1:
         low, high = low0, high0
     else:
@@ -186,18 +202,7 @@
     rows_p, rows_t = low.shape[1:]
     invs = [place(rad, n_rad, level, 2) for level in range(2)]
 
-    got = reply[...].reshape(32, 128)
-    picks = table[...]
-    ghost = jnp.dot(picks[:, 0:32], got, precision=HIGHEST, preferred_element_type=jnp.float32)
-    second = jnp.dot(picks[:, 32:64], got, precision=HIGHEST, preferred_element_type=jnp.float32)
-    ghost = ghost + pltpu.roll(second, 128 - SLOT, axis=1)
-    cosine, sine = picks[:, 64:65], picks[:, 65:66]
-    lane = iota((32, 128), 1) & 7
-    is_t = (lane == 2) | (lane == 5)
-    is_p = (lane == 3) | (lane == 6)
-    turned_t = cosine * ghost + sine * pltpu.roll(ghost, 127, axis=1)
-    turned_p = cosine * ghost - sine * pltpu.roll(ghost, 1, axis=1)
-    ghost = jnp.where(is_t, turned_t, jnp.where(is_p, turned_p, ghost))
+    ghost = ghosts[...]
 
     sine_row = sines[...]
     rim = []
@@ -351,14 +356,14 @@
     theta = math.pi / 4 + (np.arange(rows_t) + 0.5) * (math.pi / 2 / rows_t)
     sines = jnp.asarray((1.0 / np.sin(theta)).astype(np.float32)).reshape(1, rows_t)
 
-    low0, high0, first, final, ask, table = call(
+    low0, high0, first, final, ask, table, sines = call(
         open_kernel,
         [
             density, momentum, magnetic, jnp.swapaxes(partner_device, 1, 2), partner_phi, partner_theta,
-            jnp.swapaxes(partner_weight, 1, 2), border_turn,
+            jnp.swapaxes(partner_weight, 1, 2), border_turn, sines,
         ],
-        [level, level, edge, edge, message, shape(32, 128)],
-        plain=8,
+        [level, level, edge, edge, message, shape(32, 128), shape(1, rows_t)],
+        plain=9,
     )
     around = halos(low0, high0, first, final)
     corner, rowmask, answer = call(
@@ -367,7 +372,8 @@
     low, high, sums = low0, high0, []
     scratch = [pltpu.VMEM((2, NF, rows_p, rows_t), f32) for _ in range(3)]
     for stage in range(1, 5):
-        ins = [sines, low0, high0, *around, crossed(answer), table]
+        (ghosts,) = call(ghost_kernel, [crossed(answer), table], [shape(32, 128)])
+        ins = [sines, low0, high0, *around, ghosts]
         if stage > 1:
             ins += [low, high, *sums]
         if stage < 4:
@@ -383,7 +389,7 @@
         def kernel(*refs, stage=stage):
             stage_kernel(stage, n_rad, n_ang, *refs)
 
-        result = call(kernel, ins, outs, scratch, plain=1)
+        result = call(kernel, ins, outs, scratch)
         if stage == 4:
             return tuple(result)
         low, high, acc_low, acc_high, first, final, answer = result

time: 118 us -> 116 us (0.983)
  starting transfers between devices: 52.8 us -> 51.6 us
    all_to_all x4, waiting for transfers between devices: 12.6 us -> 25.9 us  [crossed(): lax.all_to_all(swap, 'ang', split_axis=0, concat_axis=0, tiled=True)]
    ppermute x16, waiting for transfers between devices: 13.3 us -> 0.04 us  [shifted(): lax.ppermute(value, axis, [(i, (i + by) % size) for i in range(size)])]
    all_to_all x4, starting transfers between devices: 31.2 us -> 29.9 us  [crossed(): lax.all_to_all(swap, 'ang', split_axis=0, concat_axis=0, tiled=True)]
    pallas_call x6 -> x10, Pallas kernels: 10.3 us -> 10.7 us  [call(): pl.pallas_call(kernel, out_shape=outs, in_specs=[vmem] * len(ins), out_sp...]
  transfers between devices with their start and end apart: 25 -> 25, of which waited for: 17 -> 9; matrix products, arithmetic and copies ran while one was open for 0% -> 0% of each run, Pallas kernels for 1% -> 2%
where the time goes in v3:
time: 116 us
  starting transfers between devices  51.6 us (44%)
  waiting for transfers between devices  32.4 us (28%)
  blocking collectives  20 us (17%)
  Pallas kernels  10.7 us (9%)
    all_to_all x4, starting transfers between devices, crossed(): lax.all_to_all(swap, 'ang', split_axis=0, concat_axis=0, tiled=True)  29.9 us
    all_to_all x4, waiting for transfers between devices, crossed(): lax.all_to_all(swap, 'ang', split_axis=0, concat_axis=0, tiled=True)  25.9 us
    ppermute x16, starting transfers between devices, shifted(): lax.ppermute(value, axis, [(i, (i + by) % size) for i in range(size)])  21.5 us
    all_to_all x1, blocking collectives, crossed(): lax.all_to_all(swap, 'ang', split_axis=0, concat_axis=0, tiled=True)  20 us
    pallas_call x10, Pallas kernels, call(): pl.pallas_call(kernel, out_shape=outs, in_specs=[vmem] * len(ins), out_sp...  10.7 us
    ppermute x5, waiting for transfers between devices, crossed(): swap = held(lax.ppermute(value, 'panel', [(0, 1), (1, 0)]))  6.42 us
  transfers between devices with their start and end apart: 25, of which 9 were waited for; matrix products, arithmetic and copies ran while one was open for 0% of the time, Pallas kernels for 2%

profile of v3, /device:TPU:2, one launch (start us, length us, event | category | flops | bytes accessed | tf_op | source)
XLA Modules:
  0.0 115.5 jit_solution(14094083336225037005)
XLA Ops:
  0.6 1.5 %shard_map.112 = (f32[7,16,512]{2,1,0:T(8,128)S(1)}, f32[7,16,512]{2,1,0:T(8,128)S(1)}, f32[7,2,512]{2,1,0:T(2,128)S(1)}, f32[7,2,512]{2,1,0:T(2,128)S(1)}, f32[...) custom-call(f32[1,2,16,512]{3,2,1,0:T(8,128)} %density.1, f32[1,3,2,16,512]{4,3,2,1,0:T(8,128)} %momentum.1, ...), custom_call_target="tpu_custom_call" | custom-call | tf_op jit(solution)/shard_map/pallas_call | solution.py:327
  2.1 3.1 %collective-permute-start.1 = (f32[7,16,512]{2,1,0:T(8,128)S(1)}, f32[7,16,512]{2,1,0:T(8,128)S(1)}, u32[]{:S(2)}, u32[]{:S(2)}) collective-permute-start(f32[7,16,512]{2,1,0:T(8,128)S(1)} %get-tuple-element.35.low_ref.refs_1_), channel_id=1, source_target_pairs={{0,3},{1,0},{2,1},{3,2},{4,7},{5,4},{6,5},{7,6},{8,11},{9,8},{10,9... | collective-permute-start | bytes 688136 | tf_op jit(solution)/shard_map/ppermute | solution.py:343
  5.2 1.2 %collective-permute-done.4 = f32[32,1,128]{2,1,0:T(1,128)S(1)} collective-permute-done((f32[32,1,128]{2,1,0:T(1,128)S(1)}, f32[32,1,128]{2,1,0:T(1,128)S(1)}, u32[]{:S(2)}, u32[]{:S(2)}) %collective-permute-start.4) | collective-permute-done | bytes 16416 | tf_op jit(solution)/shard_map/ppermute | solution.py:346
  6.4 20.0 %all_to_all.25.asked_ref = f32[32,1,128]{2,1,0:T(1,128)S(1)} all-to-all(f32[32,1,128]{2,1,0:T(1,128)S(1)} %collective-permute-done.4), channel_id=1, replica_groups=mesh['panel'=2,'ang'=32,'rad'=4] {'ang'}, dimensions={0} | all-to-all | bytes 32768 | tf_op jit(solution)/shard_map/all_to_all | solution.py:347
  26.4 1.3 %shard_map.113 = (f32[512,128]{1,0:T(8,128)S(1)}, f32[16,128]{1,0:T(8,128)S(1)}, f32[32,1,128]{2,1,0:T(1,128)S(1)}) custom-call(f32[32,1,128]{2,1,0:T(1,128)S(1)} %all_to_all.25.asked_ref, f32[7,16,512]{2,1,0:T(8,128)S(1)} %get-tuple-element.35.low_ref.refs_1_, f32[7,16,512]{2,1,0:T(8,128)S(1)} %get-tuple-element.36.high_ref.refs_2_), custom_call_target="tpu_custom_call" | custom-call | tf_op jit(solution)/shard_map/pallas_call | solution.py:327
  27.8 1.3 %collective-permute-done.5 = f32[32,1,128]{2,1,0:T(1,128)} collective-permute-done((f32[32,1,128]{2,1,0:T(1,128)S(1)}, f32[32,1,128]{2,1,0:T(1,128)}, u32[]{:S(2)}, u32[]{:S(2)}) %collective-permute-start.5) | collective-permute-done | bytes 16416 | tf_op jit(solution)/shard_map/ppermute | solution.py:346
  29.1 4.9 %all-to-all-start.1 = ((f32[32,1,128]{2,1,0:T(1,128)}), f32[32,1,128]{2,1,0:T(1,128)S(1)}, u32[]{:S(2)}, u32[]{:S(2)}) async-start(f32[32,1,128]{2,1,0:T(1,128)} %collective-permute-done.5), calls=%async_computation.1 | async-start | bytes 32768 | tf_op jit(solution)/shard_map/all_to_all | solution.py:347
  34.1 1.5 %collective-permute-start.2 = (f32[7,2,512]{2,1,0:T(2,128)S(1)}, f32[7,2,512]{2,1,0:T(2,128)S(1)}, u32[]{:S(2)}, u32[]{:S(2)}) collective-permute-start(f32[7,2,512]{2,1,0:T(2,128)S(1)} %get-tuple-element.37), channel_id=1, source_target_pairs={{0,4},{4,8},{8,12},{12,16},{16,20},{20,24},{24,28},{28,32},{32,36}... | collective-permute-start | bytes 86024 | tf_op jit(solution)/shard_map/ppermute | solution.py:343
  36.2 6.6 %all-to-all-done.1.reply = f32[32,1,128]{2,1,0:T(1,128)S(1)} async-done(((f32[32,1,128]{2,1,0:T(1,128)}), f32[32,1,128]{2,1,0:T(1,128)S(1)}, u32[]{:S(2)}, u32[]{:S(2)}) %all-to-all-start.1) | async-done | bytes 16416 | tf_op jit(solution)/shard_map/all_to_all | solution.py:347
  43.1 1.6 %shard_map.115 = (f32[7,16,512]{2,1,0:T(8,128)S(1)}, f32[7,16,512]{2,1,0:T(8,128)S(1)}, f32[7,16,512]{2,1,0:T(8,128)S(1)}, f32[7,16,512]{2,1,0:T(8,128)S(1)}, f3...) custom-call(f32[1,512]{1,0:T(1,128)S(1)} %get-tuple-element.34.refs_0_, ...), custom_call_target="tpu_custom_call" | custom-call | tf_op jit(solution)/shard_map/pallas_call | solution.py:327
  44.7 0.7 collective-permute-start.6
  45.4 2.7 %collective-permute-start.7 = (f32[7,16,512]{2,1,0:T(8,128)S(1)}, f32[7,16,512]{2,1,0:T(8,128)S(1)}, u32[]{:S(2)}, u32[]{:S(2)}) collective-permute-start(f32[7,16,512]{2,1,0:T(8,128)S(1)} %get-tuple-element.45.refs_8_), channel_id=1, source_target_pairs={{0,3},{1,0},{2,1},{3,2},{4,7},{5,4},{6,5},{7,6},{8,11},{9,8},{10,9... | collective-permute-start | bytes 688136 | tf_op jit(solution)/shard_map/ppermute | solution.py:343
  48.2 1.3 %collective-permute-done.10 = f32[32,1,128]{2,1,0:T(1,128)} collective-permute-done((f32[32,1,128]{2,1,0:T(1,128)S(1)}, f32[32,1,128]{2,1,0:T(1,128)}, u32[]{:S(2)}, u32[]{:S(2)}) %collective-permute-start.10) | collective-permute-done | bytes 16416 | tf_op jit(solution)/shard_map/ppermute | solution.py:346
  49.5 8.3 %all-to-all-start.2 = ((f32[32,1,128]{2,1,0:T(1,128)}), f32[32,1,128]{2,1,0:T(1,128)S(1)}, u32[]{:S(2)}, u32[]{:S(2)}) async-start(f32[32,1,128]{2,1,0:T(1,128)} %collective-permute-done.10), calls=%async_computation.2 | async-start | bytes 32768 | tf_op jit(solution)/shard_map/all_to_all | solution.py:347
  57.8 1.5 %collective-permute-start.8 = (f32[7,2,512]{2,1,0:T(2,128)S(1)}, f32[7,2,512]{2,1,0:T(2,128)S(1)}, u32[]{:S(2)}, u32[]{:S(2)}) collective-permute-start(f32[7,2,512]{2,1,0:T(2,128)S(1)} %get-tuple-element.46), channel_id=1, source_target_pairs={{0,4},{4,8},{8,12},{12,16},{16,20},{20,24},{24,28},{28,32},{32,36}... | collective-permute-start | bytes 86024 | tf_op jit(solution)/shard_map/ppermute | solution.py:343
  59.3 0.6 collective-permute-start.9
  59.9 6.4 %all-to-all-done.2.reply = f32[32,1,128]{2,1,0:T(1,128)S(1)} async-done(((f32[32,1,128]{2,1,0:T(1,128)}), f32[32,1,128]{2,1,0:T(1,128)S(1)}, u32[]{:S(2)}, u32[]{:S(2)}) %all-to-all-start.2) | async-done | bytes 16416 | tf_op jit(solution)/shard_map/all_to_all | solution.py:347
  66.8 1.6 %shard_map.117 = (f32[7,16,512]{2,1,0:T(8,128)S(1)}, f32[7,16,512]{2,1,0:T(8,128)S(1)}, f32[7,16,512]{2,1,0:T(8,128)S(1)}, f32[7,16,512]{2,1,0:T(8,128)S(1)}, f3...) custom-call(f32[1,512]{1,0:T(1,128)S(1)} %get-tuple-element.34.refs_0_, ...), custom_call_target="tpu_custom_call" | custom-call | tf_op jit(solution)/shard_map/pallas_call | solution.py:327
  68.5 3.2 %collective-permute-start.12 = (f32[7,16,512]{2,1,0:T(8,128)S(1)}, f32[7,16,512]{2,1,0:T(8,128)S(1)}, u32[]{:S(2)}, u32[]{:S(2)}) collective-permute-start(f32[7,16,512]{2,1,0:T(8,128)S(1)} %get-tuple-element.52.refs_8_), channel_id=1, source_target_pairs={{0,3},{1,0},{2,1},{3,2},{4,7},{5,4},{6,5},{7,6},{8,11},{9,8},{10,9... | collective-permute-start | bytes 688136 | tf_op jit(solution)/shard_map/ppermute | solution.py:343
  71.7 1.3 %collective-permute-done.15 = f32[32,1,128]{2,1,0:T(1,128)} collective-permute-done((f32[32,1,128]{2,1,0:T(1,128)S(1)}, f32[32,1,128]{2,1,0:T(1,128)}, u32[]{:S(2)}, u32[]{:S(2)}) %collective-permute-start.15) | collective-permute-done | bytes 16416 | tf_op jit(solution)/shard_map/ppermute | solution.py:346
  73.0 8.3 %all-to-all-start.3 = ((f32[32,1,128]{2,1,0:T(1,128)}), f32[32,1,128]{2,1,0:T(1,128)S(1)}, u32[]{:S(2)}, u32[]{:S(2)}) async-start(f32[32,1,128]{2,1,0:T(1,128)} %collective-permute-done.15), calls=%async_computation.3 | async-start | bytes 32768 | tf_op jit(solution)/shard_map/all_to_all | solution.py:347
  81.4 1.5 %collective-permute-start.13 = (f32[7,2,512]{2,1,0:T(2,128)S(1)}, f32[7,2,512]{2,1,0:T(2,128)S(1)}, u32[]{:S(2)}, u32[]{:S(2)}) collective-permute-start(f32[7,2,512]{2,1,0:T(2,128)S(1)} %get-tuple-element.53), channel_id=1, source_target_pairs={{0,4},{4,8},{8,12},{12,16},{16,20},{20,24},{24,28},{28,32},{32,36}... | collective-permute-start | bytes 86024 | tf_op jit(solution)/shard_map/ppermute | solution.py:343
  82.9 0.6 collective-permute-start.14
  83.5 6.4 %all-to-all-done.3.reply = f32[32,1,128]{2,1,0:T(1,128)S(1)} async-done(((f32[32,1,128]{2,1,0:T(1,128)}), f32[32,1,128]{2,1,0:T(1,128)S(1)}, u32[]{:S(2)}, u32[]{:S(2)}) %all-to-all-start.3) | async-done | bytes 16416 | tf_op jit(solution)/shard_map/all_to_all | solution.py:347
  90.3 1.6 %shard_map.119 = (f32[7,16,512]{2,1,0:T(8,128)S(1)}, f32[7,16,512]{2,1,0:T(8,128)S(1)}, f32[7,16,512]{2,1,0:T(8,128)S(1)}, f32[7,16,512]{2,1,0:T(8,128)S(1)}, f3...) custom-call(f32[1,512]{1,0:T(1,128)S(1)} %get-tuple-element.34.refs_0_, ...), custom_call_target="tpu_custom_call" | custom-call | tf_op jit(solution)/shard_map/pallas_call | solution.py:327
  92.1 3.2 %collective-permute-start.17 = (f32[7,16,512]{2,1,0:T(8,128)S(1)}, f32[7,16,512]{2,1,0:T(8,128)S(1)}, u32[]{:S(2)}, u32[]{:S(2)}) collective-permute-start(f32[7,16,512]{2,1,0:T(8,128)S(1)} %get-tuple-element.59.refs_8_), channel_id=1, source_target_pairs={{0,3},{1,0},{2,1},{3,2},{4,7},{5,4},{6,5},{7,6},{8,11},{9,8},{10,9... | collective-permute-start | bytes 688136 | tf_op jit(solution)/shard_map/ppermute | solution.py:343
  95.3 1.3 %collective-permute-done.20 = f32[32,1,128]{2,1,0:T(1,128)} collective-permute-done((f32[32,1,128]{2,1,0:T(1,128)S(1)}, f32[32,1,128]{2,1,0:T(1,128)}, u32[]{:S(2)}, u32[]{:S(2)}) %collective-permute-start.20) | collective-permute-done | bytes 16416 | tf_op jit(solution)/shard_map/ppermute | solution.py:346
  96.6 8.3 %all-to-all-start.4 = ((f32[32,1,128]{2,1,0:T(1,128)}), f32[32,1,128]{2,1,0:T(1,128)S(1)}, u32[]{:S(2)}, u32[]{:S(2)}) async-start(f32[32,1,128]{2,1,0:T(1,128)} %collective-permute-done.20), calls=%async_computation.4 | async-start | bytes 32768 | tf_op jit(solution)/shard_map/all_to_all | solution.py:347
  105.0 1.5 %collective-permute-start.18 = (f32[7,2,512]{2,1,0:T(2,128)S(1)}, f32[7,2,512]{2,1,0:T(2,128)S(1)}, u32[]{:S(2)}, u32[]{:S(2)}) collective-permute-start(f32[7,2,512]{2,1,0:T(2,128)S(1)} %get-tuple-element.60), channel_id=1, source_target_pairs={{0,4},{4,8},{8,12},{12,16},{16,20},{20,24},{24,28},{28,32},{32,36}... | collective-permute-start | bytes 86024 | tf_op jit(solution)/shard_map/ppermute | solution.py:343
  106.5 0.6 collective-permute-start.19
  107.1 6.4 %all-to-all-done.4.reply = f32[32,1,128]{2,1,0:T(1,128)S(1)} async-done(((f32[32,1,128]{2,1,0:T(1,128)}), f32[32,1,128]{2,1,0:T(1,128)S(1)}, u32[]{:S(2)}, u32[]{:S(2)}) %all-to-all-start.4) | async-done | bytes 16416 | tf_op jit(solution)/shard_map/all_to_all | solution.py:347
  113.9 1.6 %shard_map.121 = (f32[1,2,16,512]{3,2,1,0:T(8,128)}, f32[1,3,2,16,512]{4,3,2,1,0:T(8,128)}, f32[1,3,2,16,512]{4,3,2,1,0:T(8,128)}) custom-call(f32[1,512]{1,0:T(1,128)S(1)} %get-tuple-element.34.refs_0_, f32[7,16,512]{2,1,0:T(8,128)S(1)} %get-tuple-element.35.low_ref.refs_1_, f32[7,16,512]{2,1,0:T(8,128)S(1)} %get-tuple-element.36.high_ref.refs_2_, ...), custom_call_target="tpu_custom_call" | custom-call | tf_op jit(solution)/shard_map/pallas_call | solution.py:327
  (29 shorter events, 2.4 us)
Async XLA Ops:
  2.1 41.0 %collective-permute-start.1 = (f32[7,16,512]{2,1,0:T(8,128)S(1)}, f32[7,16,512]{2,1,0:T(8,128)S(1)}, u32[]{:S(2)}, u32[]{:S(2)}) collective-permute-start(f32[7,16,512]{2,1,0:T(8,128)S(1)} %get-tuple-element.35.low_ref.refs_1_), channel_id=1, source_target_pairs={{0,3},{1,0},{2,1},{3,2},{4,7},{5,4},{6,5},{7,6},{8,11},{9,8},{10,9... | collective-permute-start | bytes 688136 | tf_op jit(solution)/shard_map/ppermute | solution.py:343
  5.2 37.9 %collective-permute-start = (f32[7,16,512]{2,1,0:T(8,128)S(1)}, f32[7,16,512]{2,1,0:T(8,128)S(1)}, u32[]{:S(2)}, u32[]{:S(2)}) collective-permute-start(f32[7,16,512]{2,1,0:T(8,128)S(1)} %get-tuple-element.36.high_ref.refs_2_), channel_id=1, source_target_pairs={{0,1},{1,2},{2,3},{3,0},{4,5},{5,6},{6,7},{7,4},{8,9},{9,10},{10,1... | collective-permute-start | bytes 688136 | tf_op jit(solution)/shard_map/ppermute | solution.py:343
  5.2 1.2 %collective-permute-start.4 = (f32[32,1,128]{2,1,0:T(1,128)S(1)}, f32[32,1,128]{2,1,0:T(1,128)S(1)}, u32[]{:S(2)}, u32[]{:S(2)}) collective-permute-start(f32[32,1,128]{2,1,0:T(1,128)S(1)} %get-tuple-element.39), channel_id=1, source_target_pairs={{0,128},{128,0},{1,129},{129,1},{2,130},{130,2},{3,131},{131,3},{4... | collective-permute-start | bytes 49160 | tf_op jit(solution)/shard_map/ppermute | solution.py:346
  27.7 1.4 %collective-permute-start.5 = (f32[32,1,128]{2,1,0:T(1,128)S(1)}, f32[32,1,128]{2,1,0:T(1,128)}, u32[]{:S(2)}, u32[]{:S(2)}) collective-permute-start(f32[32,1,128]{2,1,0:T(1,128)S(1)} %get-tuple-element.40), channel_id=1, source_target_pairs={{0,128},{128,0},{1,129},{129,1},{2,130},{130,2},{3,131},{131,3},{4... | collective-permute-start | bytes 49160 | tf_op jit(solution)/shard_map/ppermute | solution.py:346
  29.1 13.6 %all-to-all-start.1 = ((f32[32,1,128]{2,1,0:T(1,128)}), f32[32,1,128]{2,1,0:T(1,128)S(1)}, u32[]{:S(2)}, u32[]{:S(2)}) async-start(f32[32,1,128]{2,1,0:T(1,128)} %collective-permute-done.5), calls=%async_computation.1 | async-start | bytes 32768 | tf_op jit(solution)/shard_map/all_to_all | solution.py:347
  34.1 9.0 %collective-permute-start.2 = (f32[7,2,512]{2,1,0:T(2,128)S(1)}, f32[7,2,512]{2,1,0:T(2,128)S(1)}, u32[]{:S(2)}, u32[]{:S(2)}) collective-permute-start(f32[7,2,512]{2,1,0:T(2,128)S(1)} %get-tuple-element.37), channel_id=1, source_target_pairs={{0,4},{4,8},{8,12},{12,16},{16,20},{20,24},{24,28},{28,32},{32,36}... | collective-permute-start | bytes 86024 | tf_op jit(solution)/shard_map/ppermute | solution.py:343
  35.6 7.5 %collective-permute-start.3 = (f32[7,2,512]{2,1,0:T(2,128)S(1)}, f32[7,2,512]{2,1,0:T(2,128)S(1)}, u32[]{:S(2)}, u32[]{:S(2)}) collective-permute-start(f32[7,2,512]{2,1,0:T(2,128)S(1)} %get-tuple-element.38), channel_id=1, source_target_pairs={{0,124},{4,0},{8,4},{12,8},{16,12},{20,16},{24,20},{28,24},{32,28}... | collective-permute-start | bytes 86024 | tf_op jit(solution)/shard_map/ppermute | solution.py:343
  44.7 22.0 %collective-permute-start.6 = (f32[7,16,512]{2,1,0:T(8,128)S(1)}, f32[7,16,512]{2,1,0:T(8,128)S(1)}, u32[]{:S(2)}, u32[]{:S(2)}) collective-permute-start(f32[7,16,512]{2,1,0:T(8,128)S(1)} %get-tuple-element.44.refs_9_), channel_id=1, source_target_pairs={{0,1},{1,2},{2,3},{3,0},{4,5},{5,6},{6,7},{7,4},{8,9},{9,10},{10,1... | collective-permute-start | bytes 688136 | tf_op jit(solution)/shard_map/ppermute | solution.py:343
  45.4 21.4 %collective-permute-start.7 = (f32[7,16,512]{2,1,0:T(8,128)S(1)}, f32[7,16,512]{2,1,0:T(8,128)S(1)}, u32[]{:S(2)}, u32[]{:S(2)}) collective-permute-start(f32[7,16,512]{2,1,0:T(8,128)S(1)} %get-tuple-element.45.refs_8_), channel_id=1, source_target_pairs={{0,3},{1,0},{2,1},{3,2},{4,7},{5,4},{6,5},{7,6},{8,11},{9,8},{10,9... | collective-permute-start | bytes 688136 | tf_op jit(solution)/shard_map/ppermute | solution.py:343
  48.1 1.3 %collective-permute-start.10 = (f32[32,1,128]{2,1,0:T(1,128)S(1)}, f32[32,1,128]{2,1,0:T(1,128)}, u32[]{:S(2)}, u32[]{:S(2)}) collective-permute-start(f32[32,1,128]{2,1,0:T(1,128)S(1)} %get-tuple-element.48), channel_id=1, source_target_pairs={{0,128},{128,0},{1,129},{129,1},{2,130},{130,2},{3,131},{131,3},{4... | collective-permute-start | bytes 49160 | tf_op jit(solution)/shard_map/ppermute | solution.py:346
  49.5 16.9 %all-to-all-start.2 = ((f32[32,1,128]{2,1,0:T(1,128)}), f32[32,1,128]{2,1,0:T(1,128)S(1)}, u32[]{:S(2)}, u32[]{:S(2)}) async-start(f32[32,1,128]{2,1,0:T(1,128)} %collective-permute-done.10), calls=%async_computation.2 | async-start | bytes 32768 | tf_op jit(solution)/shard_map/all_to_all | solution.py:347
  57.8 8.9 %collective-permute-start.8 = (f32[7,2,512]{2,1,0:T(2,128)S(1)}, f32[7,2,512]{2,1,0:T(2,128)S(1)}, u32[]{:S(2)}, u32[]{:S(2)}) collective-permute-start(f32[7,2,512]{2,1,0:T(2,128)S(1)} %get-tuple-element.46), channel_id=1, source_target_pairs={{0,4},{4,8},{8,12},{12,16},{16,20},{20,24},{24,28},{28,32},{32,36}... | collective-permute-start | bytes 86024 | tf_op jit(solution)/shard_map/ppermute | solution.py:343
  59.3 7.4 %collective-permute-start.9 = (f32[7,2,512]{2,1,0:T(2,128)S(1)}, f32[7,2,512]{2,1,0:T(2,128)S(1)}, u32[]{:S(2)}, u32[]{:S(2)}) collective-permute-start(f32[7,2,512]{2,1,0:T(2,128)S(1)} %get-tuple-element.47), channel_id=1, source_target_pairs={{0,124},{4,0},{8,4},{12,8},{16,12},{20,16},{24,20},{28,24},{32,28}... | collective-permute-start | bytes 86024 | tf_op jit(solution)/shard_map/ppermute | solution.py:343
  68.4 21.9 %collective-permute-start.11 = (f32[7,16,512]{2,1,0:T(8,128)S(1)}, f32[7,16,512]{2,1,0:T(8,128)S(1)}, u32[]{:S(2)}, u32[]{:S(2)}) collective-permute-start(f32[7,16,512]{2,1,0:T(8,128)S(1)} %get-tuple-element.51.refs_9_), channel_id=1, source_target_pairs={{0,1},{1,2},{2,3},{3,0},{4,5},{5,6},{6,7},{7,4},{8,9},{9,10},{10,1... | collective-permute-start | bytes 688136 | tf_op jit(solution)/shard_map/ppermute | solution.py:343
  68.5 21.9 %collective-permute-start.12 = (f32[7,16,512]{2,1,0:T(8,128)S(1)}, f32[7,16,512]{2,1,0:T(8,128)S(1)}, u32[]{:S(2)}, u32[]{:S(2)}) collective-permute-start(f32[7,16,512]{2,1,0:T(8,128)S(1)} %get-tuple-element.52.refs_8_), channel_id=1, source_target_pairs={{0,3},{1,0},{2,1},{3,2},{4,7},{5,4},{6,5},{7,6},{8,11},{9,8},{10,9... | collective-permute-start | bytes 688136 | tf_op jit(solution)/shard_map/ppermute | solution.py:343
  71.7 1.3 %collective-permute-start.15 = (f32[32,1,128]{2,1,0:T(1,128)S(1)}, f32[32,1,128]{2,1,0:T(1,128)}, u32[]{:S(2)}, u32[]{:S(2)}) collective-permute-start(f32[32,1,128]{2,1,0:T(1,128)S(1)} %get-tuple-element.55), channel_id=1, source_target_pairs={{0,128},{128,0},{1,129},{129,1},{2,130},{130,2},{3,131},{131,3},{4... | collective-permute-start | bytes 49160 | tf_op jit(solution)/shard_map/ppermute | solution.py:346
  73.0 16.9 %all-to-all-start.3 = ((f32[32,1,128]{2,1,0:T(1,128)}), f32[32,1,128]{2,1,0:T(1,128)S(1)}, u32[]{:S(2)}, u32[]{:S(2)}) async-start(f32[32,1,128]{2,1,0:T(1,128)} %collective-permute-done.15), calls=%async_computation.3 | async-start | bytes 32768 | tf_op jit(solution)/shard_map/all_to_all | solution.py:347
  81.4 8.9 %collective-permute-start.13 = (f32[7,2,512]{2,1,0:T(2,128)S(1)}, f32[7,2,512]{2,1,0:T(2,128)S(1)}, u32[]{:S(2)}, u32[]{:S(2)}) collective-permute-start(f32[7,2,512]{2,1,0:T(2,128)S(1)} %get-tuple-element.53), channel_id=1, source_target_pairs={{0,4},{4,8},{8,12},{12,16},{16,20},{20,24},{24,28},{28,32},{32,36}... | collective-permute-start | bytes 86024 | tf_op jit(solution)/shard_map/ppermute | solution.py:343
  82.9 7.4 %collective-permute-start.14 = (f32[7,2,512]{2,1,0:T(2,128)S(1)}, f32[7,2,512]{2,1,0:T(2,128)S(1)}, u32[]{:S(2)}, u32[]{:S(2)}) collective-permute-start(f32[7,2,512]{2,1,0:T(2,128)S(1)} %get-tuple-element.54), channel_id=1, source_target_pairs={{0,124},{4,0},{8,4},{12,8},{16,12},{20,16},{24,20},{28,24},{32,28}... | collective-permute-start | bytes 86024 | tf_op jit(solution)/shard_map/ppermute | solution.py:343
  92.0 21.9 %collective-permute-start.16 = (f32[7,16,512]{2,1,0:T(8,128)S(1)}, f32[7,16,512]{2,1,0:T(8,128)S(1)}, u32[]{:S(2)}, u32[]{:S(2)}) collective-permute-start(f32[7,16,512]{2,1,0:T(8,128)S(1)} %get-tuple-element.58.refs_9_), channel_id=1, source_target_pairs={{0,1},{1,2},{2,3},{3,0},{4,5},{5,6},{6,7},{7,4},{8,9},{9,10},{10,1... | collective-permute-start | bytes 688136 | tf_op jit(solution)/shard_map/ppermute | solution.py:343
  92.1 21.9 %collective-permute-start.17 = (f32[7,16,512]{2,1,0:T(8,128)S(1)}, f32[7,16,512]{2,1,0:T(8,128)S(1)}, u32[]{:S(2)}, u32[]{:S(2)}) collective-permute-start(f32[7,16,512]{2,1,0:T(8,128)S(1)} %get-tuple-element.59.refs_8_), channel_id=1, source_target_pairs={{0,3},{1,0},{2,1},{3,2},{4,7},{5,4},{6,5},{7,6},{8,11},{9,8},{10,9... | collective-permute-start | bytes 688136 | tf_op jit(solution)/shard_map/ppermute | solution.py:343
  95.3 1.3 %collective-permute-start.20 = (f32[32,1,128]{2,1,0:T(1,128)S(1)}, f32[32,1,128]{2,1,0:T(1,128)}, u32[]{:S(2)}, u32[]{:S(2)}) collective-permute-start(f32[32,1,128]{2,1,0:T(1,128)S(1)} %get-tuple-element.62), channel_id=1, source_target_pairs={{0,128},{128,0},{1,129},{129,1},{2,130},{130,2},{3,131},{131,3},{4... | collective-permute-start | bytes 49160 | tf_op jit(solution)/shard_map/ppermute | solution.py:346
  96.6 16.9 %all-to-all-start.4 = ((f32[32,1,128]{2,1,0:T(1,128)}), f32[32,1,128]{2,1,0:T(1,128)S(1)}, u32[]{:S(2)}, u32[]{:S(2)}) async-start(f32[32,1,128]{2,1,0:T(1,128)} %collective-permute-done.20), calls=%async_computation.4 | async-start | bytes 32768 | tf_op jit(solution)/shard_map/all_to_all | solution.py:347
  105.0 8.9 %collective-permute-start.18 = (f32[7,2,512]{2,1,0:T(2,128)S(1)}, f32[7,2,512]{2,1,0:T(2,128)S(1)}, u32[]{:S(2)}, u32[]{:S(2)}) collective-permute-start(f32[7,2,512]{2,1,0:T(2,128)S(1)} %get-tuple-element.60), channel_id=1, source_target_pairs={{0,4},{4,8},{8,12},{12,16},{16,20},{20,24},{24,28},{28,32},{32,36}... | collective-permute-start | bytes 86024 | tf_op jit(solution)/shard_map/ppermute | solution.py:343
  106.5 7.4 %collective-permute-start.19 = (f32[7,2,512]{2,1,0:T(2,128)S(1)}, f32[7,2,512]{2,1,0:T(2,128)S(1)}, u32[]{:S(2)}, u32[]{:S(2)}) collective-permute-start(f32[7,2,512]{2,1,0:T(2,128)S(1)} %get-tuple-element.61), channel_id=1, source_target_pairs={{0,124},{4,0},{8,4},{12,8},{16,12},{20,16},{24,20},{28,24},{32,28}... | collective-permute-start | bytes 86024 | tf_op jit(solution)/shard_map/ppermute | solution.py:343

commit v4 on v3

--- a/solution.py
+++ b/solution.py
@@ -14,6 +14,7 @@
 NF = 7
 MIRROR = (1.0, -1.0, -1.0, -1.0, 1.0, 1.0, 1.0)
 INTERPRET = False
+EDGE = 4
 SLOT = 16
 HIGHEST = lax.Precision.HIGHEST
 
@@ -68,25 +69,21 @@
 
 
 def answer_into(msg_ref, low, high, corner, rowmask):
-    rows_p = rowmask.shape[0]
     parts = []
     for level in (low, high):
         product = jnp.dot(level, corner, precision=HIGHEST, preferred_element_type=jnp.float32)
-        picked = product.reshape(NF, rows_p, 128) * rowmask[None]
+        product = product.reshape(NF, rowmask.shape[0], 128)
+        picked = jnp.where(rowmask[None] > 0.5, product, 0.0)
         parts.append(jnp.sum(picked, axis=1))
         parts.append(jnp.zeros((1, 128), jnp.float32))
     both = jnp.concatenate(parts, axis=0)
     both = both + pltpu.roll(both, 64, axis=1)
     turned = both.T
     lanes = jnp.concatenate([turned, jnp.zeros((128, 128 - SLOT), jnp.float32)], axis=1)
-    lane = iota((32, 128), 1)
-    message = jnp.where(lane < SLOT, lanes[0:32], pltpu.roll(lanes[32:64], SLOT, axis=1))
-    msg_ref[...] = message.reshape(msg_ref.shape)
-
-
-def send_rows(first_ref, last_ref, level, f, value):
-    first_ref[f, level : level + 1, :] = value[0:1, :]
-    last_ref[f, level : level + 1, :] = value[value.shape[0] - 1 :, :]
+    own = lanes[0:32] + pltpu.roll(lanes[32:64], SLOT, axis=1)
+    before = pltpu.roll(pltpu.roll(own, 1, axis=0), 2 * SLOT, axis=1)
+    after = pltpu.roll(pltpu.roll(own, 31, axis=0), 4 * SLOT, axis=1)
+    msg_ref[...] = (own + before + after).reshape(msg_ref.shape)
 
 
 def open_kernel(
@@ -103,7 +100,8 @@
             else:
                 value = magnetic[0, f - 4, level]
             ref[f] = value
-            send_rows(first_ref, last_ref, level, f, value)
+            first_ref[f, EDGE * level : EDGE * level + EDGE, :] = value[:EDGE]
+            last_ref[f, EDGE * level : EDGE * level + EDGE, :] = value[value.shape[0] - EDGE :]
     rows = device.shape[2]
     one, two = iota((rows, rows), 0), iota((rows, rows), 1)
     eye = one == two
@@ -134,10 +132,30 @@
     cosine = column(jnp.cos(turn[...]))
     sine = column(jnp.sin(turn[...]))
     picks = jnp.where(lane == 64, cosine, picks)
-    table_ref[...] = jnp.where(lane == 65, sine, picks)
-
-
-def asked_kernel(asked_ref, low_ref, high_ref, corner_ref, mask_ref, msg_ref):
+    picks = jnp.where(lane == 65, sine, picks)
+    table_ref[...] = picks
+    half = rows // 2
+    for ref, at in ((first_ref, 0), (last_ref, half - EDGE)):
+        ref[NF, 0:EDGE, 0:128] = picks[at : at + EDGE]
+        ref[NF, EDGE : 2 * EDGE, 0:128] = picks[half + at : half + at + EDGE]
+        ref[NF, :, 128:] = jnp.zeros((2 * EDGE, ref.shape[2] - 128), jnp.float32)
+
+
+def asked_kernel(
+    asked_ref, low_ref, high_ref, before_ref, after_ref, table_ref,
+    corner_ref, mask_ref, low_out, high_out, table_out, msg_ref,
+):
+    own_rows = low_ref.shape[1]
+    for level, ref, out in ((0, low_ref, low_out), (1, high_ref, high_out)):
+        rows = slice(EDGE * level, EDGE * level + EDGE)
+        for f in range(NF):
+            out[f] = jnp.concatenate([before_ref[f, rows, :], ref[f], after_ref[f, rows, :]], axis=0)
+    pieces = []
+    for side in range(2):
+        rows = slice(EDGE * side, EDGE * side + EDGE)
+        half = own_rows * side
+        pieces += [before_ref[NF, rows, 0:128], table_ref[half : half + own_rows, :], after_ref[NF, rows, 0:128]]
+    table_out[...] = jnp.concatenate(pieces, axis=0)
     asked = asked_ref[...].reshape(32, 128)
     lane, sub = iota((32, 128), 1), iota((32, 128), 0)
 
@@ -157,23 +175,30 @@
     corner = jnp.where(cell == theta_row, near, jnp.where(cell == theta_row + 1, far, 0.0))
     corner_ref[...] = corner
     rows_p = mask_ref.shape[0]
-    wanted = phi_row + jnp.where(iota((1, 128), 1) < 64, 0, 1)
+    wanted = phi_row + EDGE + jnp.where(iota((1, 128), 1) < 64, 0, 1)
     mask = jnp.where(iota((rows_p, 128), 0) == wanted, 1.0, 0.0)
     mask_ref[...] = mask
     rows_t = low_ref.shape[2]
-    low = low_ref[...].reshape(NF * rows_p, rows_t)
-    high = high_ref[...].reshape(NF * rows_p, rows_t)
+    low = low_out[...].reshape(NF * rows_p, rows_t)
+    high = high_out[...].reshape(NF * rows_p, rows_t)
     answer_into(msg_ref, low, high, corner, mask)
 
 
 def ghost_kernel(reply, table, out_ref):
     got = reply[...].reshape(32, 128)
     picks = table[...]
+    rows = picks.shape[0]
+    half = rows // 2
     ghost = jnp.dot(picks[:, 0:32], got, precision=HIGHEST, preferred_element_type=jnp.float32)
     second = jnp.dot(picks[:, 32:64], got, precision=HIGHEST, preferred_element_type=jnp.float32)
     ghost = ghost + pltpu.roll(second, 128 - SLOT, axis=1)
+    row = iota((rows, 128), 0)
+    row = jnp.where(row < half, row, row - half)
+    before = pltpu.roll(ghost, 128 - 2 * SLOT, axis=1)
+    after = pltpu.roll(ghost, 128 - 4 * SLOT, axis=1)
+    ghost = jnp.where(row < EDGE, before, jnp.where(row < half - EDGE, ghost, after))
     cosine, sine = picks[:, 64:65], picks[:, 65:66]
-    lane = iota((32, 128), 1) & 7
+    lane = iota((rows, 128), 1) & 7
     is_t = (lane == 2) | (lane == 5)
     is_p = (lane == 3) | (lane == 6)
     turned_t = cosine * ghost + sine * pltpu.roll(ghost, 127, axis=1)
@@ -183,8 +208,8 @@
 
 def stage_kernel(stage, n_rad, n_ang, *refs):
     last = stage == 4
-    (sines, low0, high0, below, above, before, after, ghosts) = refs[:8]
-    refs = refs[8:]
+    (sines, low0, high0, below, above, ghosts) = refs[:6]
+    refs = refs[6:]
     if stage == 1:
         low, high = low0, high0
     else:
@@ -195,8 +220,8 @@
         refs = refs[3:]
     else:
         corner, rowmask = refs[:2]
-        low_out, high_out, acc_low_out, acc_high_out, first_out, last_out, msg_out = refs[2:9]
-        refs = refs[9:]
+        low_out, high_out, acc_low_out, acc_high_out, msg_out = refs[2:7]
+        refs = refs[7:]
     slope, up, down = refs
     rad, ang = lax.axis_index("rad"), lax.axis_index("ang")
     rows_p, rows_t = low.shape[1:]
@@ -205,13 +230,11 @@
     ghost = ghosts[...]
 
     sine_row = sines[...]
+    first, final = EDGE, rows_p - EDGE - 1
     rim = []
     for f in range(NF):
-        own = [low[f, 0:1, :], high[f, 0:1, :], low[f, rows_p - 1 :, :], high[f, rows_p - 1 :, :]]
-        own = [MIRROR[f] * item for item in own]
-        start = jnp.where(ang == 0, jnp.concatenate(own[:2], axis=0), before[f])
-        end = jnp.where(ang == n_ang - 1, jnp.concatenate(own[2:], axis=0), after[f])
-        rim.append(jnp.concatenate([start, end, start, end], axis=0))
+        own = [level[f, at : at + 1, :] for at in (first, final) for level in (low, high)]
+        rim.append(MIRROR[f] * jnp.concatenate(own + own, axis=0))
     rim_row = iota((8, rows_t), 0) & 1
     rim_inv = jnp.where(rim_row == 0, invs[0], invs[1]) * sine_row
     speed, pressure = derived(rim)
@@ -255,7 +278,7 @@
             for f in range(NF):
                 at = 8 * level + f
                 lower = ghost[8 * tile : 8 * tile + 8, at : at + 1]
-                upper = ghost[16 + 8 * tile : 24 + 8 * tile, at : at + 1]
+                upper = ghost[rows_p + 8 * tile : rows_p + 8 * tile + 8, at : at + 1]
                 rim_cells.append(jnp.where(half_row, upper, lower))
             rim_speed, rim_pressure = derived(rim_cells)
             rim_flux = flux_along(rim_cells, rim_speed, rim_pressure, 1)
@@ -276,17 +299,20 @@
                 slope[level, f, rows, :] = total
 
     row = iota((rows_p, rows_t), 0)
+    wall_before = (row == first) & (ang == 0)
+    wall_after = (row == final) & (ang == n_ang - 1)
     for level in range(2):
         start, _ = (low0, low) if level == 0 else (high0, high)
         for f in range(NF):
             lower = pltpu.roll(down[level, f], 1, axis=0)
-            lower = jnp.where(row == 0, rim_low[f][level : level + 1, :], lower)
+            lower = jnp.where(wall_before, rim_low[f][level : level + 1, :], lower)
             upper = pltpu.roll(up[level, f], rows_p - 1, axis=0)
-            upper = jnp.where(row == rows_p - 1, rim_high[f][2 + level : 3 + level, :], upper)
+            upper = jnp.where(wall_after, rim_high[f][2 + level : 3 + level, :], upper)
             k = slope[level, f] + lower - upper
             if last:
                 acc = acc_low if level == 0 else acc_high
                 value = start[f] + (time_step / 6.0) * (acc[f] + k)
+                value = pltpu.roll(value, rows_p - EDGE, axis=0)[: rows_p - 2 * EDGE]
                 if f == 0:
                     density_out[0, level] = value
                 elif f < 4:
@@ -302,7 +328,6 @@
             step = time_step if stage == 3 else 0.5 * time_step
             value = start[f] + step * k
             (low_out if level == 0 else high_out)[f] = value
-            send_rows(first_out, last_out, level, f, value)
     if not last:
         new_low = low_out[...].reshape(NF * rows_p, rows_t)
         new_high = high_out[...].reshape(NF * rows_p, rows_t)
@@ -334,8 +359,10 @@
             compiler_params=pltpu.CompilerParams(vmem_limit_bytes=None if plain > 1 else 12 << 20),
         )(*[item if at < plain else held(item) for at, item in enumerate(ins)])
 
-    level = shape(NF, rows_p, rows_t)
-    edge = shape(NF, 2, rows_t)
+    wide = rows_p + 2 * EDGE
+    own_level = shape(NF, rows_p, rows_t)
+    level = shape(NF, wide, rows_t)
+    edge = shape(NF + 1, 2 * EDGE, rows_t)
     message = shape(32, 1, 128)
 
     def shifted(value, axis, by):
@@ -345,13 +372,6 @@
     def crossed(value):
         swap = held(lax.ppermute(value, "panel", [(0, 1), (1, 0)]))
         return held(lax.all_to_all(swap, "ang", split_axis=0, concat_axis=0, tiled=True))
-
-    def halos(low, high, first, final):
-        items = ((high, "rad", 1), (low, "rad", -1), (final, "ang", 1), (first, "ang", -1))
-        out = []
-        for item in items:
-            out.append(shifted(*item))
-        return out
 
     theta = math.pi / 4 + (np.arange(rows_t) + 0.5) * (math.pi / 2 / rows_t)
     sines = jnp.asarray((1.0 / np.sin(theta)).astype(np.float32)).reshape(1, rows_t)
@@ -362,23 +382,28 @@
             density, momentum, magnetic, jnp.swapaxes(partner_device, 1, 2), partner_phi, partner_theta,
             jnp.swapaxes(partner_weight, 1, 2), border_turn, sines,
         ],
-        [level, level, edge, edge, message, shape(32, 128), shape(1, rows_t)],
+        [own_level, own_level, edge, edge, message, shape(32, 128), shape(1, rows_t)],
         plain=9,
     )
-    around = halos(low0, high0, first, final)
-    corner, rowmask, answer = call(
-        asked_kernel, [crossed(ask), low0, high0], [shape(rows_t, 128), shape(rows_p, 128), message]
+    before = shifted(final, "ang", 1)
+    after = shifted(first, "ang", -1)
+    corner, rowmask, low0, high0, table, answer = call(
+        asked_kernel,
+        [crossed(ask), low0, high0, before, after, table],
+        [shape(rows_t, 128), shape(wide, 128), level, level, shape(2 * wide, 128), message],
     )
     low, high, sums = low0, high0, []
-    scratch = [pltpu.VMEM((2, NF, rows_p, rows_t), f32) for _ in range(3)]
+    scratch = [pltpu.VMEM((2, NF, wide, rows_t), f32) for _ in range(3)]
     for stage in range(1, 5):
-        (ghosts,) = call(ghost_kernel, [crossed(answer), table], [shape(32, 128)])
-        ins = [sines, low0, high0, *around, ghosts]
+        below = shifted(high, "rad", 1)
+        above = shifted(low, "rad", -1)
+        (ghosts,) = call(ghost_kernel, [crossed(answer), table], [shape(2 * wide, 128)])
+        ins = [sines, low0, high0, below, above, ghosts]
         if stage > 1:
             ins += [low, high, *sums]
         if stage < 4:
             ins += [corner, rowmask]
-            outs = [level, level, level, level, edge, edge, message]
+            outs = [level, level, level, level, message]
         else:
             outs = [
                 shape(1, rows_r, rows_p, rows_t, final=True),
@@ -392,9 +417,8 @@
         result = call(kernel, ins, outs, scratch)
         if stage == 4:
             return tuple(result)
-        low, high, acc_low, acc_high, first, final, answer = result
+        low, high, acc_low, acc_high, answer = result
         sums = [acc_low, acc_high]
-        around = halos(low, high, first, final)
 
 
 def solution(mesh):

time: 116 us -> 109 us (0.940)
  blocking collectives: 20 us -> 71.4 us
  starting transfers between devices: 51.6 us -> 15.5 us
  waiting for transfers between devices: 32.4 us -> 5.93 us
  Pallas kernels: 10.7 us -> 14.1 us
    all_to_all x1 -> x5, blocking collectives: 20 us -> 71.4 us  [crossed(): lax.all_to_all(swap, 'ang', split_axis=0, concat_axis=0, tiled=True)]
    all_to_all x4 -> x0, starting transfers between devices: 29.9 us -> none  [crossed(): lax.all_to_all(swap, 'ang', split_axis=0, concat_axis=0, tiled=True)]
    all_to_all x4 -> x0, waiting for transfers between devices: 25.9 us -> none  [crossed(): lax.all_to_all(swap, 'ang', split_axis=0, concat_axis=0, tiled=True)]
    ppermute x16 -> x10, starting transfers between devices: 21.5 us -> 15.5 us  [shifted(): lax.ppermute(value, axis, [(i, (i + by) % size) for i in range(size)])]
    pallas_call x10, Pallas kernels: 10.7 us -> 14.1 us  [call(): pl.pallas_call(kernel, out_shape=outs, in_specs=[vmem] * len(ins), out_sp...]
  transfers between devices with their start and end apart: 25 -> 15, of which waited for: 9 -> 5; matrix products, arithmetic and copies ran while one was open for 0% -> 0% of each run, Pallas kernels for 2% -> 2%
where the time goes in v4:
time: 109 us; the launch traced here: 108 us
  blocking collectives  71.4 us (66%)
  starting transfers between devices  15.5 us (14%)
  Pallas kernels  14.1 us (13%)
  waiting for transfers between devices  5.93 us (5%)
    all_to_all x5, blocking collectives, crossed(): lax.all_to_all(swap, 'ang', split_axis=0, concat_axis=0, tiled=True)  71.4 us
    ppermute x10, starting transfers between devices, shifted(): lax.ppermute(value, axis, [(i, (i + by) % size) for i in range(size)])  15.5 us
    pallas_call x10, Pallas kernels, call(): pl.pallas_call(kernel, out_shape=outs, in_specs=[vmem] * len(ins), out_sp...  14.1 us
    ppermute x5, waiting for transfers between devices, crossed(): swap = held(lax.ppermute(value, 'panel', [(0, 1), (1, 0)]))  5.91 us
  transfers between devices with their start and end apart: 15, of which 5 were waited for; matrix products, arithmetic and copies ran while one was open for 0% of the time, Pallas kernels for 2%

profile of v4, /device:TPU:2, one launch (start us, length us, event | category | flops | bytes accessed | tf_op | source)
XLA Modules:
  0.0 107.7 jit_solution(17433529749659479091)
XLA Ops:
  0.6 1.5 %shard_map.112 = (f32[7,16,512]{2,1,0:T(8,128)S(1)}, f32[7,16,512]{2,1,0:T(8,128)S(1)}, f32[8,8,512]{2,1,0:T(8,128)S(1)}, f32[8,8,512]{2,1,0:T(8,128)S(1)}, f32[...) custom-call(f32[1,2,16,512]{3,2,1,0:T(8,128)} %density.1, f32[1,3,2,16,512]{4,3,2,1,0:T(8,128)} %momentum.1, ...), custom_call_target="tpu_custom_call" | custom-call | tf_op jit(solution)/shard_map/pallas_call | solution.py:352
  2.1 1.6 %collective-permute-start.1 = (f32[8,8,512]{2,1,0:T(8,128)S(1)}, f32[8,8,512]{2,1,0:T(8,128)S(1)}, u32[]{:S(2)}, u32[]{:S(2)}) collective-permute-start(f32[8,8,512]{2,1,0:T(8,128)S(1)} %get-tuple-element.35), channel_id=1, source_target_pairs={{0,4},{4,8},{8,12},{12,16},{16,20},{20,24},{24,28},{28,32},{32,36}... | collective-permute-start | bytes 393224 | tf_op jit(solution)/shard_map/ppermute | solution.py:370
  3.7 0.8 collective-permute-start.2
  4.6 0.0 collective-permute-start
  4.6 1.2 %collective-permute-done = f32[32,1,128]{2,1,0:T(1,128)S(1)} collective-permute-done((f32[32,1,128]{2,1,0:T(1,128)S(1)}, f32[32,1,128]{2,1,0:T(1,128)S(1)}, u32[]{:S(2)}, u32[]{:S(2)}) %collective-permute-start) | collective-permute-done | bytes 16416 | tf_op jit(solution)/shard_map/ppermute | solution.py:373
  5.7 20.5 %all_to_all.25.asked_ref = f32[32,1,128]{2,1,0:T(1,128)S(1)} all-to-all(f32[32,1,128]{2,1,0:T(1,128)S(1)} %collective-permute-done), channel_id=1, replica_groups=mesh['panel'=2,'ang'=32,'rad'=4] {'ang'}, dimensions={0} | all-to-all | bytes 32768 | tf_op jit(solution)/shard_map/all_to_all | solution.py:374
  26.2 0.0 collective-permute-done.1.before_ref
  26.2 0.0 collective-permute-done.2.after_ref
  26.3 1.6 %shard_map.113 = (f32[512,128]{1,0:T(8,128)S(1)}, f32[24,128]{1,0:T(8,128)S(1)}, f32[7,24,512]{2,1,0:T(8,128)S(1)}, f32[7,24,512]{2,1,0:T(8,128)S(1)}, f32[48,128]{1,0:T(8,128)S(1)}, /*index=5*/f32[32,1,128]{2,1,0:T(1,128)S(1)}) custom-call(f32[32,1,128]{2,1,0:T(1,128)S(1)} %all_to_all.25.asked_ref, f32[7,16,512]{2,1,0:T(8,128)S(1)} %get-tuple-element.33.low_ref, ...), custom_call_target="tpu_custom_call" | custom-call | tf_op jit(solution)/shard_map/pallas_call | solution.py:352
  27.8 3.1 %collective-permute-start.4 = (f32[7,24,512]{2,1,0:T(8,128)S(1)}, f32[7,24,512]{2,1,0:T(8,128)S(1)}, u32[]{:S(2)}, u32[]{:S(2)}) collective-permute-start(f32[7,24,512]{2,1,0:T(8,128)S(1)} %get-tuple-element.38.refs_1_), channel_id=1, source_target_pairs={{0,3},{1,0},{2,1},{3,2},{4,7},{5,4},{6,5},{7,6},{8,11},{9,8},{10,9... | collective-permute-start | bytes 1032200 | tf_op jit(solution)/shard_map/ppermute | solution.py:370
  30.9 1.2 %collective-permute-done.5 = f32[32,1,128]{2,1,0:T(1,128)S(1)} collective-permute-done((f32[32,1,128]{2,1,0:T(1,128)S(1)}, f32[32,1,128]{2,1,0:T(1,128)S(1)}, u32[]{:S(2)}, u32[]{:S(2)}) %collective-permute-start.5) | collective-permute-done | bytes 16416 | tf_op jit(solution)/shard_map/ppermute | solution.py:373
  32.1 12.7 %all_to_all.26.reply = f32[32,1,128]{2,1,0:T(1,128)S(1)} all-to-all(f32[32,1,128]{2,1,0:T(1,128)S(1)} %collective-permute-done.5), channel_id=1, replica_groups=mesh['panel'=2,'ang'=32,'rad'=4] {'ang'}, dimensions={0} | all-to-all | bytes 32768 | tf_op jit(solution)/shard_map/all_to_all | solution.py:374
  44.8 0.4 shard_map.114.refs_5_
  45.3 2.3 %shard_map.115 = (f32[7,24,512]{2,1,0:T(8,128)S(1)}, f32[7,24,512]{2,1,0:T(8,128)S(1)}, f32[7,24,512]{2,1,0:T(8,128)S(1)}, f32[7,24,512]{2,1,0:T(8,128)S(1)}, f32[32,1,128]{2,1,0:T(1,128)S(1)}) custom-call(f32[1,512]{1,0:T(1,128)S(1)} %get-tuple-element.31.refs_0_, f32[7,24,512]{2,1,0:T(8,128)S(1)} %get-tuple-element.38.refs_1_, ...), custom_call_target="tpu_custom_call" | custom-call | tf_op jit(solution)/shard_map/pallas_call | solution.py:352
  47.7 0.7 collective-permute-start.6
  48.3 2.7 %collective-permute-start.7 = (f32[7,24,512]{2,1,0:T(8,128)S(1)}, f32[7,24,512]{2,1,0:T(8,128)S(1)}, u32[]{:S(2)}, u32[]{:S(2)}) collective-permute-start(f32[7,24,512]{2,1,0:T(8,128)S(1)} %get-tuple-element.45.refs_6_), channel_id=1, source_target_pairs={{0,3},{1,0},{2,1},{3,2},{4,7},{5,4},{6,5},{7,6},{8,11},{9,8},{10,9... | collective-permute-start | bytes 1032200 | tf_op jit(solution)/shard_map/ppermute | solution.py:370
  51.1 1.2 %collective-permute-done.8 = f32[32,1,128]{2,1,0:T(1,128)S(1)} collective-permute-done((f32[32,1,128]{2,1,0:T(1,128)S(1)}, f32[32,1,128]{2,1,0:T(1,128)S(1)}, u32[]{:S(2)}, u32[]{:S(2)}) %collective-permute-start.8) | collective-permute-done | bytes 16416 | tf_op jit(solution)/shard_map/ppermute | solution.py:373
  52.2 12.7 %all_to_all.27.reply = f32[32,1,128]{2,1,0:T(1,128)S(1)} all-to-all(f32[32,1,128]{2,1,0:T(1,128)S(1)} %collective-permute-done.8), channel_id=1, replica_groups=mesh['panel'=2,'ang'=32,'rad'=4] {'ang'}, dimensions={0} | all-to-all | bytes 32768 | tf_op jit(solution)/shard_map/all_to_all | solution.py:374
  65.0 0.4 shard_map.116.refs_5_
  65.4 2.4 %shard_map.117 = (f32[7,24,512]{2,1,0:T(8,128)S(1)}, f32[7,24,512]{2,1,0:T(8,128)S(1)}, f32[7,24,512]{2,1,0:T(8,128)S(1)}, f32[7,24,512]{2,1,0:T(8,128)S(1)}, f32[32,1,128]{2,1,0:T(1,128)S(1)}) custom-call(f32[1,512]{1,0:T(1,128)S(1)} %get-tuple-element.31.refs_0_, f32[7,24,512]{2,1,0:T(8,128)S(1)} %get-tuple-element.38.refs_1_, ...), custom_call_target="tpu_custom_call" | custom-call | tf_op jit(solution)/shard_map/pallas_call | solution.py:352
  67.9 0.1 collective-permute-start.9
  68.0 3.2 %collective-permute-start.10 = (f32[7,24,512]{2,1,0:T(8,128)S(1)}, f32[7,24,512]{2,1,0:T(8,128)S(1)}, u32[]{:S(2)}, u32[]{:S(2)}) collective-permute-start(f32[7,24,512]{2,1,0:T(8,128)S(1)} %get-tuple-element.50.refs_6_), channel_id=1, source_target_pairs={{0,3},{1,0},{2,1},{3,2},{4,7},{5,4},{6,5},{7,6},{8,11},{9,8},{10,9... | collective-permute-start | bytes 1032200 | tf_op jit(solution)/shard_map/ppermute | solution.py:370
  71.2 1.2 %collective-permute-done.11 = f32[32,1,128]{2,1,0:T(1,128)S(1)} collective-permute-done((f32[32,1,128]{2,1,0:T(1,128)S(1)}, f32[32,1,128]{2,1,0:T(1,128)S(1)}, u32[]{:S(2)}, u32[]{:S(2)}) %collective-permute-start.11) | collective-permute-done | bytes 16416 | tf_op jit(solution)/shard_map/ppermute | solution.py:373
  72.4 12.7 %all_to_all.28.reply = f32[32,1,128]{2,1,0:T(1,128)S(1)} all-to-all(f32[32,1,128]{2,1,0:T(1,128)S(1)} %collective-permute-done.11), channel_id=1, replica_groups=mesh['panel'=2,'ang'=32,'rad'=4] {'ang'}, dimensions={0} | all-to-all | bytes 32768 | tf_op jit(solution)/shard_map/all_to_all | solution.py:374
  85.1 0.4 shard_map.118.refs_5_
  85.5 2.4 %shard_map.119 = (f32[7,24,512]{2,1,0:T(8,128)S(1)}, f32[7,24,512]{2,1,0:T(8,128)S(1)}, f32[7,24,512]{2,1,0:T(8,128)S(1)}, f32[7,24,512]{2,1,0:T(8,128)S(1)}, f32[32,1,128]{2,1,0:T(1,128)S(1)}) custom-call(f32[1,512]{1,0:T(1,128)S(1)} %get-tuple-element.31.refs_0_, f32[7,24,512]{2,1,0:T(8,128)S(1)} %get-tuple-element.38.refs_1_, ...), custom_call_target="tpu_custom_call" | custom-call | tf_op jit(solution)/shard_map/pallas_call | solution.py:352
  87.9 0.1 collective-permute-start.12
  88.0 3.2 %collective-permute-start.13 = (f32[7,24,512]{2,1,0:T(8,128)S(1)}, f32[7,24,512]{2,1,0:T(8,128)S(1)}, u32[]{:S(2)}, u32[]{:S(2)}) collective-permute-start(f32[7,24,512]{2,1,0:T(8,128)S(1)} %get-tuple-element.55.refs_6_), channel_id=1, source_target_pairs={{0,3},{1,0},{2,1},{3,2},{4,7},{5,4},{6,5},{7,6},{8,11},{9,8},{10,9... | collective-permute-start | bytes 1032200 | tf_op jit(solution)/shard_map/ppermute | solution.py:370
  91.2 1.2 %collective-permute-done.14 = f32[32,1,128]{2,1,0:T(1,128)S(1)} collective-permute-done((f32[32,1,128]{2,1,0:T(1,128)S(1)}, f32[32,1,128]{2,1,0:T(1,128)S(1)}, u32[]{:S(2)}, u32[]{:S(2)}) %collective-permute-start.14) | collective-permute-done | bytes 16416 | tf_op jit(solution)/shard_map/ppermute | solution.py:373
  92.4 12.7 %all_to_all.29.reply = f32[32,1,128]{2,1,0:T(1,128)S(1)} all-to-all(f32[32,1,128]{2,1,0:T(1,128)S(1)} %collective-permute-done.14), channel_id=1, replica_groups=mesh['panel'=2,'ang'=32,'rad'=4] {'ang'}, dimensions={0} | all-to-all | bytes 32768 | tf_op jit(solution)/shard_map/all_to_all | solution.py:374
  105.1 0.4 shard_map.120.refs_5_
  105.6 2.1 %shard_map.121 = (f32[1,2,16,512]{3,2,1,0:T(8,128)}, f32[1,3,2,16,512]{4,3,2,1,0:T(8,128)}, f32[1,3,2,16,512]{4,3,2,1,0:T(8,128)}) custom-call(f32[1,512]{1,0:T(1,128)S(1)} %get-tuple-element.31.refs_0_, f32[7,24,512]{2,1,0:T(8,128)S(1)} %get-tuple-element.38.refs_1_, f32[7,24,512]{2,1,0:T(8,128)S(1)} %get-tuple-element.39.refs_2_, ...), custom_call_target="tpu_custom_call" | custom-call | tf_op jit(solution)/shard_map/pallas_call | solution.py:352
  (13 shorter events, 0.0 us)
Async XLA Ops:
  2.1 24.1 %collective-permute-start.1 = (f32[8,8,512]{2,1,0:T(8,128)S(1)}, f32[8,8,512]{2,1,0:T(8,128)S(1)}, u32[]{:S(2)}, u32[]{:S(2)}) collective-permute-start(f32[8,8,512]{2,1,0:T(8,128)S(1)} %get-tuple-element.35), channel_id=1, source_target_pairs={{0,4},{4,8},{8,12},{12,16},{16,20},{20,24},{24,28},{28,32},{32,36}... | collective-permute-start | bytes 393224 | tf_op jit(solution)/shard_map/ppermute | solution.py:370
  3.7 22.5 %collective-permute-start.2 = (f32[8,8,512]{2,1,0:T(8,128)S(1)}, f32[8,8,512]{2,1,0:T(8,128)S(1)}, u32[]{:S(2)}, u32[]{:S(2)}) collective-permute-start(f32[8,8,512]{2,1,0:T(8,128)S(1)} %get-tuple-element.36), channel_id=1, source_target_pairs={{0,124},{4,0},{8,4},{12,8},{16,12},{20,16},{24,20},{28,24},{32,28}... | collective-permute-start | bytes 393224 | tf_op jit(solution)/shard_map/ppermute | solution.py:370
  4.6 1.2 %collective-permute-start = (f32[32,1,128]{2,1,0:T(1,128)S(1)}, f32[32,1,128]{2,1,0:T(1,128)S(1)}, u32[]{:S(2)}, u32[]{:S(2)}) collective-permute-start(f32[32,1,128]{2,1,0:T(1,128)S(1)} %get-tuple-element.32), channel_id=1, source_target_pairs={{0,128},{128,0},{1,129},{129,1},{2,130},{130,2},{3,131},{131,3},{4... | collective-permute-start | bytes 49160 | tf_op jit(solution)/shard_map/ppermute | solution.py:373
  27.8 17.5 %collective-permute-start.4 = (f32[7,24,512]{2,1,0:T(8,128)S(1)}, f32[7,24,512]{2,1,0:T(8,128)S(1)}, u32[]{:S(2)}, u32[]{:S(2)}) collective-permute-start(f32[7,24,512]{2,1,0:T(8,128)S(1)} %get-tuple-element.38.refs_1_), channel_id=1, source_target_pairs={{0,3},{1,0},{2,1},{3,2},{4,7},{5,4},{6,5},{7,6},{8,11},{9,8},{10,9... | collective-permute-start | bytes 1032200 | tf_op jit(solution)/shard_map/ppermute | solution.py:370
  30.9 14.4 %collective-permute-start.3 = (f32[7,24,512]{2,1,0:T(8,128)S(1)}, f32[7,24,512]{2,1,0:T(8,128)S(1)}, u32[]{:S(2)}, u32[]{:S(2)}) collective-permute-start(f32[7,24,512]{2,1,0:T(8,128)S(1)} %get-tuple-element.39.refs_2_), channel_id=1, source_target_pairs={{0,1},{1,2},{2,3},{3,0},{4,5},{5,6},{6,7},{7,4},{8,9},{9,10},{10,1... | collective-permute-start | bytes 1032200 | tf_op jit(solution)/shard_map/ppermute | solution.py:370
  30.9 1.2 %collective-permute-start.5 = (f32[32,1,128]{2,1,0:T(1,128)S(1)}, f32[32,1,128]{2,1,0:T(1,128)S(1)}, u32[]{:S(2)}, u32[]{:S(2)}) collective-permute-start(f32[32,1,128]{2,1,0:T(1,128)S(1)} %get-tuple-element.40), channel_id=1, source_target_pairs={{0,128},{128,0},{1,129},{129,1},{2,130},{130,2},{3,131},{131,3},{4... | collective-permute-start | bytes 49160 | tf_op jit(solution)/shard_map/ppermute | solution.py:373
  47.7 17.8 %collective-permute-start.6 = (f32[7,24,512]{2,1,0:T(8,128)S(1)}, f32[7,24,512]{2,1,0:T(8,128)S(1)}, u32[]{:S(2)}, u32[]{:S(2)}) collective-permute-start(f32[7,24,512]{2,1,0:T(8,128)S(1)} %get-tuple-element.44.refs_7_), channel_id=1, source_target_pairs={{0,1},{1,2},{2,3},{3,0},{4,5},{5,6},{6,7},{7,4},{8,9},{9,10},{10,1... | collective-permute-start | bytes 1032200 | tf_op jit(solution)/shard_map/ppermute | solution.py:370
  48.3 17.1 %collective-permute-start.7 = (f32[7,24,512]{2,1,0:T(8,128)S(1)}, f32[7,24,512]{2,1,0:T(8,128)S(1)}, u32[]{:S(2)}, u32[]{:S(2)}) collective-permute-start(f32[7,24,512]{2,1,0:T(8,128)S(1)} %get-tuple-element.45.refs_6_), channel_id=1, source_target_pairs={{0,3},{1,0},{2,1},{3,2},{4,7},{5,4},{6,5},{7,6},{8,11},{9,8},{10,9... | collective-permute-start | bytes 1032200 | tf_op jit(solution)/shard_map/ppermute | solution.py:370
  51.1 1.2 %collective-permute-start.8 = (f32[32,1,128]{2,1,0:T(1,128)S(1)}, f32[32,1,128]{2,1,0:T(1,128)S(1)}, u32[]{:S(2)}, u32[]{:S(2)}) collective-permute-start(f32[32,1,128]{2,1,0:T(1,128)S(1)} %get-tuple-element.46), channel_id=1, source_target_pairs={{0,128},{128,0},{1,129},{129,1},{2,130},{130,2},{3,131},{131,3},{4... | collective-permute-start | bytes 49160 | tf_op jit(solution)/shard_map/ppermute | solution.py:373
  67.9 17.7 %collective-permute-start.9 = (f32[7,24,512]{2,1,0:T(8,128)S(1)}, f32[7,24,512]{2,1,0:T(8,128)S(1)}, u32[]{:S(2)}, u32[]{:S(2)}) collective-permute-start(f32[7,24,512]{2,1,0:T(8,128)S(1)} %get-tuple-element.49.refs_7_), channel_id=1, source_target_pairs={{0,1},{1,2},{2,3},{3,0},{4,5},{5,6},{6,7},{7,4},{8,9},{9,10},{10,1... | collective-permute-start | bytes 1032200 | tf_op jit(solution)/shard_map/ppermute | solution.py:370
  68.0 17.6 %collective-permute-start.10 = (f32[7,24,512]{2,1,0:T(8,128)S(1)}, f32[7,24,512]{2,1,0:T(8,128)S(1)}, u32[]{:S(2)}, u32[]{:S(2)}) collective-permute-start(f32[7,24,512]{2,1,0:T(8,128)S(1)} %get-tuple-element.50.refs_6_), channel_id=1, source_target_pairs={{0,3},{1,0},{2,1},{3,2},{4,7},{5,4},{6,5},{7,6},{8,11},{9,8},{10,9... | collective-permute-start | bytes 1032200 | tf_op jit(solution)/shard_map/ppermute | solution.py:370
  71.2 1.2 %collective-permute-start.11 = (f32[32,1,128]{2,1,0:T(1,128)S(1)}, f32[32,1,128]{2,1,0:T(1,128)S(1)}, u32[]{:S(2)}, u32[]{:S(2)}) collective-permute-start(f32[32,1,128]{2,1,0:T(1,128)S(1)} %get-tuple-element.51), channel_id=1, source_target_pairs={{0,128},{128,0},{1,129},{129,1},{2,130},{130,2},{3,131},{131,3},{4... | collective-permute-start | bytes 49160 | tf_op jit(solution)/shard_map/ppermute | solution.py:373
  87.9 17.7 %collective-permute-start.12 = (f32[7,24,512]{2,1,0:T(8,128)S(1)}, f32[7,24,512]{2,1,0:T(8,128)S(1)}, u32[]{:S(2)}, u32[]{:S(2)}) collective-permute-start(f32[7,24,512]{2,1,0:T(8,128)S(1)} %get-tuple-element.54.refs_7_), channel_id=1, source_target_pairs={{0,1},{1,2},{2,3},{3,0},{4,5},{5,6},{6,7},{7,4},{8,9},{9,10},{10,1... | collective-permute-start | bytes 1032200 | tf_op jit(solution)/shard_map/ppermute | solution.py:370
  88.0 17.6 %collective-permute-start.13 = (f32[7,24,512]{2,1,0:T(8,128)S(1)}, f32[7,24,512]{2,1,0:T(8,128)S(1)}, u32[]{:S(2)}, u32[]{:S(2)}) collective-permute-start(f32[7,24,512]{2,1,0:T(8,128)S(1)} %get-tuple-element.55.refs_6_), channel_id=1, source_target_pairs={{0,3},{1,0},{2,1},{3,2},{4,7},{5,4},{6,5},{7,6},{8,11},{9,8},{10,9... | collective-permute-start | bytes 1032200 | tf_op jit(solution)/shard_map/ppermute | solution.py:370
  91.2 1.2 %collective-permute-start.14 = (f32[32,1,128]{2,1,0:T(1,128)S(1)}, f32[32,1,128]{2,1,0:T(1,128)S(1)}, u32[]{:S(2)}, u32[]{:S(2)}) collective-permute-start(f32[32,1,128]{2,1,0:T(1,128)S(1)} %get-tuple-element.56), channel_id=1, source_target_pairs={{0,128},{128,0},{1,129},{129,1},{2,130},{130,2},{3,131},{131,3},{4... | collective-permute-start | bytes 49160 | tf_op jit(solution)/shard_map/ppermute | solution.py:373

commit v5 on v4

v5 whole, which is shorter than its diff:
```python
import math

import jax
import jax.numpy as jnp
import numpy as np
from jax import lax
from jax.experimental import pallas as pl
from jax.experimental.pallas import tpu as pltpu
from jax.sharding import PartitionSpec as P

time_step = 0.15
diffusion = 0.1
r_inner = 0.35
NF = 7
MIRROR = (1.0, -1.0, -1.0, -1.0, 1.0, 1.0, 1.0)
INTERPRET = False
EDGE = 4
SLOT = 16
HIGHEST = lax.Precision.HIGHEST


def iota(shape, dim):
    return lax.broadcasted_iota(jnp.int32, shape, dim)


def derived(cells):
    inverse = 1.0 / cells[0]
    speed = [cells[1 + c] * inverse for c in range(3)]
    pressure = cells[0] + 0.5 * (
        cells[4] * cells[4] + cells[5] * cells[5] + cells[6] * cells[6]
    )
    return speed, pressure


def stresses(cells, speed, pressure, pairs):
    moment, magnet = cells[1:4], cells[4:7]
    out = {}
    for c, d in pairs:
        term = moment[c] * speed[d] - magnet[c] * magnet[d]
        if c == d:
            out["T", c, d] = term + pressure
        else:
            out["T", c, d] = out["T", d, c] = term
            out["E", c, d] = speed[c] * magnet[d] - magnet[c] * speed[d]
    return out


def flux_along(cells, found, d):
    out = [(1, cells[1 + d])]
    for c in range(3):
        out.append((1, found["T", d, c]))
    for c in range(3):
        if c == d:
            out.append((0, None))
        elif c > d:
            out.append((1, found["E", d, c]))
        else:
            out.append((-1, found["E", c, d]))
    return out


ALL_PAIRS = ((0, 0), (0, 1), (0, 2), (1, 1), (1, 2), (2, 2))


def given(flux, cell, half, spread):
    sign, value = flux
    if cell is None:
        moved = half * value
        return moved, -moved
    spreading = spread * cell
    if not sign:
        return spreading, spreading
    moved = half * value
    plus, minus = spreading + moved, spreading - moved
    return (plus, minus) if sign > 0 else (minus, plus)


def inverse_radius(rad, n_rad, slot, rows_r):
    value = None
    for at in range(n_rad):
        level = 1 - (at & 1) if slot == 0 else at & 1
        radius = r_inner + (at * rows_r + level + 0.5) * ((1.0 - r_inner) / (rows_r * n_rad))
        item = jnp.float32(1.0 / radius)
        value = item if value is None else jnp.where(rad == at, item, value)
    return value


def partners(size, step):
    return [(i, (i ^ 1) if step == 0 else (((i + 1) ^ 1) - 1) % size) for i in range(size)]


def answer_into(msg_ref, low, high, corner, rowmask):
    cells = jnp.concatenate([low, high], axis=0)
    product = None
    for _ in range(3):
        part = cells.astype(jnp.bfloat16)
        cells = cells - part.astype(jnp.float32)
        item = jnp.dot(part, corner, preferred_element_type=jnp.float32)
        product = item if product is None else product + item
    product = product.reshape(2, NF, rowmask.shape[0], 128)
    picked = jnp.sum(jnp.where(rowmask != 0.0, product * rowmask, 0.0), axis=2)
    gap = jnp.zeros((1, 128), jnp.float32)
    parts = [picked[0], gap, picked[1], gap]
    both = jnp.concatenate(parts, axis=0)
    both = both + pltpu.roll(both, 64, axis=1)
    turned = both.T
    lanes = jnp.concatenate([turned, jnp.zeros((128, 128 - SLOT), jnp.float32)], axis=1)
    own = lanes[0:32] + pltpu.roll(lanes[32:64], SLOT, axis=1)
    before = pltpu.roll(pltpu.roll(own, 1, axis=0), 2 * SLOT, axis=1)
    after = pltpu.roll(pltpu.roll(own, 31, axis=0), 4 * SLOT, axis=1)
    msg_ref[...] = (own + before + after).reshape(msg_ref.shape)


def open_kernel(
    density, momentum, magnetic, device, phi, theta, weight, turn, sines,
    low_ref, high_ref, first_ref, last_ref, ask_ref, table_ref, sines_ref,
):
    sines_ref[...] = sines[...]
    odd = lax.axis_index("rad") & 1
    even_ang = (lax.axis_index("ang") & 1) == 0

    def edges(f, at, top, bottom):
        width = top.shape[1]
        first_ref[f, at : at + EDGE, 0:width] = jnp.where(even_ang, bottom, top)
        last_ref[f, at : at + EDGE, 0:width] = jnp.where(even_ang, top, bottom)

    for slot, ref in ((0, low_ref), (1, high_ref)):
        level = 1 - odd if slot == 0 else odd
        for f in range(NF):
            if f == 0:
                value = density[0, level]
            elif f < 4:
                value = momentum[0, f - 1, level]
            else:
                value = magnetic[0, f - 4, level]
            ref[f] = value
            edges(f, EDGE * slot, value[:EDGE], value[value.shape[0] - EDGE :])
    rows = device.shape[2]
    one, two = iota((rows, rows), 0), iota((rows, rows), 1)
    eye = one == two
    dev_row = device[0]
    dev_col = jnp.sum(jnp.where(eye, jnp.broadcast_to(dev_row, (rows, rows)), 0), axis=1, keepdims=True)
    same = dev_col == dev_row
    rank_row = jnp.sum(jnp.where(same & (one < two), 1, 0), axis=0, keepdims=True)
    rank_col = jnp.sum(jnp.where(same & (two < one), 1, 0), axis=1, keepdims=True)

    def column(row):
        return jnp.sum(jnp.where(eye, jnp.broadcast_to(row, (rows, rows)), 0.0), axis=1, keepdims=True)

    phi_col = column(phi[...].astype(jnp.float32))
    theta_col = column(theta[...].astype(jnp.float32))
    weights = weight[0]
    lane = iota((rows, 128), 1)
    items = [phi_col, theta_col] + [column(weights[c : c + 1, :]) for c in range(4)]
    record = jnp.zeros((rows, 128), jnp.float32)
    for at, item in enumerate(items):
        record = jnp.where(lane == at, item, record)
    asked = jnp.zeros((rows, 128), jnp.float32)
    for slot in range(2):
        placing = jnp.where((one == dev_row) & (rank_row == slot), 1.0, 0.0)
        moved = record if slot == 0 else pltpu.roll(record, 8, axis=1)
        asked = asked + jnp.dot(placing, moved, precision=HIGHEST, preferred_element_type=jnp.float32)
    ask_ref[...] = asked.reshape(ask_ref.shape)
    picks = jnp.where(((lane & 31) == dev_col) & ((lane >> 5) == rank_col) & (lane < 64), 1.0, 0.0)
    cosine = column(jnp.cos(turn[...]))
    sine = column(jnp.sin(turn[...]))
    picks = jnp.where(lane == 64, cosine, picks)
    picks = jnp.where(lane == 65, sine, picks)
    table_ref[...] = picks
    half = rows // 2
    for side in range(2):
        at = half * side
        edges(NF, EDGE * side, picks[at : at + EDGE], picks[at + half - EDGE : at + half])
    for ref in (first_ref, last_ref):
        ref[NF, :, 128:] = jnp.zeros((2 * EDGE, ref.shape[2] - 128), jnp.float32)


def asked_kernel(
    asked_ref, low_ref, high_ref, one_ref, two_ref, table_ref,
    corner_ref, mask_ref, low_out, high_out, table_out, msg_ref,
):
    own_rows = low_ref.shape[1]
    even_ang = (lax.axis_index("ang") & 1) == 0

    def beside(f, rows, width):
        one, two = one_ref[f, rows, 0:width], two_ref[f, rows, 0:width]
        return jnp.where(even_ang, two, one), jnp.where(even_ang, one, two)

    for level, ref, out in ((0, low_ref, low_out), (1, high_ref, high_out)):
        rows = slice(EDGE * level, EDGE * level + EDGE)
        for f in range(NF):
            before, after = beside(f, rows, ref.shape[2])
            out[f] = jnp.concatenate([before, ref[f], after], axis=0)
    pieces = []
    for side in range(2):
        rows = slice(EDGE * side, EDGE * side + EDGE)
        half = own_rows * side
        before, after = beside(NF, rows, 128)
        pieces += [before, table_ref[half : half + own_rows, :], after]
    table_out[...] = jnp.concatenate(pieces, axis=0)
    asked = asked_ref[...].reshape(32, 128)
    lane, sub = iota((32, 128), 1), iota((32, 128), 0)

    def row_of(at):
        total = jnp.zeros((32, 128), jnp.float32)
        for part in range(4):
            slot = part & 1
            col = asked[:, slot * 8 + at[part >> 1] : slot * 8 + at[part >> 1] + 1]
            total = jnp.where(lane == sub + 32 * part, col, total)
        return jnp.sum(total, axis=0, keepdims=True)

    phi_row = row_of((0, 0)).astype(jnp.int32) + EDGE
    theta_row = row_of((1, 1)).astype(jnp.int32) + jnp.where(iota((1, 128), 1) < 64, 0, 1)
    near = row_of((2, 3))
    far = row_of((4, 5))
    corner = jnp.where(iota((corner_ref.shape[0], 128), 0) == theta_row, 1.0, 0.0).astype(jnp.bfloat16)
    corner_ref[...] = corner
    rows_p = mask_ref.shape[0]
    at = iota((rows_p, 128), 0)
    mask = jnp.where(at == phi_row, near, jnp.where(at == phi_row + 1, far, 0.0))
    mask_ref[...] = mask
    rows_t = low_ref.shape[2]
    low = low_out[...].reshape(NF * rows_p, rows_t)
    high = high_out[...].reshape(NF * rows_p, rows_t)
    answer_into(msg_ref, low, high, corner, mask)


def ghost_kernel(reply, table, out_ref):
    got = reply[...].reshape(32, 128)
    picks = table[...]
    rows = picks.shape[0]
    half = rows // 2
    ghost = jnp.dot(picks[:, 0:32], got, precision=HIGHEST, preferred_element_type=jnp.float32)
    second = jnp.dot(picks[:, 32:64], got, precision=HIGHEST, preferred_element_type=jnp.float32)
    ghost = ghost + pltpu.roll(second, 128 - SLOT, axis=1)
    row = iota((rows, 128), 0)
    row = jnp.where(row < half, row, row - half)
    before = pltpu.roll(ghost, 128 - 2 * SLOT, axis=1)
    after = pltpu.roll(ghost, 128 - 4 * SLOT, axis=1)
    ghost = jnp.where(row < EDGE, before, jnp.where(row < half - EDGE, ghost, after))
    cosine, sine = picks[:, 64:65], picks[:, 65:66]
    lane = iota((rows, 128), 1) & 7
    is_t = (lane == 2) | (lane == 5)
    is_p = (lane == 3) | (lane == 6)
    turned_t = cosine * ghost + sine * pltpu.roll(ghost, 127, axis=1)
    turned_p = cosine * ghost - sine * pltpu.roll(ghost, 1, axis=1)
    out_ref[...] = jnp.where(is_t, turned_t, jnp.where(is_p, turned_p, ghost))


def stage_kernel(stage, n_rad, n_ang, *refs):
    last = stage == 4
    (sines, low0, high0, below, above, ghosts) = refs[:6]
    refs = refs[6:]
    if stage == 1:
        low, high = low0, high0
    else:
        low, high, acc_low, acc_high = refs[:4]
        refs = refs[4:]
    if last:
        density_out, momentum_out, magnetic_out = refs[:3]
        refs = refs[3:]
    else:
        corner, rowmask = refs[:2]
        low_out, high_out, acc_low_out, acc_high_out, msg_out = refs[2:7]
        refs = refs[7:]
    slope, up, down = refs
    rad, ang = lax.axis_index("rad"), lax.axis_index("ang")
    rows_p, rows_t = low.shape[1:]
    width = rows_t + 128
    invs = [inverse_radius(rad, n_rad, slot, 2) for slot in range(2)]
    outward = jnp.where((rad & 1) == 0, jnp.float32(0.5), jnp.float32(-0.5))
    wall = (rad == 0) | (rad == n_rad - 1)
    ghost = ghosts[...]
    sine_row = sines[...]
    first, final = EDGE, rows_p - EDGE - 1
    half_row = iota((8, 128), 1) < 64
    r_pairs = ((0, 0), (0, 1), (0, 2))
    t_pairs = ((0, 1), (1, 1), (1, 2))
    for tile in range(rows_p // 8):
        rows = slice(8 * tile, 8 * tile + 8)
        both = [[ref[f, rows, :] for f in range(NF)] for ref in (low, high)]
        found, r_flux = [], []
        for cells in both:
            found.append(stresses(cells, *derived(cells), ALL_PAIRS))
            r_flux.append(flux_along(cells, found[-1], 0))
        for slot in range(2):
            cells, inner, inner_flux = both[slot], both[1 - slot], r_flux[1 - slot]
            outer = [(below if slot == 0 else above)[f, rows, :] for f in range(NF)]
            if slot == 1:
                outer = [jnp.where(wall, MIRROR[f] * cells[f], outer[f]) for f in range(NF)]
            outer_flux = flux_along(outer, stresses(outer, *derived(outer), r_pairs), 0)
            half_r = outward if slot == 0 else -outward
            inv = invs[slot]
            inv_sine = inv * sine_row
            half, spread = 0.5 * inv_sine, diffusion * inv_sine * inv_sine
            half_t, spread_t = 0.5 * inv, diffusion * inv * inv
            centre = 2.0 * diffusion + 2.0 * spread_t + 2.0 * spread
            rim = []
            for f in range(NF):
                at = 8 * slot + f
                lower = ghost[8 * tile : 8 * tile + 8, at : at + 1]
                upper = ghost[rows_p + 8 * tile : rows_p + 8 * tile + 8, at : at + 1]
                rim.append(jnp.where(half_row, upper, lower))
            rim_flux = flux_along(rim, stresses(rim, *derived(rim), t_pairs), 1)
            t_flux = flux_along(cells, found[slot], 1)
            p_flux = flux_along(cells, found[slot], 2)
            for f in range(NF):
                cell = cells[f] if f else None
                down[slot, f, rows, :], up[slot, f, rows, :] = given(p_flux[f], cell, half, spread)
                total = None
                if r_flux[slot][f][0]:
                    total = half_r * (inner_flux[f][1] - outer_flux[f][1])
                if f:
                    item = diffusion * (inner[f] + outer[f]) - centre * cell
                    total = item if total is None else total + item
                whole = (t_flux[f][0], None)
                if t_flux[f][0]:
                    whole = (t_flux[f][0], jnp.concatenate([t_flux[f][1], rim_flux[f][1]], axis=1))
                full = jnp.concatenate([cell, rim[f]], axis=1) if f else None
                to_upper, to_lower = given(whole, full, half_t, spread_t)
                total = total + pltpu.roll(to_upper, 1, axis=1)[:, :rows_t]
                slope[slot, f, rows, :] = total + pltpu.roll(to_lower, width - 1, axis=1)[:, :rows_t]

    @pl.when(ang == 0)
    def _():
        for slot in range(2):
            for f in range(NF):
                down[slot, f, first - 1 : first, :] = MIRROR[f] * up[slot, f, first : first + 1, :]

    @pl.when(ang == n_ang - 1)
    def _():
        for slot in range(2):
            for f in range(NF):
                up[slot, f, final + 1 : final + 2, :] = MIRROR[f] * down[slot, f, final : final + 1, :]

    for slot in range(2):
        start = low0 if slot == 0 else high0
        for f in range(NF):
            k = slope[slot, f] + pltpu.roll(down[slot, f], 1, axis=0)
            k = k + pltpu.roll(up[slot, f], rows_p - 1, axis=0)
            if last:
                level = 1 - (rad & 1) if slot == 0 else rad & 1
                acc = acc_low if slot == 0 else acc_high
                value = start[f] + (time_step / 6.0) * (acc[f] + k)
                value = pltpu.roll(value, rows_p - EDGE, axis=0)[: rows_p - 2 * EDGE]
                if f == 0:
                    density_out[0, level] = value
                elif f < 4:
                    momentum_out[0, f - 1, level] = value
                else:
                    magnetic_out[0, f - 4, level] = value
                continue
            acc_out = acc_low_out if slot == 0 else acc_high_out
            if stage == 1:
                acc_out[f] = k
            else:
                acc_out[f] = (acc_low if slot == 0 else acc_high)[f] + 2.0 * k
            step = time_step if stage == 3 else 0.5 * time_step
            (low_out if slot == 0 else high_out)[f] = start[f] + step * k
    if not last:
        new_low = low_out[...].reshape(NF * rows_p, rows_t)
        new_high = high_out[...].reshape(NF * rows_p, rows_t)
        answer_into(msg_out, new_low, new_high, corner[...], rowmask[...])


def body(
    density, momentum, magnetic, partner_device, partner_phi, partner_theta, partner_weight, border_turn
):
    _, rows_r, rows_p, rows_t = density.shape
    n_ang, n_rad = lax.axis_size("ang"), lax.axis_size("rad")
    f32 = jnp.float32
    vmem = pl.BlockSpec(memory_space=pltpu.VMEM)

    def shape(*dims, final=False, dtype=f32):
        return jax.ShapeDtypeStruct(dims, dtype) if final or INTERPRET else pltpu.VMEM(dims, dtype)

    def held(value):
        return value if INTERPRET else pltpu.with_memory_space_constraint(value, pltpu.VMEM)

    def call(kernel, ins, outs, scratch=(), plain=0):
        return pl.pallas_call(
            kernel,
            out_shape=outs,
            in_specs=[vmem] * len(ins),
            out_specs=[vmem] * len(outs),
            scratch_shapes=list(scratch),
            interpret=INTERPRET,
            compiler_params=pltpu.CompilerParams(vmem_limit_bytes=None if plain > 1 else 12 << 20),
        )(*[item if at < plain else held(item) for at, item in enumerate(ins)])

    wide = rows_p + 2 * EDGE
    own_level = shape(NF, rows_p, rows_t)
    level = shape(NF, wide, rows_t)
    edge = shape(NF + 1, 2 * EDGE, rows_t)
    message = shape(32, 1, 128)

    def exchanged(value, axis, step):
        return held(lax.ppermute(value, axis, partners(lax.axis_size(axis), step)))

    def crossed(value):
        swap = held(lax.ppermute(value, "panel", [(0, 1), (1, 0)]))
        return held(lax.all_to_all(swap, "ang", split_axis=0, concat_axis=0, tiled=True))

    theta = math.pi / 4 + (np.arange(rows_t) + 0.5) * (math.pi / 2 / rows_t)
    sines = jnp.asarray((1.0 / np.sin(theta)).astype(np.float32)).reshape(1, rows_t)

    low0, high0, first, final, ask, table, sines = call(
        open_kernel,
        [
            density, momentum, magnetic, jnp.swapaxes(partner_device, 1, 2), partner_phi, partner_theta,
            jnp.swapaxes(partner_weight, 1, 2), border_turn, sines,
        ],
        [own_level, own_level, edge, edge, message, shape(32, 128), shape(1, rows_t)],
        plain=9,
    )
    one = exchanged(first, "ang", 0)
    two = exchanged(final, "ang", 1)
    corner, rowmask, low0, high0, table, answer = call(
        asked_kernel,
        [crossed(ask), low0, high0, one, two, table],
        [shape(rows_t, 128, dtype=jnp.bfloat16), shape(wide, 128), level, level, shape(2 * wide, 128), message],
    )
    low, high, sums = low0, high0, []
    scratch = [pltpu.VMEM((2, NF, wide, rows_t), f32) for _ in range(3)]
    for stage in range(1, 5):
        below = exchanged(low, "rad", 0)
        above = exchanged(high, "rad", 1)
        (ghosts,) = call(ghost_kernel, [crossed(answer), table], [shape(2 * wide, 128)])
        ins = [sines, low0, high0, below, above, ghosts]
        if stage > 1:
            ins += [low, high, *sums]
        if stage < 4:
            ins += [corner, rowmask]
            outs = [level, level, level, level, message]
        else:
            outs = [
                shape(1, rows_r, rows_p, rows_t, final=True),
                shape(1, 3, rows_r, rows_p, rows_t, final=True),
                shape(1, 3, rows_r, rows_p, rows_t, final=True),
            ]

        def kernel(*refs, stage=stage):
            stage_kernel(stage, n_rad, n_ang, *refs)

        result = call(kernel, ins, outs, scratch)
        if stage == 4:
            return tuple(result)
        low, high, acc_low, acc_high, answer = result
        sums = [acc_low, acc_high]


def solution(mesh):
    in_specs = (
        P("panel", "rad", "ang", None),
        P("panel", None, "rad", "ang", None),
        P("panel", None, "rad", "ang", None),
        P("panel", "ang", None),
        P("panel", "ang"),
        P("panel", "ang"),
        P("panel", "ang", None),
        P("panel", "ang"),
    )
    out_specs = (
        P("panel", "rad", "ang", None),
        P("panel", None, "rad", "ang", None),
        P("panel", None, "rad", "ang", None),
    )
    return jax.shard_map(body, mesh=mesh, in_specs=in_specs, out_specs=out_specs, check_vma=False)
```

time: 109 us -> 103 us (0.945)
  starting transfers between devices: 15.5 us -> 12.8 us
  Pallas kernels: 14.1 us -> 12 us
  blocking collectives: 71.4 us -> 70.3 us
    ppermute x10, starting transfers between devices: 15.5 us -> 12.8 us  [exchanged(): return held(lax.ppermute(value, axis, partners(lax.axis_size(axis), step)))]
    pallas_call x10, Pallas kernels: 14.1 us -> 12 us  [call(): pl.pallas_call(kernel, out_shape=outs, in_specs=[vmem] * len(ins), out_sp...]
where the time goes in v5:
time: 103 us; the launch traced here: 102 us
  blocking collectives  70.3 us (68%)
  starting transfers between devices  12.8 us (12%)
  Pallas kernels  12 us (12%)
  waiting for transfers between devices  5.93 us (6%)
    all_to_all x5, blocking collectives, crossed(): lax.all_to_all(swap, 'ang', split_axis=0, concat_axis=0, tiled=True)  70.3 us
    ppermute x10, starting transfers between devices, exchanged(): return held(lax.ppermute(value, axis, partners(lax.axis_size(axis), step)))  12.8 us
    pallas_call x10, Pallas kernels, call(): pl.pallas_call(kernel, out_shape=outs, in_specs=[vmem] * len(ins), out_sp...  12 us
    ppermute x5, waiting for transfers between devices, crossed(): swap = held(lax.ppermute(value, 'panel', [(0, 1), (1, 0)]))  5.91 us
  transfers between devices with their start and end apart: 15, of which 5 were waited for; matrix products, arithmetic and copies ran while one was open for 0% of the time, Pallas kernels for 2%

profile of v5, /device:TPU:2, one launch (start us, length us, event | category | flops | bytes accessed | tf_op | source)
XLA Modules:
  0.0 101.9 jit_solution(3506732129896121666)
XLA Ops:
  0.6 1.5 %shard_map.112 = (f32[7,16,512]{2,1,0:T(8,128)S(1)}, f32[7,16,512]{2,1,0:T(8,128)S(1)}, f32[8,8,512]{2,1,0:T(8,128)S(1)}, f32[8,8,512]{2,1,0:T(8,128)S(1)}, f32[...) custom-call(f32[1,2,16,512]{3,2,1,0:T(8,128)} %density.1, f32[1,3,2,16,512]{4,3,2,1,0:T(8,128)} %momentum.1, ...), custom_call_target="tpu_custom_call" | custom-call | tf_op jit(solution)/shard_map/pallas_call | solution.py:381
  2.1 2.3 %collective-permute-start.1 = (f32[8,8,512]{2,1,0:T(8,128)S(1)}, f32[8,8,512]{2,1,0:T(8,128)S(1)}, u32[]{:S(2)}, u32[]{:S(2)}) collective-permute-start(f32[8,8,512]{2,1,0:T(8,128)S(1)} %get-tuple-element.35), channel_id=1, source_target_pairs={{0,4},{4,0},{8,12},{12,8},{16,20},{20,16},{24,28},{28,24},{32,36},... | collective-permute-start | bytes 393224 | tf_op jit(solution)/shard_map/ppermute | solution.py:398
  4.4 0.4 collective-permute-start.2
  4.9 0.0 collective-permute-start
  4.9 1.2 %collective-permute-done = f32[32,1,128]{2,1,0:T(1,128)S(1)} collective-permute-done((f32[32,1,128]{2,1,0:T(1,128)S(1)}, f32[32,1,128]{2,1,0:T(1,128)S(1)}, u32[]{:S(2)}, u32[]{:S(2)}) %collective-permute-start) | collective-permute-done | bytes 16416 | tf_op jit(solution)/shard_map/ppermute | solution.py:401
  6.1 19.4 %all_to_all.25.asked_ref = f32[32,1,128]{2,1,0:T(1,128)S(1)} all-to-all(f32[32,1,128]{2,1,0:T(1,128)S(1)} %collective-permute-done), channel_id=1, replica_groups=mesh['panel'=2,'ang'=32,'rad'=4] {'ang'}, dimensions={0} | all-to-all | bytes 32768 | tf_op jit(solution)/shard_map/all_to_all | solution.py:402
  25.5 1.1 %shard_map.113 = (bf16[512,128]{1,0:T(8,128)(2,1)S(1)}, f32[24,128]{1,0:T(8,128)S(1)}, f32[7,24,512]{2,1,0:T(8,128)S(1)}, f32[7,24,512]{2,1,0:T(8,128)S(1)}, f32...) custom-call(f32[32,1,128]{2,1,0:T(1,128)S(1)} %all_to_all.25.asked_ref, f32[7,16,512]{2,1,0:T(8,128)S(1)} %get-tuple-element.33.low_ref, ...), custom_call_target="tpu_custom_call" | custom-call | tf_op jit(solution)/shard_map/pallas_call | solution.py:381
  26.6 1.7 %collective-permute-start.3 = (f32[7,24,512]{2,1,0:T(8,128)S(1)}, f32[7,24,512]{2,1,0:T(8,128)S(1)}, u32[]{:S(2)}, u32[]{:S(2)}) collective-permute-start(f32[7,24,512]{2,1,0:T(8,128)S(1)} %get-tuple-element.38.refs_1_), channel_id=1, source_target_pairs={{0,1},{1,0},{2,3},{3,2},{4,5},{5,4},{6,7},{7,6},{8,9},{9,8},{10,11... | collective-permute-start | bytes 1032200 | tf_op jit(solution)/shard_map/ppermute | solution.py:398
  28.3 2.2 %collective-permute-start.4 = (f32[7,24,512]{2,1,0:T(8,128)S(1)}, f32[7,24,512]{2,1,0:T(8,128)S(1)}, u32[]{:S(2)}, u32[]{:S(2)}) collective-permute-start(f32[7,24,512]{2,1,0:T(8,128)S(1)} %get-tuple-element.39.refs_2_), channel_id=1, source_target_pairs={{0,3},{1,2},{2,1},{3,0},{4,7},{5,6},{6,5},{7,4},{8,11},{9,10},{10,... | collective-permute-start | bytes 1032200 | tf_op jit(solution)/shard_map/ppermute | solution.py:398
  30.4 1.2 %collective-permute-done.5 = f32[32,1,128]{2,1,0:T(1,128)S(1)} collective-permute-done((f32[32,1,128]{2,1,0:T(1,128)S(1)}, f32[32,1,128]{2,1,0:T(1,128)S(1)}, u32[]{:S(2)}, u32[]{:S(2)}) %collective-permute-start.5) | collective-permute-done | bytes 16416 | tf_op jit(solution)/shard_map/ppermute | solution.py:401
  31.6 12.7 %all_to_all.26.reply = f32[32,1,128]{2,1,0:T(1,128)S(1)} all-to-all(f32[32,1,128]{2,1,0:T(1,128)S(1)} %collective-permute-done.5), channel_id=1, replica_groups=mesh['panel'=2,'ang'=32,'rad'=4] {'ang'}, dimensions={0} | all-to-all | bytes 32768 | tf_op jit(solution)/shard_map/all_to_all | solution.py:402
  44.3 0.4 shard_map.114.refs_5_
  44.8 1.9 %shard_map.115 = (f32[7,24,512]{2,1,0:T(8,128)S(1)}, f32[7,24,512]{2,1,0:T(8,128)S(1)}, f32[7,24,512]{2,1,0:T(8,128)S(1)}, f32[7,24,512]{2,1,0:T(8,128)S(1)}, f32[32,1,128]{2,1,0:T(1,128)S(1)}) custom-call(f32[1,512]{1,0:T(1,128)S(1)} %get-tuple-element.31.refs_0_, f32[7,24,512]{2,1,0:T(8,128)S(1)} %get-tuple-element.38.refs_1_, ...), custom_call_target="tpu_custom_call" | custom-call | tf_op jit(solution)/shard_map/pallas_call | solution.py:381
  46.7 0.8 collective-permute-start.6
  47.5 0.6 collective-permute-start.7
  48.1 1.2 %collective-permute-done.8 = f32[32,1,128]{2,1,0:T(1,128)S(1)} collective-permute-done((f32[32,1,128]{2,1,0:T(1,128)S(1)}, f32[32,1,128]{2,1,0:T(1,128)S(1)}, u32[]{:S(2)}, u32[]{:S(2)}) %collective-permute-start.8) | collective-permute-done | bytes 16416 | tf_op jit(solution)/shard_map/ppermute | solution.py:401
  49.3 12.7 %all_to_all.27.reply = f32[32,1,128]{2,1,0:T(1,128)S(1)} all-to-all(f32[32,1,128]{2,1,0:T(1,128)S(1)} %collective-permute-done.8), channel_id=1, replica_groups=mesh['panel'=2,'ang'=32,'rad'=4] {'ang'}, dimensions={0} | all-to-all | bytes 32768 | tf_op jit(solution)/shard_map/all_to_all | solution.py:402
  62.0 0.4 shard_map.116.refs_5_
  62.5 2.0 %shard_map.117 = (f32[7,24,512]{2,1,0:T(8,128)S(1)}, f32[7,24,512]{2,1,0:T(8,128)S(1)}, f32[7,24,512]{2,1,0:T(8,128)S(1)}, f32[7,24,512]{2,1,0:T(8,128)S(1)}, f32[32,1,128]{2,1,0:T(1,128)S(1)}) custom-call(f32[1,512]{1,0:T(1,128)S(1)} %get-tuple-element.31.refs_0_, f32[7,24,512]{2,1,0:T(8,128)S(1)} %get-tuple-element.38.refs_1_, ...), custom_call_target="tpu_custom_call" | custom-call | tf_op jit(solution)/shard_map/pallas_call | solution.py:381
  64.4 1.3 %collective-permute-start.9 = (f32[7,24,512]{2,1,0:T(8,128)S(1)}, f32[7,24,512]{2,1,0:T(8,128)S(1)}, u32[]{:S(2)}, u32[]{:S(2)}) collective-permute-start(f32[7,24,512]{2,1,0:T(8,128)S(1)} %get-tuple-element.49.refs_6_), channel_id=1, source_target_pairs={{0,1},{1,0},{2,3},{3,2},{4,5},{5,4},{6,7},{7,6},{8,9},{9,8},{10,11... | collective-permute-start | bytes 1032200 | tf_op jit(solution)/shard_map/ppermute | solution.py:398
  65.7 2.2 %collective-permute-start.10 = (f32[7,24,512]{2,1,0:T(8,128)S(1)}, f32[7,24,512]{2,1,0:T(8,128)S(1)}, u32[]{:S(2)}, u32[]{:S(2)}) collective-permute-start(f32[7,24,512]{2,1,0:T(8,128)S(1)} %get-tuple-element.50.refs_7_), channel_id=1, source_target_pairs={{0,3},{1,2},{2,1},{3,0},{4,7},{5,6},{6,5},{7,4},{8,11},{9,10},{10,... | collective-permute-start | bytes 1032200 | tf_op jit(solution)/shard_map/ppermute | solution.py:398
  67.9 0.0 collective-permute-start.11
  67.9 1.2 %collective-permute-done.11 = f32[32,1,128]{2,1,0:T(1,128)S(1)} collective-permute-done((f32[32,1,128]{2,1,0:T(1,128)S(1)}, f32[32,1,128]{2,1,0:T(1,128)S(1)}, u32[]{:S(2)}, u32[]{:S(2)}) %collective-permute-start.11) | collective-permute-done | bytes 16416 | tf_op jit(solution)/shard_map/ppermute | solution.py:401
  69.1 12.7 %all_to_all.28.reply = f32[32,1,128]{2,1,0:T(1,128)S(1)} all-to-all(f32[32,1,128]{2,1,0:T(1,128)S(1)} %collective-permute-done.11), channel_id=1, replica_groups=mesh['panel'=2,'ang'=32,'rad'=4] {'ang'}, dimensions={0} | all-to-all | bytes 32768 | tf_op jit(solution)/shard_map/all_to_all | solution.py:402
  81.8 0.4 shard_map.118.refs_5_
  82.3 1.9 %shard_map.119 = (f32[7,24,512]{2,1,0:T(8,128)S(1)}, f32[7,24,512]{2,1,0:T(8,128)S(1)}, f32[7,24,512]{2,1,0:T(8,128)S(1)}, f32[7,24,512]{2,1,0:T(8,128)S(1)}, f32[32,1,128]{2,1,0:T(1,128)S(1)}) custom-call(f32[1,512]{1,0:T(1,128)S(1)} %get-tuple-element.31.refs_0_, f32[7,24,512]{2,1,0:T(8,128)S(1)} %get-tuple-element.38.refs_1_, ...), custom_call_target="tpu_custom_call" | custom-call | tf_op jit(solution)/shard_map/pallas_call | solution.py:381
  84.2 0.8 collective-permute-start.12
  85.0 0.6 collective-permute-start.13
  85.6 1.2 %collective-permute-done.14 = f32[32,1,128]{2,1,0:T(1,128)S(1)} collective-permute-done((f32[32,1,128]{2,1,0:T(1,128)S(1)}, f32[32,1,128]{2,1,0:T(1,128)S(1)}, u32[]{:S(2)}, u32[]{:S(2)}) %collective-permute-start.14) | collective-permute-done | bytes 16416 | tf_op jit(solution)/shard_map/ppermute | solution.py:401
  86.8 12.7 %all_to_all.29.reply = f32[32,1,128]{2,1,0:T(1,128)S(1)} all-to-all(f32[32,1,128]{2,1,0:T(1,128)S(1)} %collective-permute-done.14), channel_id=1, replica_groups=mesh['panel'=2,'ang'=32,'rad'=4] {'ang'}, dimensions={0} | all-to-all | bytes 32768 | tf_op jit(solution)/shard_map/all_to_all | solution.py:402
  99.5 0.4 shard_map.120.refs_5_
  100.0 1.9 %shard_map.121 = (f32[1,2,16,512]{3,2,1,0:T(8,128)}, f32[1,3,2,16,512]{4,3,2,1,0:T(8,128)}, f32[1,3,2,16,512]{4,3,2,1,0:T(8,128)}) custom-call(f32[1,512]{1,0:T(1,128)S(1)} %get-tuple-element.31.refs_0_, f32[7,24,512]{2,1,0:T(8,128)S(1)} %get-tuple-element.38.refs_1_, f32[7,24,512]{2,1,0:T(8,128)S(1)} %get-tuple-element.39.refs_2_, ...), custom_call_target="tpu_custom_call" | custom-call | tf_op jit(solution)/shard_map/pallas_call | solution.py:381
  (13 shorter events, 0.0 us)
Async XLA Ops:
  2.1 23.4 %collective-permute-start.1 = (f32[8,8,512]{2,1,0:T(8,128)S(1)}, f32[8,8,512]{2,1,0:T(8,128)S(1)}, u32[]{:S(2)}, u32[]{:S(2)}) collective-permute-start(f32[8,8,512]{2,1,0:T(8,128)S(1)} %get-tuple-element.35), channel_id=1, source_target_pairs={{0,4},{4,0},{8,12},{12,8},{16,20},{20,16},{24,28},{28,24},{32,36},... | collective-permute-start | bytes 393224 | tf_op jit(solution)/shard_map/ppermute | solution.py:398
  4.4 21.1 %collective-permute-start.2 = (f32[8,8,512]{2,1,0:T(8,128)S(1)}, f32[8,8,512]{2,1,0:T(8,128)S(1)}, u32[]{:S(2)}, u32[]{:S(2)}) collective-permute-start(f32[8,8,512]{2,1,0:T(8,128)S(1)} %get-tuple-element.36), channel_id=1, source_target_pairs={{0,124},{4,8},{8,4},{12,16},{16,12},{20,24},{24,20},{28,32},{32,28... | collective-permute-start | bytes 393224 | tf_op jit(solution)/shard_map/ppermute | solution.py:398
  4.9 1.2 %collective-permute-start = (f32[32,1,128]{2,1,0:T(1,128)S(1)}, f32[32,1,128]{2,1,0:T(1,128)S(1)}, u32[]{:S(2)}, u32[]{:S(2)}) collective-permute-start(f32[32,1,128]{2,1,0:T(1,128)S(1)} %get-tuple-element.32), channel_id=1, source_target_pairs={{0,128},{128,0},{1,129},{129,1},{2,130},{130,2},{3,131},{131,3},{4... | collective-permute-start | bytes 49160 | tf_op jit(solution)/shard_map/ppermute | solution.py:401
  26.6 18.2 %collective-permute-start.3 = (f32[7,24,512]{2,1,0:T(8,128)S(1)}, f32[7,24,512]{2,1,0:T(8,128)S(1)}, u32[]{:S(2)}, u32[]{:S(2)}) collective-permute-start(f32[7,24,512]{2,1,0:T(8,128)S(1)} %get-tuple-element.38.refs_1_), channel_id=1, source_target_pairs={{0,1},{1,0},{2,3},{3,2},{4,5},{5,4},{6,7},{7,6},{8,9},{9,8},{10,11... | collective-permute-start | bytes 1032200 | tf_op jit(solution)/shard_map/ppermute | solution.py:398
  28.3 16.5 %collective-permute-start.4 = (f32[7,24,512]{2,1,0:T(8,128)S(1)}, f32[7,24,512]{2,1,0:T(8,128)S(1)}, u32[]{:S(2)}, u32[]{:S(2)}) collective-permute-start(f32[7,24,512]{2,1,0:T(8,128)S(1)} %get-tuple-element.39.refs_2_), channel_id=1, source_target_pairs={{0,3},{1,2},{2,1},{3,0},{4,7},{5,6},{6,5},{7,4},{8,11},{9,10},{10,... | collective-permute-start | bytes 1032200 | tf_op jit(solution)/shard_map/ppermute | solution.py:398
  30.4 1.2 %collective-permute-start.5 = (f32[32,1,128]{2,1,0:T(1,128)S(1)}, f32[32,1,128]{2,1,0:T(1,128)S(1)}, u32[]{:S(2)}, u32[]{:S(2)}) collective-permute-start(f32[32,1,128]{2,1,0:T(1,128)S(1)} %get-tuple-element.40), channel_id=1, source_target_pairs={{0,128},{128,0},{1,129},{129,1},{2,130},{130,2},{3,131},{131,3},{4... | collective-permute-start | bytes 49160 | tf_op jit(solution)/shard_map/ppermute | solution.py:401
  46.7 15.7 %collective-permute-start.6 = (f32[7,24,512]{2,1,0:T(8,128)S(1)}, f32[7,24,512]{2,1,0:T(8,128)S(1)}, u32[]{:S(2)}, u32[]{:S(2)}) collective-permute-start(f32[7,24,512]{2,1,0:T(8,128)S(1)} %get-tuple-element.44.refs_6_), channel_id=1, source_target_pairs={{0,1},{1,0},{2,3},{3,2},{4,5},{5,4},{6,7},{7,6},{8,9},{9,8},{10,11... | collective-permute-start | bytes 1032200 | tf_op jit(solution)/shard_map/ppermute | solution.py:398
  47.5 15.0 %collective-permute-start.7 = (f32[7,24,512]{2,1,0:T(8,128)S(1)}, f32[7,24,512]{2,1,0:T(8,128)S(1)}, u32[]{:S(2)}, u32[]{:S(2)}) collective-permute-start(f32[7,24,512]{2,1,0:T(8,128)S(1)} %get-tuple-element.45.refs_7_), channel_id=1, source_target_pairs={{0,3},{1,2},{2,1},{3,0},{4,7},{5,6},{6,5},{7,4},{8,11},{9,10},{10,... | collective-permute-start | bytes 1032200 | tf_op jit(solution)/shard_map/ppermute | solution.py:398
  48.1 1.2 %collective-permute-start.8 = (f32[32,1,128]{2,1,0:T(1,128)S(1)}, f32[32,1,128]{2,1,0:T(1,128)S(1)}, u32[]{:S(2)}, u32[]{:S(2)}) collective-permute-start(f32[32,1,128]{2,1,0:T(1,128)S(1)} %get-tuple-element.46), channel_id=1, source_target_pairs={{0,128},{128,0},{1,129},{129,1},{2,130},{130,2},{3,131},{131,3},{4... | collective-permute-start | bytes 49160 | tf_op jit(solution)/shard_map/ppermute | solution.py:401
  64.4 17.8 %collective-permute-start.9 = (f32[7,24,512]{2,1,0:T(8,128)S(1)}, f32[7,24,512]{2,1,0:T(8,128)S(1)}, u32[]{:S(2)}, u32[]{:S(2)}) collective-permute-start(f32[7,24,512]{2,1,0:T(8,128)S(1)} %get-tuple-element.49.refs_6_), channel_id=1, source_target_pairs={{0,1},{1,0},{2,3},{3,2},{4,5},{5,4},{6,7},{7,6},{8,9},{9,8},{10,11... | collective-permute-start | bytes 1032200 | tf_op jit(solution)/shard_map/ppermute | solution.py:398
  65.7 16.5 %collective-permute-start.10 = (f32[7,24,512]{2,1,0:T(8,128)S(1)}, f32[7,24,512]{2,1,0:T(8,128)S(1)}, u32[]{:S(2)}, u32[]{:S(2)}) collective-permute-start(f32[7,24,512]{2,1,0:T(8,128)S(1)} %get-tuple-element.50.refs_7_), channel_id=1, source_target_pairs={{0,3},{1,2},{2,1},{3,0},{4,7},{5,6},{6,5},{7,4},{8,11},{9,10},{10,... | collective-permute-start | bytes 1032200 | tf_op jit(solution)/shard_map/ppermute | solution.py:398
  67.9 1.2 %collective-permute-start.11 = (f32[32,1,128]{2,1,0:T(1,128)S(1)}, f32[32,1,128]{2,1,0:T(1,128)S(1)}, u32[]{:S(2)}, u32[]{:S(2)}) collective-permute-start(f32[32,1,128]{2,1,0:T(1,128)S(1)} %get-tuple-element.51), channel_id=1, source_target_pairs={{0,128},{128,0},{1,129},{129,1},{2,130},{130,2},{3,131},{131,3},{4... | collective-permute-start | bytes 49160 | tf_op jit(solution)/shard_map/ppermute | solution.py:401
  84.2 15.7 %collective-permute-start.12 = (f32[7,24,512]{2,1,0:T(8,128)S(1)}, f32[7,24,512]{2,1,0:T(8,128)S(1)}, u32[]{:S(2)}, u32[]{:S(2)}) collective-permute-start(f32[7,24,512]{2,1,0:T(8,128)S(1)} %get-tuple-element.54.refs_6_), channel_id=1, source_target_pairs={{0,1},{1,0},{2,3},{3,2},{4,5},{5,4},{6,7},{7,6},{8,9},{9,8},{10,11... | collective-permute-start | bytes 1032200 | tf_op jit(solution)/shard_map/ppermute | solution.py:398
  85.0 15.0 %collective-permute-start.13 = (f32[7,24,512]{2,1,0:T(8,128)S(1)}, f32[7,24,512]{2,1,0:T(8,128)S(1)}, u32[]{:S(2)}, u32[]{:S(2)}) collective-permute-start(f32[7,24,512]{2,1,0:T(8,128)S(1)} %get-tuple-element.55.refs_7_), channel_id=1, source_target_pairs={{0,3},{1,2},{2,1},{3,0},{4,7},{5,6},{6,5},{7,4},{8,11},{9,10},{10,... | collective-permute-start | bytes 1032200 | tf_op jit(solution)/shard_map/ppermute | solution.py:398
  85.6 1.2 %collective-permute-start.14 = (f32[32,1,128]{2,1,0:T(1,128)S(1)}, f32[32,1,128]{2,1,0:T(1,128)S(1)}, u32[]{:S(2)}, u32[]{:S(2)}) collective-permute-start(f32[32,1,128]{2,1,0:T(1,128)S(1)} %get-tuple-element.56), channel_id=1, source_target_pairs={{0,128},{128,0},{1,129},{129,1},{2,130},{130,2},{3,131},{131,3},{4... | collective-permute-start | bytes 49160 | tf_op jit(solution)/shard_map/ppermute | solution.py:401

commit v6 on v5

--- a/solution.py
+++ b/solution.py
@@ -89,23 +89,32 @@
     return [(i, (i ^ 1) if step == 0 else (((i + 1) ^ 1) - 1) % size) for i in range(size)]
 
 
-def answer_into(msg_ref, low, high, corner, rowmask):
-    cells = jnp.concatenate([low, high], axis=0)
-    product = None
-    for _ in range(3):
-        part = cells.astype(jnp.bfloat16)
-        cells = cells - part.astype(jnp.float32)
-        item = jnp.dot(part, corner, preferred_element_type=jnp.float32)
-        product = item if product is None else product + item
-    product = product.reshape(2, NF, rowmask.shape[0], 128)
-    picked = jnp.sum(jnp.where(rowmask != 0.0, product * rowmask, 0.0), axis=2)
+def answer_part(cells, lanes, rowmask):
+    at, tile = lanes & 127, lanes >> 7
+    out = []
+    for field in cells:
+        total = None
+        for row in range(0, rowmask.shape[0], 8):
+            found = None
+            for q in range(field.shape[1] // 128):
+                item = jnp.take_along_axis(
+                    field[row : row + 8, 128 * q : 128 * q + 128], at, axis=1, mode="promise_in_bounds"
+                )
+                found = item if found is None else jnp.where(tile == q, item, found)
+            found = found * rowmask[row : row + 8, :]
+            total = found if total is None else total + found
+        out.append(jnp.sum(total, axis=0, keepdims=True))
+    return out
+
+
+def answer_into(msg_ref, picked):
     gap = jnp.zeros((1, 128), jnp.float32)
-    parts = [picked[0], gap, picked[1], gap]
+    parts = [*picked[0], gap, *picked[1], gap]
     both = jnp.concatenate(parts, axis=0)
     both = both + pltpu.roll(both, 64, axis=1)
     turned = both.T
-    lanes = jnp.concatenate([turned, jnp.zeros((128, 128 - SLOT), jnp.float32)], axis=1)
-    own = lanes[0:32] + pltpu.roll(lanes[32:64], SLOT, axis=1)
+    turned = jnp.concatenate([turned, jnp.zeros((128, 128 - SLOT), jnp.float32)], axis=1)
+    own = turned[0:32] + pltpu.roll(turned[32:64], SLOT, axis=1)
     before = pltpu.roll(pltpu.roll(own, 1, axis=0), 2 * SLOT, axis=1)
     after = pltpu.roll(pltpu.roll(own, 31, axis=0), 4 * SLOT, axis=1)
     msg_ref[...] = (own + before + after).reshape(msg_ref.shape)
@@ -177,7 +186,7 @@
 
 def asked_kernel(
     asked_ref, low_ref, high_ref, one_ref, two_ref, table_ref,
-    corner_ref, mask_ref, low_out, high_out, table_out, msg_ref,
+    lanes_ref, mask_ref, low_out, high_out, table_out, msg_ref,
 ):
     own_rows = low_ref.shape[1]
     even_ang = (lax.axis_index("ang") & 1) == 0
@@ -190,13 +199,13 @@
         rows = slice(EDGE * level, EDGE * level + EDGE)
         for f in range(NF):
             before, after = beside(f, rows, ref.shape[2])
-            out[f] = jnp.concatenate([before, ref[f], after], axis=0)
+            out[f] = jnp.concatenate([ref[f], after, before], axis=0)
     pieces = []
     for side in range(2):
         rows = slice(EDGE * side, EDGE * side + EDGE)
         half = own_rows * side
         before, after = beside(NF, rows, 128)
-        pieces += [before, table_ref[half : half + own_rows, :], after]
+        pieces += [table_ref[half : half + own_rows, :], after, before]
     table_out[...] = jnp.concatenate(pieces, axis=0)
     asked = asked_ref[...].reshape(32, 128)
     lane, sub = iota((32, 128), 1), iota((32, 128), 0)
@@ -209,20 +218,20 @@
             total = jnp.where(lane == sub + 32 * part, col, total)
         return jnp.sum(total, axis=0, keepdims=True)
 
-    phi_row = row_of((0, 0)).astype(jnp.int32) + EDGE
+    phi_row = row_of((0, 0)).astype(jnp.int32)
     theta_row = row_of((1, 1)).astype(jnp.int32) + jnp.where(iota((1, 128), 1) < 64, 0, 1)
     near = row_of((2, 3))
     far = row_of((4, 5))
-    corner = jnp.where(iota((corner_ref.shape[0], 128), 0) == theta_row, 1.0, 0.0).astype(jnp.bfloat16)
-    corner_ref[...] = corner
+    lanes = jnp.broadcast_to(theta_row, (8, 128))
+    lanes_ref[...] = lanes
     rows_p = mask_ref.shape[0]
     at = iota((rows_p, 128), 0)
     mask = jnp.where(at == phi_row, near, jnp.where(at == phi_row + 1, far, 0.0))
     mask_ref[...] = mask
-    rows_t = low_ref.shape[2]
-    low = low_out[...].reshape(NF * rows_p, rows_t)
-    high = high_out[...].reshape(NF * rows_p, rows_t)
-    answer_into(msg_ref, low, high, corner, mask)
+    answer_into(
+        msg_ref,
+        [answer_part([ref[f] for f in range(NF)], lanes, mask) for ref in (low_ref, high_ref)],
+    )
 
 
 def ghost_kernel(reply, table, out_ref):
@@ -237,7 +246,7 @@
     row = jnp.where(row < half, row, row - half)
     before = pltpu.roll(ghost, 128 - 2 * SLOT, axis=1)
     after = pltpu.roll(ghost, 128 - 4 * SLOT, axis=1)
-    ghost = jnp.where(row < EDGE, before, jnp.where(row < half - EDGE, ghost, after))
+    ghost = jnp.where(row < half - 2 * EDGE, ghost, jnp.where(row < half - EDGE, after, before))
     cosine, sine = picks[:, 64:65], picks[:, 65:66]
     lane = iota((rows, 128), 1) & 7
     is_t = (lane == 2) | (lane == 5)
@@ -260,7 +269,7 @@
         density_out, momentum_out, magnetic_out = refs[:3]
         refs = refs[3:]
     else:
-        corner, rowmask = refs[:2]
+        lanes, rowmask = refs[:2]
         low_out, high_out, acc_low_out, acc_high_out, msg_out = refs[2:7]
         refs = refs[7:]
     slope, up, down = refs
@@ -272,13 +281,24 @@
     wall = (rad == 0) | (rad == n_rad - 1)
     ghost = ghosts[...]
     sine_row = sines[...]
-    first, final = EDGE, rows_p - EDGE - 1
+    own = rows_p - 2 * EDGE
     half_row = iota((8, 128), 1) < 64
     r_pairs = ((0, 0), (0, 1), (0, 2))
     t_pairs = ((0, 1), (1, 1), (1, 2))
+    p_pairs = ((0, 2), (1, 2), (2, 2))
     for tile in range(rows_p // 8):
         rows = slice(8 * tile, 8 * tile + 8)
         both = [[ref[f, rows, :] for f in range(NF)] for ref in (low, high)]
+        if last and 8 * tile >= own:
+            for slot in range(2):
+                cells = both[slot]
+                inv_sine = invs[slot] * sine_row
+                half, spread = 0.5 * inv_sine, diffusion * inv_sine * inv_sine
+                p_flux = flux_along(cells, stresses(cells, *derived(cells), p_pairs), 2)
+                for f in range(NF):
+                    cell = cells[f] if f else None
+                    down[slot, f, rows, :], up[slot, f, rows, :] = given(p_flux[f], cell, half, spread)
+            continue
         found, r_flux = [], []
         for cells in both:
             found.append(stresses(cells, *derived(cells), ALL_PAIRS))
@@ -325,24 +345,26 @@
     def _():
         for slot in range(2):
             for f in range(NF):
-                down[slot, f, first - 1 : first, :] = MIRROR[f] * up[slot, f, first : first + 1, :]
+                down[slot, f, rows_p - 1 :, :] = MIRROR[f] * up[slot, f, 0:1, :]
 
     @pl.when(ang == n_ang - 1)
     def _():
         for slot in range(2):
             for f in range(NF):
-                up[slot, f, final + 1 : final + 2, :] = MIRROR[f] * down[slot, f, final : final + 1, :]
-
+                up[slot, f, own : own + 1, :] = MIRROR[f] * down[slot, f, own - 1 : own, :]
+
+    picked = []
+    used = own if last else rows_p
     for slot in range(2):
         start = low0 if slot == 0 else high0
+        values = []
         for f in range(NF):
-            k = slope[slot, f] + pltpu.roll(down[slot, f], 1, axis=0)
-            k = k + pltpu.roll(up[slot, f], rows_p - 1, axis=0)
+            k = slope[slot, f, :used] + pltpu.roll(down[slot, f], 1, axis=0)[:used]
+            k = k + pltpu.roll(up[slot, f], rows_p - 1, axis=0)[:used]
             if last:
                 level = 1 - (rad & 1) if slot == 0 else rad & 1
                 acc = acc_low if slot == 0 else acc_high
-                value = start[f] + (time_step / 6.0) * (acc[f] + k)
-                value = pltpu.roll(value, rows_p - EDGE, axis=0)[: rows_p - 2 * EDGE]
+                value = start[f, :own] + (time_step / 6.0) * (acc[f] + k)
                 if f == 0:
                     density_out[0, level] = value
                 elif f < 4:
@@ -352,15 +374,17 @@
                 continue
             acc_out = acc_low_out if slot == 0 else acc_high_out
             if stage == 1:
-                acc_out[f] = k
+                acc_out[f] = k[:own]
             else:
-                acc_out[f] = (acc_low if slot == 0 else acc_high)[f] + 2.0 * k
+                acc_out[f] = (acc_low if slot == 0 else acc_high)[f] + 2.0 * k[:own]
             step = time_step if stage == 3 else 0.5 * time_step
-            (low_out if slot == 0 else high_out)[f] = start[f] + step * k
+            value = start[f] + step * k
+            (low_out if slot == 0 else high_out)[f] = value
+            values.append(value[:own])
+        if not last:
+            picked.append(answer_part(values, lanes[...], rowmask[...]))
     if not last:
-        new_low = low_out[...].reshape(NF * rows_p, rows_t)
-        new_high = high_out[...].reshape(NF * rows_p, rows_t)
-        answer_into(msg_out, new_low, new_high, corner[...], rowmask[...])
+        answer_into(msg_out, picked)
 
 
 def body(
@@ -415,10 +439,10 @@
     )
     one = exchanged(first, "ang", 0)
     two = exchanged(final, "ang", 1)
-    corner, rowmask, low0, high0, table, answer = call(
+    lanes, rowmask, low0, high0, table, answer = call(
         asked_kernel,
         [crossed(ask), low0, high0, one, two, table],
-        [shape(rows_t, 128, dtype=jnp.bfloat16), shape(wide, 128), level, level, shape(2 * wide, 128), message],
+        [shape(8, 128, dtype=jnp.int32), shape(rows_p, 128), level, level, shape(2 * wide, 128), message],
     )
     low, high, sums = low0, high0, []
     scratch = [pltpu.VMEM((2, NF, wide, rows_t), f32) for _ in range(3)]
@@ -430,8 +454,8 @@
         if stage > 1:
             ins += [low, high, *sums]
         if stage < 4:
-            ins += [corner, rowmask]
-            outs = [level, level, level, level, message]
+            ins += [lanes, rowmask]
+            outs = [level, level, own_level, own_level, message]
         else:
             outs = [
                 shape(1, rows_r, rows_p, rows_t, final=True),

time: 103 us -> 102 us (level)
  Pallas kernels: 12 us -> 10.6 us
    pallas_call x10, Pallas kernels: 12 us -> 10.6 us  [call(): pl.pallas_call(kernel, out_shape=outs, in_specs=[vmem] * len(ins), out_sp...]
where the time goes in v6:
time: 102 us; the launch traced here: 100 us
  blocking collectives  70.3 us (69%)
  starting transfers between devices  12.8 us (13%)
  Pallas kernels  10.6 us (10%)
  waiting for transfers between devices  5.94 us (6%)
    all_to_all x5, blocking collectives, crossed(): lax.all_to_all(swap, 'ang', split_axis=0, concat_axis=0, tiled=True)  70.3 us
    ppermute x10, starting transfers between devices, exchanged(): return held(lax.ppermute(value, axis, partners(lax.axis_size(axis), step)))  12.8 us
    pallas_call x10, Pallas kernels, call(): pl.pallas_call(kernel, out_shape=outs, in_specs=[vmem] * len(ins), out_sp...  10.6 us
    ppermute x5, waiting for transfers between devices, crossed(): swap = held(lax.ppermute(value, 'panel', [(0, 1), (1, 0)]))  5.91 us
  transfers between devices with their start and end apart: 15, of which 5 were waited for; matrix products, arithmetic and copies ran while one was open for 0% of the time, Pallas kernels for 2%

profile of v6, /device:TPU:2, one launch (start us, length us, event | category | flops | bytes accessed | tf_op | source)
XLA Modules:
  0.0 100.4 jit_solution(15327007953916752708)
XLA Ops:
  0.6 1.5 %shard_map.112 = (f32[7,16,512]{2,1,0:T(8,128)S(1)}, f32[7,16,512]{2,1,0:T(8,128)S(1)}, f32[8,8,512]{2,1,0:T(8,128)S(1)}, f32[8,8,512]{2,1,0:T(8,128)S(1)}, f32[...) custom-call(f32[1,2,16,512]{3,2,1,0:T(8,128)} %density.1, f32[1,3,2,16,512]{4,3,2,1,0:T(8,128)} %momentum.1, ...), custom_call_target="tpu_custom_call" | custom-call | tf_op jit(solution)/shard_map/pallas_call | solution.py:405
  2.1 2.3 %collective-permute-start.1 = (f32[8,8,512]{2,1,0:T(8,128)S(1)}, f32[8,8,512]{2,1,0:T(8,128)S(1)}, u32[]{:S(2)}, u32[]{:S(2)}) collective-permute-start(f32[8,8,512]{2,1,0:T(8,128)S(1)} %get-tuple-element.35), channel_id=1, source_target_pairs={{0,4},{4,0},{8,12},{12,8},{16,20},{20,16},{24,28},{28,24},{32,36},... | collective-permute-start | bytes 393224 | tf_op jit(solution)/shard_map/ppermute | solution.py:422
  4.4 0.4 collective-permute-start.2
  4.9 1.2 %collective-permute-done = f32[32,1,128]{2,1,0:T(1,128)S(1)} collective-permute-done((f32[32,1,128]{2,1,0:T(1,128)S(1)}, f32[32,1,128]{2,1,0:T(1,128)S(1)}, u32[]{:S(2)}, u32[]{:S(2)}) %collective-permute-start) | collective-permute-done | bytes 16416 | tf_op jit(solution)/shard_map/ppermute | solution.py:425
  6.1 19.4 %all_to_all.25.asked_ref = f32[32,1,128]{2,1,0:T(1,128)S(1)} all-to-all(f32[32,1,128]{2,1,0:T(1,128)S(1)} %collective-permute-done), channel_id=1, replica_groups=mesh['panel'=2,'ang'=32,'rad'=4] {'ang'}, dimensions={0} | all-to-all | bytes 32768 | tf_op jit(solution)/shard_map/all_to_all | solution.py:426
  25.5 0.9 shard_map.113
  26.4 1.7 %collective-permute-start.3 = (f32[7,24,512]{2,1,0:T(8,128)S(1)}, f32[7,24,512]{2,1,0:T(8,128)S(1)}, u32[]{:S(2)}, u32[]{:S(2)}) collective-permute-start(f32[7,24,512]{2,1,0:T(8,128)S(1)} %get-tuple-element.38.refs_1_), channel_id=1, source_target_pairs={{0,1},{1,0},{2,3},{3,2},{4,5},{5,4},{6,7},{7,6},{8,9},{9,8},{10,11... | collective-permute-start | bytes 1032200 | tf_op jit(solution)/shard_map/ppermute | solution.py:422
  28.1 2.2 %collective-permute-start.4 = (f32[7,24,512]{2,1,0:T(8,128)S(1)}, f32[7,24,512]{2,1,0:T(8,128)S(1)}, u32[]{:S(2)}, u32[]{:S(2)}) collective-permute-start(f32[7,24,512]{2,1,0:T(8,128)S(1)} %get-tuple-element.39.refs_2_), channel_id=1, source_target_pairs={{0,3},{1,2},{2,1},{3,0},{4,7},{5,6},{6,5},{7,4},{8,11},{9,10},{10,... | collective-permute-start | bytes 1032200 | tf_op jit(solution)/shard_map/ppermute | solution.py:422
  30.3 1.2 %collective-permute-done.5 = f32[32,1,128]{2,1,0:T(1,128)S(1)} collective-permute-done((f32[32,1,128]{2,1,0:T(1,128)S(1)}, f32[32,1,128]{2,1,0:T(1,128)S(1)}, u32[]{:S(2)}, u32[]{:S(2)}) %collective-permute-start.5) | collective-permute-done | bytes 16416 | tf_op jit(solution)/shard_map/ppermute | solution.py:425
  31.5 12.7 %all_to_all.26.reply = f32[32,1,128]{2,1,0:T(1,128)S(1)} all-to-all(f32[32,1,128]{2,1,0:T(1,128)S(1)} %collective-permute-done.5), channel_id=1, replica_groups=mesh['panel'=2,'ang'=32,'rad'=4] {'ang'}, dimensions={0} | all-to-all | bytes 32768 | tf_op jit(solution)/shard_map/all_to_all | solution.py:426
  44.2 0.4 shard_map.114.refs_5_
  44.6 0.0 collective-permute-done.3.refs_3_
  44.7 1.6 %shard_map.115 = (f32[7,24,512]{2,1,0:T(8,128)S(1)}, f32[7,24,512]{2,1,0:T(8,128)S(1)}, f32[7,16,512]{2,1,0:T(8,128)S(1)}, f32[7,16,512]{2,1,0:T(8,128)S(1)}, f32[32,1,128]{2,1,0:T(1,128)S(1)}) custom-call(f32[1,512]{1,0:T(1,128)S(1)} %get-tuple-element.31.refs_0_, f32[7,24,512]{2,1,0:T(8,128)S(1)} %get-tuple-element.38.refs_1_, ...), custom_call_target="tpu_custom_call" | custom-call | tf_op jit(solution)/shard_map/pallas_call | solution.py:405
  46.3 0.8 collective-permute-start.6
  47.0 0.6 collective-permute-start.7
  47.6 1.2 %collective-permute-done.8 = f32[32,1,128]{2,1,0:T(1,128)S(1)} collective-permute-done((f32[32,1,128]{2,1,0:T(1,128)S(1)}, f32[32,1,128]{2,1,0:T(1,128)S(1)}, u32[]{:S(2)}, u32[]{:S(2)}) %collective-permute-start.8) | collective-permute-done | bytes 16416 | tf_op jit(solution)/shard_map/ppermute | solution.py:425
  48.8 12.7 %all_to_all.27.reply = f32[32,1,128]{2,1,0:T(1,128)S(1)} all-to-all(f32[32,1,128]{2,1,0:T(1,128)S(1)} %collective-permute-done.8), channel_id=1, replica_groups=mesh['panel'=2,'ang'=32,'rad'=4] {'ang'}, dimensions={0} | all-to-all | bytes 32768 | tf_op jit(solution)/shard_map/all_to_all | solution.py:426
  61.5 0.4 shard_map.116.refs_5_
  62.0 0.0 collective-permute-done.6.refs_3_
  62.0 1.6 %shard_map.117 = (f32[7,24,512]{2,1,0:T(8,128)S(1)}, f32[7,24,512]{2,1,0:T(8,128)S(1)}, f32[7,16,512]{2,1,0:T(8,128)S(1)}, f32[7,16,512]{2,1,0:T(8,128)S(1)}, f32[32,1,128]{2,1,0:T(1,128)S(1)}) custom-call(f32[1,512]{1,0:T(1,128)S(1)} %get-tuple-element.31.refs_0_, f32[7,24,512]{2,1,0:T(8,128)S(1)} %get-tuple-element.38.refs_1_, ...), custom_call_target="tpu_custom_call" | custom-call | tf_op jit(solution)/shard_map/pallas_call | solution.py:405
  63.6 1.3 %collective-permute-start.9 = (f32[7,24,512]{2,1,0:T(8,128)S(1)}, f32[7,24,512]{2,1,0:T(8,128)S(1)}, u32[]{:S(2)}, u32[]{:S(2)}) collective-permute-start(f32[7,24,512]{2,1,0:T(8,128)S(1)} %get-tuple-element.49.refs_6_), channel_id=1, source_target_pairs={{0,1},{1,0},{2,3},{3,2},{4,5},{5,4},{6,7},{7,6},{8,9},{9,8},{10,11... | collective-permute-start | bytes 1032200 | tf_op jit(solution)/shard_map/ppermute | solution.py:422
  64.9 2.2 %collective-permute-start.10 = (f32[7,24,512]{2,1,0:T(8,128)S(1)}, f32[7,24,512]{2,1,0:T(8,128)S(1)}, u32[]{:S(2)}, u32[]{:S(2)}) collective-permute-start(f32[7,24,512]{2,1,0:T(8,128)S(1)} %get-tuple-element.50.refs_7_), channel_id=1, source_target_pairs={{0,3},{1,2},{2,1},{3,0},{4,7},{5,6},{6,5},{7,4},{8,11},{9,10},{10,... | collective-permute-start | bytes 1032200 | tf_op jit(solution)/shard_map/ppermute | solution.py:422
  67.1 1.2 %collective-permute-done.11 = f32[32,1,128]{2,1,0:T(1,128)S(1)} collective-permute-done((f32[32,1,128]{2,1,0:T(1,128)S(1)}, f32[32,1,128]{2,1,0:T(1,128)S(1)}, u32[]{:S(2)}, u32[]{:S(2)}) %collective-permute-start.11) | collective-permute-done | bytes 16416 | tf_op jit(solution)/shard_map/ppermute | solution.py:425
  68.3 12.7 %all_to_all.28.reply = f32[32,1,128]{2,1,0:T(1,128)S(1)} all-to-all(f32[32,1,128]{2,1,0:T(1,128)S(1)} %collective-permute-done.11), channel_id=1, replica_groups=mesh['panel'=2,'ang'=32,'rad'=4] {'ang'}, dimensions={0} | all-to-all | bytes 32768 | tf_op jit(solution)/shard_map/all_to_all | solution.py:426
  81.0 0.4 shard_map.118.refs_5_
  81.5 1.6 %shard_map.119 = (f32[7,24,512]{2,1,0:T(8,128)S(1)}, f32[7,24,512]{2,1,0:T(8,128)S(1)}, f32[7,16,512]{2,1,0:T(8,128)S(1)}, f32[7,16,512]{2,1,0:T(8,128)S(1)}, f32[32,1,128]{2,1,0:T(1,128)S(1)}) custom-call(f32[1,512]{1,0:T(1,128)S(1)} %get-tuple-element.31.refs_0_, f32[7,24,512]{2,1,0:T(8,128)S(1)} %get-tuple-element.38.refs_1_, ...), custom_call_target="tpu_custom_call" | custom-call | tf_op jit(solution)/shard_map/pallas_call | solution.py:405
  83.1 0.8 collective-permute-start.12
  83.9 0.6 collective-permute-start.13
  84.5 1.2 %collective-permute-done.14 = f32[32,1,128]{2,1,0:T(1,128)S(1)} collective-permute-done((f32[32,1,128]{2,1,0:T(1,128)S(1)}, f32[32,1,128]{2,1,0:T(1,128)S(1)}, u32[]{:S(2)}, u32[]{:S(2)}) %collective-permute-start.14) | collective-permute-done | bytes 16416 | tf_op jit(solution)/shard_map/ppermute | solution.py:425
  85.6 12.7 %all_to_all.29.reply = f32[32,1,128]{2,1,0:T(1,128)S(1)} all-to-all(f32[32,1,128]{2,1,0:T(1,128)S(1)} %collective-permute-done.14), channel_id=1, replica_groups=mesh['panel'=2,'ang'=32,'rad'=4] {'ang'}, dimensions={0} | all-to-all | bytes 32768 | tf_op jit(solution)/shard_map/all_to_all | solution.py:426
  98.4 0.4 shard_map.120.refs_5_
  98.8 1.6 %shard_map.121 = (f32[1,2,16,512]{3,2,1,0:T(8,128)}, f32[1,3,2,16,512]{4,3,2,1,0:T(8,128)}, f32[1,3,2,16,512]{4,3,2,1,0:T(8,128)}) custom-call(f32[1,512]{1,0:T(1,128)S(1)} %get-tuple-element.31.refs_0_, f32[7,24,512]{2,1,0:T(8,128)S(1)} %get-tuple-element.38.refs_1_, f32[7,24,512]{2,1,0:T(8,128)S(1)} %get-tuple-element.39.refs_2_, ...), custom_call_target="tpu_custom_call" | custom-call | tf_op jit(solution)/shard_map/pallas_call | solution.py:405
  (13 shorter events, 0.0 us)
Async XLA Ops:
  2.1 23.4 %collective-permute-start.1 = (f32[8,8,512]{2,1,0:T(8,128)S(1)}, f32[8,8,512]{2,1,0:T(8,128)S(1)}, u32[]{:S(2)}, u32[]{:S(2)}) collective-permute-start(f32[8,8,512]{2,1,0:T(8,128)S(1)} %get-tuple-element.35), channel_id=1, source_target_pairs={{0,4},{4,0},{8,12},{12,8},{16,20},{20,16},{24,28},{28,24},{32,36},... | collective-permute-start | bytes 393224 | tf_op jit(solution)/shard_map/ppermute | solution.py:422
  4.4 21.1 %collective-permute-start.2 = (f32[8,8,512]{2,1,0:T(8,128)S(1)}, f32[8,8,512]{2,1,0:T(8,128)S(1)}, u32[]{:S(2)}, u32[]{:S(2)}) collective-permute-start(f32[8,8,512]{2,1,0:T(8,128)S(1)} %get-tuple-element.36), channel_id=1, source_target_pairs={{0,124},{4,8},{8,4},{12,16},{16,12},{20,24},{24,20},{28,32},{32,28... | collective-permute-start | bytes 393224 | tf_op jit(solution)/shard_map/ppermute | solution.py:422
  4.9 1.2 %collective-permute-start = (f32[32,1,128]{2,1,0:T(1,128)S(1)}, f32[32,1,128]{2,1,0:T(1,128)S(1)}, u32[]{:S(2)}, u32[]{:S(2)}) collective-permute-start(f32[32,1,128]{2,1,0:T(1,128)S(1)} %get-tuple-element.32), channel_id=1, source_target_pairs={{0,128},{128,0},{1,129},{129,1},{2,130},{130,2},{3,131},{131,3},{4... | collective-permute-start | bytes 49160 | tf_op jit(solution)/shard_map/ppermute | solution.py:425
  26.4 18.2 %collective-permute-start.3 = (f32[7,24,512]{2,1,0:T(8,128)S(1)}, f32[7,24,512]{2,1,0:T(8,128)S(1)}, u32[]{:S(2)}, u32[]{:S(2)}) collective-permute-start(f32[7,24,512]{2,1,0:T(8,128)S(1)} %get-tuple-element.38.refs_1_), channel_id=1, source_target_pairs={{0,1},{1,0},{2,3},{3,2},{4,5},{5,4},{6,7},{7,6},{8,9},{9,8},{10,11... | collective-permute-start | bytes 1032200 | tf_op jit(solution)/shard_map/ppermute | solution.py:422
  28.1 16.5 %collective-permute-start.4 = (f32[7,24,512]{2,1,0:T(8,128)S(1)}, f32[7,24,512]{2,1,0:T(8,128)S(1)}, u32[]{:S(2)}, u32[]{:S(2)}) collective-permute-start(f32[7,24,512]{2,1,0:T(8,128)S(1)} %get-tuple-element.39.refs_2_), channel_id=1, source_target_pairs={{0,3},{1,2},{2,1},{3,0},{4,7},{5,6},{6,5},{7,4},{8,11},{9,10},{10,... | collective-permute-start | bytes 1032200 | tf_op jit(solution)/shard_map/ppermute | solution.py:422
  30.3 1.2 %collective-permute-start.5 = (f32[32,1,128]{2,1,0:T(1,128)S(1)}, f32[32,1,128]{2,1,0:T(1,128)S(1)}, u32[]{:S(2)}, u32[]{:S(2)}) collective-permute-start(f32[32,1,128]{2,1,0:T(1,128)S(1)} %get-tuple-element.40), channel_id=1, source_target_pairs={{0,128},{128,0},{1,129},{129,1},{2,130},{130,2},{3,131},{131,3},{4... | collective-permute-start | bytes 49160 | tf_op jit(solution)/shard_map/ppermute | solution.py:425
  46.3 15.7 %collective-permute-start.6 = (f32[7,24,512]{2,1,0:T(8,128)S(1)}, f32[7,24,512]{2,1,0:T(8,128)S(1)}, u32[]{:S(2)}, u32[]{:S(2)}) collective-permute-start(f32[7,24,512]{2,1,0:T(8,128)S(1)} %get-tuple-element.44.refs_6_), channel_id=1, source_target_pairs={{0,1},{1,0},{2,3},{3,2},{4,5},{5,4},{6,7},{7,6},{8,9},{9,8},{10,11... | collective-permute-start | bytes 1032200 | tf_op jit(solution)/shard_map/ppermute | solution.py:422
  47.0 15.0 %collective-permute-start.7 = (f32[7,24,512]{2,1,0:T(8,128)S(1)}, f32[7,24,512]{2,1,0:T(8,128)S(1)}, u32[]{:S(2)}, u32[]{:S(2)}) collective-permute-start(f32[7,24,512]{2,1,0:T(8,128)S(1)} %get-tuple-element.45.refs_7_), channel_id=1, source_target_pairs={{0,3},{1,2},{2,1},{3,0},{4,7},{5,6},{6,5},{7,4},{8,11},{9,10},{10,... | collective-permute-start | bytes 1032200 | tf_op jit(solution)/shard_map/ppermute | solution.py:422
  47.6 1.2 %collective-permute-start.8 = (f32[32,1,128]{2,1,0:T(1,128)S(1)}, f32[32,1,128]{2,1,0:T(1,128)S(1)}, u32[]{:S(2)}, u32[]{:S(2)}) collective-permute-start(f32[32,1,128]{2,1,0:T(1,128)S(1)} %get-tuple-element.46), channel_id=1, source_target_pairs={{0,128},{128,0},{1,129},{129,1},{2,130},{130,2},{3,131},{131,3},{4... | collective-permute-start | bytes 49160 | tf_op jit(solution)/shard_map/ppermute | solution.py:425
  63.6 17.8 %collective-permute-start.9 = (f32[7,24,512]{2,1,0:T(8,128)S(1)}, f32[7,24,512]{2,1,0:T(8,128)S(1)}, u32[]{:S(2)}, u32[]{:S(2)}) collective-permute-start(f32[7,24,512]{2,1,0:T(8,128)S(1)} %get-tuple-element.49.refs_6_), channel_id=1, source_target_pairs={{0,1},{1,0},{2,3},{3,2},{4,5},{5,4},{6,7},{7,6},{8,9},{9,8},{10,11... | collective-permute-start | bytes 1032200 | tf_op jit(solution)/shard_map/ppermute | solution.py:422
  64.9 16.5 %collective-permute-start.10 = (f32[7,24,512]{2,1,0:T(8,128)S(1)}, f32[7,24,512]{2,1,0:T(8,128)S(1)}, u32[]{:S(2)}, u32[]{:S(2)}) collective-permute-start(f32[7,24,512]{2,1,0:T(8,128)S(1)} %get-tuple-element.50.refs_7_), channel_id=1, source_target_pairs={{0,3},{1,2},{2,1},{3,0},{4,7},{5,6},{6,5},{7,4},{8,11},{9,10},{10,... | collective-permute-start | bytes 1032200 | tf_op jit(solution)/shard_map/ppermute | solution.py:422
  67.1 1.2 %collective-permute-start.11 = (f32[32,1,128]{2,1,0:T(1,128)S(1)}, f32[32,1,128]{2,1,0:T(1,128)S(1)}, u32[]{:S(2)}, u32[]{:S(2)}) collective-permute-start(f32[32,1,128]{2,1,0:T(1,128)S(1)} %get-tuple-element.51), channel_id=1, source_target_pairs={{0,128},{128,0},{1,129},{129,1},{2,130},{130,2},{3,131},{131,3},{4... | collective-permute-start | bytes 49160 | tf_op jit(solution)/shard_map/ppermute | solution.py:425
  83.1 15.7 %collective-permute-start.12 = (f32[7,24,512]{2,1,0:T(8,128)S(1)}, f32[7,24,512]{2,1,0:T(8,128)S(1)}, u32[]{:S(2)}, u32[]{:S(2)}) collective-permute-start(f32[7,24,512]{2,1,0:T(8,128)S(1)} %get-tuple-element.54.refs_6_), channel_id=1, source_target_pairs={{0,1},{1,0},{2,3},{3,2},{4,5},{5,4},{6,7},{7,6},{8,9},{9,8},{10,11... | collective-permute-start | bytes 1032200 | tf_op jit(solution)/shard_map/ppermute | solution.py:422
  83.9 15.0 %collective-permute-start.13 = (f32[7,24,512]{2,1,0:T(8,128)S(1)}, f32[7,24,512]{2,1,0:T(8,128)S(1)}, u32[]{:S(2)}, u32[]{:S(2)}) collective-permute-start(f32[7,24,512]{2,1,0:T(8,128)S(1)} %get-tuple-element.55.refs_7_), channel_id=1, source_target_pairs={{0,3},{1,2},{2,1},{3,0},{4,7},{5,6},{6,5},{7,4},{8,11},{9,10},{10,... | collective-permute-start | bytes 1032200 | tf_op jit(solution)/shard_map/ppermute | solution.py:422
  84.5 1.2 %collective-permute-start.14 = (f32[32,1,128]{2,1,0:T(1,128)S(1)}, f32[32,1,128]{2,1,0:T(1,128)S(1)}, u32[]{:S(2)}, u32[]{:S(2)}) collective-permute-start(f32[32,1,128]{2,1,0:T(1,128)S(1)} %get-tuple-element.56), channel_id=1, source_target_pairs={{0,128},{128,0},{1,129},{129,1},{2,130},{130,2},{3,131},{131,3},{4... | collective-permute-start | bytes 49160 | tf_op jit(solution)/shard_map/ppermute | solution.py:425

commit v7 on v6

--- a/solution.py
+++ b/solution.py
@@ -234,7 +234,7 @@
     )
 
 
-def ghost_kernel(reply, table, out_ref):
+def ghosts_of(reply, table):
     got = reply[...].reshape(32, 128)
     picks = table[...]
     rows = picks.shape[0]
@@ -253,13 +253,13 @@
     is_p = (lane == 3) | (lane == 6)
     turned_t = cosine * ghost + sine * pltpu.roll(ghost, 127, axis=1)
     turned_p = cosine * ghost - sine * pltpu.roll(ghost, 1, axis=1)
-    out_ref[...] = jnp.where(is_t, turned_t, jnp.where(is_p, turned_p, ghost))
+    return jnp.where(is_t, turned_t, jnp.where(is_p, turned_p, ghost))
 
 
 def stage_kernel(stage, n_rad, n_ang, *refs):
     last = stage == 4
-    (sines, low0, high0, below, above, ghosts) = refs[:6]
-    refs = refs[6:]
+    (sines, low0, high0, below, above, reply, table) = refs[:7]
+    refs = refs[7:]
     if stage == 1:
         low, high = low0, high0
     else:
@@ -279,7 +279,7 @@
     invs = [inverse_radius(rad, n_rad, slot, 2) for slot in range(2)]
     outward = jnp.where((rad & 1) == 0, jnp.float32(0.5), jnp.float32(-0.5))
     wall = (rad == 0) | (rad == n_rad - 1)
-    ghost = ghosts[...]
+    ghost = ghosts_of(reply, table)
     sine_row = sines[...]
     own = rows_p - 2 * EDGE
     half_row = iota((8, 128), 1) < 64
@@ -449,8 +449,7 @@
     for stage in range(1, 5):
         below = exchanged(low, "rad", 0)
         above = exchanged(high, "rad", 1)
-        (ghosts,) = call(ghost_kernel, [crossed(answer), table], [shape(2 * wide, 128)])
-        ins = [sines, low0, high0, below, above, ghosts]
+        ins = [sines, low0, high0, below, above, crossed(answer), table]
         if stage > 1:
             ins += [low, high, *sums]
         if stage < 4:

time: 102 us -> 100 us (0.980)
  Pallas kernels: 10.6 us -> 8.97 us
    pallas_call x10 -> x6, Pallas kernels: 10.6 us -> 8.97 us  [call(): pl.pallas_call(kernel, out_shape=outs, in_specs=[vmem] * len(ins), out_sp...]
  transfers between devices with their start and end apart: 15 -> 15, of which waited for: 5 -> 5; matrix products, arithmetic and copies ran while one was open for 0% -> 0% of each run, Pallas kernels for 2% -> 0%
where the time goes in v7:
time: 100 us; the launch traced here: 98.7 us
  blocking collectives  70.3 us (70%)
  starting transfers between devices  12.8 us (13%)
  Pallas kernels  8.97 us (9%)
  waiting for transfers between devices  5.93 us (6%)
    all_to_all x5, blocking collectives, crossed(): lax.all_to_all(swap, 'ang', split_axis=0, concat_axis=0, tiled=True)  70.3 us
    ppermute x10, starting transfers between devices, exchanged(): return held(lax.ppermute(value, axis, partners(lax.axis_size(axis), step)))  12.8 us
    pallas_call x6, Pallas kernels, call(): pl.pallas_call(kernel, out_shape=outs, in_specs=[vmem] * len(ins), out_sp...  8.97 us
    ppermute x5, waiting for transfers between devices, crossed(): swap = held(lax.ppermute(value, 'panel', [(0, 1), (1, 0)]))  5.91 us
  transfers between devices with their start and end apart: 15, of which 5 were waited for; matrix products, arithmetic and copies ran while one was open for 0% of the time, Pallas kernels for 0%

profile of v7, /device:TPU:2, one launch (start us, length us, event | category | flops | bytes accessed | tf_op | source)
XLA Modules:
  0.0 98.7 jit_solution(12127196040302701598)
XLA Ops:
  0.6 1.5 %shard_map.112 = (f32[7,16,512]{2,1,0:T(8,128)S(1)}, f32[7,16,512]{2,1,0:T(8,128)S(1)}, f32[8,8,512]{2,1,0:T(8,128)S(1)}, f32[8,8,512]{2,1,0:T(8,128)S(1)}, f32[...) custom-call(f32[1,2,16,512]{3,2,1,0:T(8,128)} %density.1, f32[1,3,2,16,512]{4,3,2,1,0:T(8,128)} %momentum.1, ...), custom_call_target="tpu_custom_call" | custom-call | tf_op jit(solution)/shard_map/pallas_call | solution.py:405
  2.1 2.3 %collective-permute-start.1 = (f32[8,8,512]{2,1,0:T(8,128)S(1)}, f32[8,8,512]{2,1,0:T(8,128)S(1)}, u32[]{:S(2)}, u32[]{:S(2)}) collective-permute-start(f32[8,8,512]{2,1,0:T(8,128)S(1)} %get-tuple-element.35), channel_id=1, source_target_pairs={{0,4},{4,0},{8,12},{12,8},{16,20},{20,16},{24,28},{28,24},{32,36},... | collective-permute-start | bytes 393224 | tf_op jit(solution)/shard_map/ppermute | solution.py:422
  4.4 0.4 collective-permute-start.2
  4.9 0.0 collective-permute-start
  4.9 1.2 %collective-permute-done = f32[32,1,128]{2,1,0:T(1,128)S(1)} collective-permute-done((f32[32,1,128]{2,1,0:T(1,128)S(1)}, f32[32,1,128]{2,1,0:T(1,128)S(1)}, u32[]{:S(2)}, u32[]{:S(2)}) %collective-permute-start) | collective-permute-done | bytes 16416 | tf_op jit(solution)/shard_map/ppermute | solution.py:425
  6.1 19.4 %all_to_all.25.asked_ref = f32[32,1,128]{2,1,0:T(1,128)S(1)} all-to-all(f32[32,1,128]{2,1,0:T(1,128)S(1)} %collective-permute-done), channel_id=1, replica_groups=mesh['panel'=2,'ang'=32,'rad'=4] {'ang'}, dimensions={0} | all-to-all | bytes 32768 | tf_op jit(solution)/shard_map/all_to_all | solution.py:426
  25.5 0.0 collective-permute-done.1.one_ref
  25.5 0.0 collective-permute-done.2.two_ref
  25.5 0.9 shard_map.113
  26.4 1.7 %collective-permute-start.3 = (f32[7,24,512]{2,1,0:T(8,128)S(1)}, f32[7,24,512]{2,1,0:T(8,128)S(1)}, u32[]{:S(2)}, u32[]{:S(2)}) collective-permute-start(f32[7,24,512]{2,1,0:T(8,128)S(1)} %get-tuple-element.38.refs_1_), channel_id=1, source_target_pairs={{0,1},{1,0},{2,3},{3,2},{4,5},{5,4},{6,7},{7,6},{8,9},{9,8},{10,11... | collective-permute-start | bytes 1032200 | tf_op jit(solution)/shard_map/ppermute | solution.py:422
  28.1 2.2 %collective-permute-start.4 = (f32[7,24,512]{2,1,0:T(8,128)S(1)}, f32[7,24,512]{2,1,0:T(8,128)S(1)}, u32[]{:S(2)}, u32[]{:S(2)}) collective-permute-start(f32[7,24,512]{2,1,0:T(8,128)S(1)} %get-tuple-element.39.refs_2_), channel_id=1, source_target_pairs={{0,3},{1,2},{2,1},{3,0},{4,7},{5,6},{6,5},{7,4},{8,11},{9,10},{10,... | collective-permute-start | bytes 1032200 | tf_op jit(solution)/shard_map/ppermute | solution.py:422
  30.3 1.2 %collective-permute-done.5 = f32[32,1,128]{2,1,0:T(1,128)S(1)} collective-permute-done((f32[32,1,128]{2,1,0:T(1,128)S(1)}, f32[32,1,128]{2,1,0:T(1,128)S(1)}, u32[]{:S(2)}, u32[]{:S(2)}) %collective-permute-start.5) | collective-permute-done | bytes 16416 | tf_op jit(solution)/shard_map/ppermute | solution.py:425
  31.5 12.7 %all_to_all.26.refs_5_ = f32[32,1,128]{2,1,0:T(1,128)S(1)} all-to-all(f32[32,1,128]{2,1,0:T(1,128)S(1)} %collective-permute-done.5), channel_id=1, replica_groups=mesh['panel'=2,'ang'=32,'rad'=4] {'ang'}, dimensions={0} | all-to-all | bytes 32768 | tf_op jit(solution)/shard_map/all_to_all | solution.py:426
  44.2 0.0 collective-permute-done.3.refs_3_
  44.2 0.0 collective-permute-done.4.refs_4_
  44.2 1.6 %shard_map.114 = (f32[7,24,512]{2,1,0:T(8,128)S(1)}, f32[7,24,512]{2,1,0:T(8,128)S(1)}, f32[7,16,512]{2,1,0:T(8,128)S(1)}, f32[7,16,512]{2,1,0:T(8,128)S(1)}, f32[32,1,128]{2,1,0:T(1,128)S(1)}) custom-call(f32[1,512]{1,0:T(1,128)S(1)} %get-tuple-element.31.refs_0_, f32[7,24,512]{2,1,0:T(8,128)S(1)} %get-tuple-element.38.refs_1_, ...), custom_call_target="tpu_custom_call" | custom-call | tf_op jit(solution)/shard_map/pallas_call | solution.py:405
  45.8 0.8 collective-permute-start.6
  46.6 0.6 collective-permute-start.7
  47.2 1.2 %collective-permute-done.8 = f32[32,1,128]{2,1,0:T(1,128)S(1)} collective-permute-done((f32[32,1,128]{2,1,0:T(1,128)S(1)}, f32[32,1,128]{2,1,0:T(1,128)S(1)}, u32[]{:S(2)}, u32[]{:S(2)}) %collective-permute-start.8) | collective-permute-done | bytes 16416 | tf_op jit(solution)/shard_map/ppermute | solution.py:425
  48.4 12.7 %all_to_all.27.refs_5_ = f32[32,1,128]{2,1,0:T(1,128)S(1)} all-to-all(f32[32,1,128]{2,1,0:T(1,128)S(1)} %collective-permute-done.8), channel_id=1, replica_groups=mesh['panel'=2,'ang'=32,'rad'=4] {'ang'}, dimensions={0} | all-to-all | bytes 32768 | tf_op jit(solution)/shard_map/all_to_all | solution.py:426
  61.1 1.6 %shard_map.115 = (f32[7,24,512]{2,1,0:T(8,128)S(1)}, f32[7,24,512]{2,1,0:T(8,128)S(1)}, f32[7,16,512]{2,1,0:T(8,128)S(1)}, f32[7,16,512]{2,1,0:T(8,128)S(1)}, f32[32,1,128]{2,1,0:T(1,128)S(1)}) custom-call(f32[1,512]{1,0:T(1,128)S(1)} %get-tuple-element.31.refs_0_, f32[7,24,512]{2,1,0:T(8,128)S(1)} %get-tuple-element.38.refs_1_, ...), custom_call_target="tpu_custom_call" | custom-call | tf_op jit(solution)/shard_map/pallas_call | solution.py:405
  62.7 1.3 %collective-permute-start.9 = (f32[7,24,512]{2,1,0:T(8,128)S(1)}, f32[7,24,512]{2,1,0:T(8,128)S(1)}, u32[]{:S(2)}, u32[]{:S(2)}) collective-permute-start(f32[7,24,512]{2,1,0:T(8,128)S(1)} %get-tuple-element.49.refs_7_), channel_id=1, source_target_pairs={{0,1},{1,0},{2,3},{3,2},{4,5},{5,4},{6,7},{7,6},{8,9},{9,8},{10,11... | collective-permute-start | bytes 1032200 | tf_op jit(solution)/shard_map/ppermute | solution.py:422
  64.0 2.2 %collective-permute-start.10 = (f32[7,24,512]{2,1,0:T(8,128)S(1)}, f32[7,24,512]{2,1,0:T(8,128)S(1)}, u32[]{:S(2)}, u32[]{:S(2)}) collective-permute-start(f32[7,24,512]{2,1,0:T(8,128)S(1)} %get-tuple-element.50.refs_8_), channel_id=1, source_target_pairs={{0,3},{1,2},{2,1},{3,0},{4,7},{5,6},{6,5},{7,4},{8,11},{9,10},{10,... | collective-permute-start | bytes 1032200 | tf_op jit(solution)/shard_map/ppermute | solution.py:422
  66.2 1.2 %collective-permute-done.11 = f32[32,1,128]{2,1,0:T(1,128)S(1)} collective-permute-done((f32[32,1,128]{2,1,0:T(1,128)S(1)}, f32[32,1,128]{2,1,0:T(1,128)S(1)}, u32[]{:S(2)}, u32[]{:S(2)}) %collective-permute-start.11) | collective-permute-done | bytes 16416 | tf_op jit(solution)/shard_map/ppermute | solution.py:425
  67.4 12.7 %all_to_all.28.refs_5_ = f32[32,1,128]{2,1,0:T(1,128)S(1)} all-to-all(f32[32,1,128]{2,1,0:T(1,128)S(1)} %collective-permute-done.11), channel_id=1, replica_groups=mesh['panel'=2,'ang'=32,'rad'=4] {'ang'}, dimensions={0} | all-to-all | bytes 32768 | tf_op jit(solution)/shard_map/all_to_all | solution.py:426
  80.1 0.0 collective-permute-done.9.refs_3_
  80.1 1.6 %shard_map.116 = (f32[7,24,512]{2,1,0:T(8,128)S(1)}, f32[7,24,512]{2,1,0:T(8,128)S(1)}, f32[7,16,512]{2,1,0:T(8,128)S(1)}, f32[7,16,512]{2,1,0:T(8,128)S(1)}, f32[32,1,128]{2,1,0:T(1,128)S(1)}) custom-call(f32[1,512]{1,0:T(1,128)S(1)} %get-tuple-element.31.refs_0_, f32[7,24,512]{2,1,0:T(8,128)S(1)} %get-tuple-element.38.refs_1_, ...), custom_call_target="tpu_custom_call" | custom-call | tf_op jit(solution)/shard_map/pallas_call | solution.py:405
  81.7 0.8 collective-permute-start.12
  82.5 0.6 collective-permute-start.13
  83.1 1.2 %collective-permute-done.14 = f32[32,1,128]{2,1,0:T(1,128)S(1)} collective-permute-done((f32[32,1,128]{2,1,0:T(1,128)S(1)}, f32[32,1,128]{2,1,0:T(1,128)S(1)}, u32[]{:S(2)}, u32[]{:S(2)}) %collective-permute-start.14) | collective-permute-done | bytes 16416 | tf_op jit(solution)/shard_map/ppermute | solution.py:425
  84.3 12.7 %all_to_all.29.refs_5_ = f32[32,1,128]{2,1,0:T(1,128)S(1)} all-to-all(f32[32,1,128]{2,1,0:T(1,128)S(1)} %collective-permute-done.14), channel_id=1, replica_groups=mesh['panel'=2,'ang'=32,'rad'=4] {'ang'}, dimensions={0} | all-to-all | bytes 32768 | tf_op jit(solution)/shard_map/all_to_all | solution.py:426
  97.0 1.7 %shard_map.117 = (f32[1,2,16,512]{3,2,1,0:T(8,128)}, f32[1,3,2,16,512]{4,3,2,1,0:T(8,128)}, f32[1,3,2,16,512]{4,3,2,1,0:T(8,128)}) custom-call(f32[1,512]{1,0:T(1,128)S(1)} %get-tuple-element.31.refs_0_, f32[7,24,512]{2,1,0:T(8,128)S(1)} %get-tuple-element.38.refs_1_, f32[7,24,512]{2,1,0:T(8,128)S(1)} %get-tuple-element.39.refs_2_, ...), custom_call_target="tpu_custom_call" | custom-call | tf_op jit(solution)/shard_map/pallas_call | solution.py:405
  (9 shorter events, 0.0 us)
Async XLA Ops:
  2.1 23.4 %collective-permute-start.1 = (f32[8,8,512]{2,1,0:T(8,128)S(1)}, f32[8,8,512]{2,1,0:T(8,128)S(1)}, u32[]{:S(2)}, u32[]{:S(2)}) collective-permute-start(f32[8,8,512]{2,1,0:T(8,128)S(1)} %get-tuple-element.35), channel_id=1, source_target_pairs={{0,4},{4,0},{8,12},{12,8},{16,20},{20,16},{24,28},{28,24},{32,36},... | collective-permute-start | bytes 393224 | tf_op jit(solution)/shard_map/ppermute | solution.py:422
  4.4 21.1 %collective-permute-start.2 = (f32[8,8,512]{2,1,0:T(8,128)S(1)}, f32[8,8,512]{2,1,0:T(8,128)S(1)}, u32[]{:S(2)}, u32[]{:S(2)}) collective-permute-start(f32[8,8,512]{2,1,0:T(8,128)S(1)} %get-tuple-element.36), channel_id=1, source_target_pairs={{0,124},{4,8},{8,4},{12,16},{16,12},{20,24},{24,20},{28,32},{32,28... | collective-permute-start | bytes 393224 | tf_op jit(solution)/shard_map/ppermute | solution.py:422
  4.9 1.2 %collective-permute-start = (f32[32,1,128]{2,1,0:T(1,128)S(1)}, f32[32,1,128]{2,1,0:T(1,128)S(1)}, u32[]{:S(2)}, u32[]{:S(2)}) collective-permute-start(f32[32,1,128]{2,1,0:T(1,128)S(1)} %get-tuple-element.32), channel_id=1, source_target_pairs={{0,128},{128,0},{1,129},{129,1},{2,130},{130,2},{3,131},{131,3},{4... | collective-permute-start | bytes 49160 | tf_op jit(solution)/shard_map/ppermute | solution.py:425
  26.4 17.8 %collective-permute-start.3 = (f32[7,24,512]{2,1,0:T(8,128)S(1)}, f32[7,24,512]{2,1,0:T(8,128)S(1)}, u32[]{:S(2)}, u32[]{:S(2)}) collective-permute-start(f32[7,24,512]{2,1,0:T(8,128)S(1)} %get-tuple-element.38.refs_1_), channel_id=1, source_target_pairs={{0,1},{1,0},{2,3},{3,2},{4,5},{5,4},{6,7},{7,6},{8,9},{9,8},{10,11... | collective-permute-start | bytes 1032200 | tf_op jit(solution)/shard_map/ppermute | solution.py:422
  28.1 16.1 %collective-permute-start.4 = (f32[7,24,512]{2,1,0:T(8,128)S(1)}, f32[7,24,512]{2,1,0:T(8,128)S(1)}, u32[]{:S(2)}, u32[]{:S(2)}) collective-permute-start(f32[7,24,512]{2,1,0:T(8,128)S(1)} %get-tuple-element.39.refs_2_), channel_id=1, source_target_pairs={{0,3},{1,2},{2,1},{3,0},{4,7},{5,6},{6,5},{7,4},{8,11},{9,10},{10,... | collective-permute-start | bytes 1032200 | tf_op jit(solution)/shard_map/ppermute | solution.py:422
  30.3 1.2 %collective-permute-start.5 = (f32[32,1,128]{2,1,0:T(1,128)S(1)}, f32[32,1,128]{2,1,0:T(1,128)S(1)}, u32[]{:S(2)}, u32[]{:S(2)}) collective-permute-start(f32[32,1,128]{2,1,0:T(1,128)S(1)} %get-tuple-element.40), channel_id=1, source_target_pairs={{0,128},{128,0},{1,129},{129,1},{2,130},{130,2},{3,131},{131,3},{4... | collective-permute-start | bytes 49160 | tf_op jit(solution)/shard_map/ppermute | solution.py:425
  45.8 15.3 %collective-permute-start.6 = (f32[7,24,512]{2,1,0:T(8,128)S(1)}, f32[7,24,512]{2,1,0:T(8,128)S(1)}, u32[]{:S(2)}, u32[]{:S(2)}) collective-permute-start(f32[7,24,512]{2,1,0:T(8,128)S(1)} %get-tuple-element.44.refs_7_), channel_id=1, source_target_pairs={{0,1},{1,0},{2,3},{3,2},{4,5},{5,4},{6,7},{7,6},{8,9},{9,8},{10,11... | collective-permute-start | bytes 1032200 | tf_op jit(solution)/shard_map/ppermute | solution.py:422
  46.6 14.5 %collective-permute-start.7 = (f32[7,24,512]{2,1,0:T(8,128)S(1)}, f32[7,24,512]{2,1,0:T(8,128)S(1)}, u32[]{:S(2)}, u32[]{:S(2)}) collective-permute-start(f32[7,24,512]{2,1,0:T(8,128)S(1)} %get-tuple-element.45.refs_8_), channel_id=1, source_target_pairs={{0,3},{1,2},{2,1},{3,0},{4,7},{5,6},{6,5},{7,4},{8,11},{9,10},{10,... | collective-permute-start | bytes 1032200 | tf_op jit(solution)/shard_map/ppermute | solution.py:422
  47.2 1.2 %collective-permute-start.8 = (f32[32,1,128]{2,1,0:T(1,128)S(1)}, f32[32,1,128]{2,1,0:T(1,128)S(1)}, u32[]{:S(2)}, u32[]{:S(2)}) collective-permute-start(f32[32,1,128]{2,1,0:T(1,128)S(1)} %get-tuple-element.46), channel_id=1, source_target_pairs={{0,128},{128,0},{1,129},{129,1},{2,130},{130,2},{3,131},{131,3},{4... | collective-permute-start | bytes 49160 | tf_op jit(solution)/shard_map/ppermute | solution.py:425
  62.7 17.4 %collective-permute-start.9 = (f32[7,24,512]{2,1,0:T(8,128)S(1)}, f32[7,24,512]{2,1,0:T(8,128)S(1)}, u32[]{:S(2)}, u32[]{:S(2)}) collective-permute-start(f32[7,24,512]{2,1,0:T(8,128)S(1)} %get-tuple-element.49.refs_7_), channel_id=1, source_target_pairs={{0,1},{1,0},{2,3},{3,2},{4,5},{5,4},{6,7},{7,6},{8,9},{9,8},{10,11... | collective-permute-start | bytes 1032200 | tf_op jit(solution)/shard_map/ppermute | solution.py:422
  64.0 16.1 %collective-permute-start.10 = (f32[7,24,512]{2,1,0:T(8,128)S(1)}, f32[7,24,512]{2,1,0:T(8,128)S(1)}, u32[]{:S(2)}, u32[]{:S(2)}) collective-permute-start(f32[7,24,512]{2,1,0:T(8,128)S(1)} %get-tuple-element.50.refs_8_), channel_id=1, source_target_pairs={{0,3},{1,2},{2,1},{3,0},{4,7},{5,6},{6,5},{7,4},{8,11},{9,10},{10,... | collective-permute-start | bytes 1032200 | tf_op jit(solution)/shard_map/ppermute | solution.py:422
  66.2 1.2 %collective-permute-start.11 = (f32[32,1,128]{2,1,0:T(1,128)S(1)}, f32[32,1,128]{2,1,0:T(1,128)S(1)}, u32[]{:S(2)}, u32[]{:S(2)}) collective-permute-start(f32[32,1,128]{2,1,0:T(1,128)S(1)} %get-tuple-element.51), channel_id=1, source_target_pairs={{0,128},{128,0},{1,129},{129,1},{2,130},{130,2},{3,131},{131,3},{4... | collective-permute-start | bytes 49160 | tf_op jit(solution)/shard_map/ppermute | solution.py:425
  81.7 15.3 %collective-permute-start.12 = (f32[7,24,512]{2,1,0:T(8,128)S(1)}, f32[7,24,512]{2,1,0:T(8,128)S(1)}, u32[]{:S(2)}, u32[]{:S(2)}) collective-permute-start(f32[7,24,512]{2,1,0:T(8,128)S(1)} %get-tuple-element.54.refs_7_), channel_id=1, source_target_pairs={{0,1},{1,0},{2,3},{3,2},{4,5},{5,4},{6,7},{7,6},{8,9},{9,8},{10,11... | collective-permute-start | bytes 1032200 | tf_op jit(solution)/shard_map/ppermute | solution.py:422
  82.5 14.5 %collective-permute-start.13 = (f32[7,24,512]{2,1,0:T(8,128)S(1)}, f32[7,24,512]{2,1,0:T(8,128)S(1)}, u32[]{:S(2)}, u32[]{:S(2)}) collective-permute-start(f32[7,24,512]{2,1,0:T(8,128)S(1)} %get-tuple-element.55.refs_8_), channel_id=1, source_target_pairs={{0,3},{1,2},{2,1},{3,0},{4,7},{5,6},{6,5},{7,4},{8,11},{9,10},{10,... | collective-permute-start | bytes 1032200 | tf_op jit(solution)/shard_map/ppermute | solution.py:422
  83.1 1.2 %collective-permute-start.14 = (f32[32,1,128]{2,1,0:T(1,128)S(1)}, f32[32,1,128]{2,1,0:T(1,128)S(1)}, u32[]{:S(2)}, u32[]{:S(2)}) collective-permute-start(f32[32,1,128]{2,1,0:T(1,128)S(1)} %get-tuple-element.56), channel_id=1, source_target_pairs={{0,128},{128,0},{1,129},{129,1},{2,130},{130,2},{3,131},{131,3},{4... | collective-permute-start | bytes 49160 | tf_op jit(solution)/shard_map/ppermute | solution.py:425

commit v8 on v7

--- a/solution.py
+++ b/solution.py
@@ -263,15 +263,16 @@
     if stage == 1:
         low, high = low0, high0
     else:
-        low, high, acc_low, acc_high = refs[:4]
-        refs = refs[4:]
+        low, high = refs[:2]
+        refs = refs[2:]
     if last:
-        density_out, momentum_out, magnetic_out = refs[:3]
-        refs = refs[3:]
+        two, three = refs[0:2], refs[2:4]
+        density_out, momentum_out, magnetic_out = refs[4:7]
+        refs = refs[7:]
     else:
         lanes, rowmask = refs[:2]
-        low_out, high_out, acc_low_out, acc_high_out, msg_out = refs[2:7]
-        refs = refs[7:]
+        low_out, high_out, msg_out = refs[2:5]
+        refs = refs[5:]
     slope, up, down = refs
     rad, ang = lax.axis_index("rad"), lax.axis_index("ang")
     rows_p, rows_t = low.shape[1:]
@@ -363,8 +364,9 @@
             k = k + pltpu.roll(up[slot, f], rows_p - 1, axis=0)[:used]
             if last:
                 level = 1 - (rad & 1) if slot == 0 else rad & 1
-                acc = acc_low if slot == 0 else acc_high
-                value = start[f, :own] + (time_step / 6.0) * (acc[f] + k)
+                now = low if slot == 0 else high
+                value = two[slot][f, :own] + 2.0 * three[slot][f, :own] + now[f, :own] - start[f, :own]
+                value = (1.0 / 3.0) * value + (time_step / 6.0) * k
                 if f == 0:
                     density_out[0, level] = value
                 elif f < 4:
@@ -372,11 +374,6 @@
                 else:
                     magnetic_out[0, f - 4, level] = value
                 continue
-            acc_out = acc_low_out if slot == 0 else acc_high_out
-            if stage == 1:
-                acc_out[f] = k[:own]
-            else:
-                acc_out[f] = (acc_low if slot == 0 else acc_high)[f] + 2.0 * k[:own]
             step = time_step if stage == 3 else 0.5 * time_step
             value = start[f] + step * k
             (low_out if slot == 0 else high_out)[f] = value
@@ -444,18 +441,19 @@
         [crossed(ask), low0, high0, one, two, table],
         [shape(8, 128, dtype=jnp.int32), shape(rows_p, 128), level, level, shape(2 * wide, 128), message],
     )
-    low, high, sums = low0, high0, []
+    low, high, kept = low0, high0, []
     scratch = [pltpu.VMEM((2, NF, wide, rows_t), f32) for _ in range(3)]
     for stage in range(1, 5):
         below = exchanged(low, "rad", 0)
         above = exchanged(high, "rad", 1)
         ins = [sines, low0, high0, below, above, crossed(answer), table]
         if stage > 1:
-            ins += [low, high, *sums]
+            ins += [low, high]
         if stage < 4:
             ins += [lanes, rowmask]
-            outs = [level, level, own_level, own_level, message]
+            outs = [level, level, message]
         else:
+            ins += kept
             outs = [
                 shape(1, rows_r, rows_p, rows_t, final=True),
                 shape(1, 3, rows_r, rows_p, rows_t, final=True),
@@ -468,8 +466,9 @@
         result = call(kernel, ins, outs, scratch)
         if stage == 4:
             return tuple(result)
-        low, high, acc_low, acc_high, answer = result
-        sums = [acc_low, acc_high]
+        low, high, answer = result
+        if stage < 3:
+            kept += [low, high]
 
 
 def solution(mesh):

time: 100 us -> 100 us (level)
  no operation moved by 1% of the time
where the time goes in v8:
time: 100 us; the launch traced here: 98.8 us
  blocking collectives  70.3 us (70%)
  starting transfers between devices  12.8 us (13%)
  Pallas kernels  9 us (9%)
  waiting for transfers between devices  5.93 us (6%)
    all_to_all x5, blocking collectives, crossed(): lax.all_to_all(swap, 'ang', split_axis=0, concat_axis=0, tiled=True)  70.3 us
    ppermute x10, starting transfers between devices, exchanged(): return held(lax.ppermute(value, axis, partners(lax.axis_size(axis), step)))  12.8 us
    pallas_call x6, Pallas kernels, call(): pl.pallas_call(kernel, out_shape=outs, in_specs=[vmem] * len(ins), out_sp...  9 us
    ppermute x5, waiting for transfers between devices, crossed(): swap = held(lax.ppermute(value, 'panel', [(0, 1), (1, 0)]))  5.91 us
  transfers between devices with their start and end apart: 15, of which 5 were waited for; matrix products, arithmetic and copies ran while one was open for 0% of the time, Pallas kernels for 0%

profile of v8, /device:TPU:2, one launch (start us, length us, event | category | flops | bytes accessed | tf_op | source)
XLA Modules:
  0.0 98.8 jit_solution(4156030134357111657)
XLA Ops:
  0.6 1.5 %shard_map.112 = (f32[7,16,512]{2,1,0:T(8,128)S(1)}, f32[7,16,512]{2,1,0:T(8,128)S(1)}, f32[8,8,512]{2,1,0:T(8,128)S(1)}, f32[8,8,512]{2,1,0:T(8,128)S(1)}, f32[...) custom-call(f32[1,2,16,512]{3,2,1,0:T(8,128)} %density.1, f32[1,3,2,16,512]{4,3,2,1,0:T(8,128)} %momentum.1, ...), custom_call_target="tpu_custom_call" | custom-call | tf_op jit(solution)/shard_map/pallas_call | solution.py:402
  2.1 2.3 %collective-permute-start.1 = (f32[8,8,512]{2,1,0:T(8,128)S(1)}, f32[8,8,512]{2,1,0:T(8,128)S(1)}, u32[]{:S(2)}, u32[]{:S(2)}) collective-permute-start(f32[8,8,512]{2,1,0:T(8,128)S(1)} %get-tuple-element.29), channel_id=1, source_target_pairs={{0,4},{4,0},{8,12},{12,8},{16,20},{20,16},{24,28},{28,24},{32,36},... | collective-permute-start | bytes 393224 | tf_op jit(solution)/shard_map/ppermute | solution.py:419
  4.4 0.4 collective-permute-start.2
  4.9 0.0 collective-permute-start
  4.9 1.2 %collective-permute-done = f32[32,1,128]{2,1,0:T(1,128)S(1)} collective-permute-done((f32[32,1,128]{2,1,0:T(1,128)S(1)}, f32[32,1,128]{2,1,0:T(1,128)S(1)}, u32[]{:S(2)}, u32[]{:S(2)}) %collective-permute-start) | collective-permute-done | bytes 16416 | tf_op jit(solution)/shard_map/ppermute | solution.py:422
  6.1 19.4 %all_to_all.25.asked_ref = f32[32,1,128]{2,1,0:T(1,128)S(1)} all-to-all(f32[32,1,128]{2,1,0:T(1,128)S(1)} %collective-permute-done), channel_id=1, replica_groups=mesh['panel'=2,'ang'=32,'rad'=4] {'ang'}, dimensions={0} | all-to-all | bytes 32768 | tf_op jit(solution)/shard_map/all_to_all | solution.py:423
  25.5 0.0 collective-permute-done.1.one_ref
  25.5 0.0 collective-permute-done.2.two_ref
  25.5 0.9 shard_map.113
  26.4 1.7 %collective-permute-start.3 = (f32[7,24,512]{2,1,0:T(8,128)S(1)}, f32[7,24,512]{2,1,0:T(8,128)S(1)}, u32[]{:S(2)}, u32[]{:S(2)}) collective-permute-start(f32[7,24,512]{2,1,0:T(8,128)S(1)} %get-tuple-element.32.refs_1_), channel_id=1, source_target_pairs={{0,1},{1,0},{2,3},{3,2},{4,5},{5,4},{6,7},{7,6},{8,9},{9,8},{10,11... | collective-permute-start | bytes 1032200 | tf_op jit(solution)/shard_map/ppermute | solution.py:419
  28.1 2.2 %collective-permute-start.4 = (f32[7,24,512]{2,1,0:T(8,128)S(1)}, f32[7,24,512]{2,1,0:T(8,128)S(1)}, u32[]{:S(2)}, u32[]{:S(2)}) collective-permute-start(f32[7,24,512]{2,1,0:T(8,128)S(1)} %get-tuple-element.33.refs_2_), channel_id=1, source_target_pairs={{0,3},{1,2},{2,1},{3,0},{4,7},{5,6},{6,5},{7,4},{8,11},{9,10},{10,... | collective-permute-start | bytes 1032200 | tf_op jit(solution)/shard_map/ppermute | solution.py:419
  30.3 1.2 %collective-permute-done.5 = f32[32,1,128]{2,1,0:T(1,128)S(1)} collective-permute-done((f32[32,1,128]{2,1,0:T(1,128)S(1)}, f32[32,1,128]{2,1,0:T(1,128)S(1)}, u32[]{:S(2)}, u32[]{:S(2)}) %collective-permute-start.5) | collective-permute-done | bytes 16416 | tf_op jit(solution)/shard_map/ppermute | solution.py:422
  31.5 12.7 %all_to_all.26.refs_5_ = f32[32,1,128]{2,1,0:T(1,128)S(1)} all-to-all(f32[32,1,128]{2,1,0:T(1,128)S(1)} %collective-permute-done.5), channel_id=1, replica_groups=mesh['panel'=2,'ang'=32,'rad'=4] {'ang'}, dimensions={0} | all-to-all | bytes 32768 | tf_op jit(solution)/shard_map/all_to_all | solution.py:423
  44.2 0.0 collective-permute-done.3.refs_3_
  44.2 0.0 collective-permute-done.4.refs_4_
  44.2 1.6 %shard_map.114 = (f32[7,24,512]{2,1,0:T(8,128)S(1)}, f32[7,24,512]{2,1,0:T(8,128)S(1)}, f32[32,1,128]{2,1,0:T(1,128)S(1)}) custom-call(f32[1,512]{1,0:T(1,128)S(1)} %get-tuple-element.25.refs_0_, f32[7,24,512]{2,1,0:T(8,128)S(1)} %get-tuple-element.32.refs_1_, f32[7,24,512]{2,1,0:T(8,128)S(1)} %get-tuple-element.33.refs_2_, ...), custom_call_target="tpu_custom_call" | custom-call | tf_op jit(solution)/shard_map/pallas_call | solution.py:402
  45.8 0.8 collective-permute-start.6
  46.6 0.6 collective-permute-start.7
  47.2 1.2 %collective-permute-done.8 = f32[32,1,128]{2,1,0:T(1,128)S(1)} collective-permute-done((f32[32,1,128]{2,1,0:T(1,128)S(1)}, f32[32,1,128]{2,1,0:T(1,128)S(1)}, u32[]{:S(2)}, u32[]{:S(2)}) %collective-permute-start.8) | collective-permute-done | bytes 16416 | tf_op jit(solution)/shard_map/ppermute | solution.py:422
  48.4 12.7 %all_to_all.27.refs_5_ = f32[32,1,128]{2,1,0:T(1,128)S(1)} all-to-all(f32[32,1,128]{2,1,0:T(1,128)S(1)} %collective-permute-done.8), channel_id=1, replica_groups=mesh['panel'=2,'ang'=32,'rad'=4] {'ang'}, dimensions={0} | all-to-all | bytes 32768 | tf_op jit(solution)/shard_map/all_to_all | solution.py:423
  61.1 1.6 %shard_map.115 = (f32[7,24,512]{2,1,0:T(8,128)S(1)}, f32[7,24,512]{2,1,0:T(8,128)S(1)}, f32[32,1,128]{2,1,0:T(1,128)S(1)}) custom-call(f32[1,512]{1,0:T(1,128)S(1)} %get-tuple-element.25.refs_0_, f32[7,24,512]{2,1,0:T(8,128)S(1)} %get-tuple-element.32.refs_1_, f32[7,24,512]{2,1,0:T(8,128)S(1)} %get-tuple-element.33.refs_2_, ...), custom_call_target="tpu_custom_call" | custom-call | tf_op jit(solution)/shard_map/pallas_call | solution.py:402
  62.7 1.3 %collective-permute-start.9 = (f32[7,24,512]{2,1,0:T(8,128)S(1)}, f32[7,24,512]{2,1,0:T(8,128)S(1)}, u32[]{:S(2)}, u32[]{:S(2)}) collective-permute-start(f32[7,24,512]{2,1,0:T(8,128)S(1)} %get-tuple-element.41.refs_7_.refs_11_), channel_id=1, source_target_pairs={{0,1},{1,0},{2,3},{3,2},{4,5},{5,4},{6,7},{7,6},{8,9},{9,8},{10,11... | collective-permute-start | bytes 1032200 | tf_op jit(solution)/shard_map/ppermute | solution.py:419
  64.0 2.2 %collective-permute-start.10 = (f32[7,24,512]{2,1,0:T(8,128)S(1)}, f32[7,24,512]{2,1,0:T(8,128)S(1)}, u32[]{:S(2)}, u32[]{:S(2)}) collective-permute-start(f32[7,24,512]{2,1,0:T(8,128)S(1)} %get-tuple-element.42.refs_8_.refs_12_), channel_id=1, source_target_pairs={{0,3},{1,2},{2,1},{3,0},{4,7},{5,6},{6,5},{7,4},{8,11},{9,10},{10,... | collective-permute-start | bytes 1032200 | tf_op jit(solution)/shard_map/ppermute | solution.py:419
  66.2 1.2 %collective-permute-done.11 = f32[32,1,128]{2,1,0:T(1,128)S(1)} collective-permute-done((f32[32,1,128]{2,1,0:T(1,128)S(1)}, f32[32,1,128]{2,1,0:T(1,128)S(1)}, u32[]{:S(2)}, u32[]{:S(2)}) %collective-permute-start.11) | collective-permute-done | bytes 16416 | tf_op jit(solution)/shard_map/ppermute | solution.py:422
  67.4 12.7 %all_to_all.28.refs_5_ = f32[32,1,128]{2,1,0:T(1,128)S(1)} all-to-all(f32[32,1,128]{2,1,0:T(1,128)S(1)} %collective-permute-done.11), channel_id=1, replica_groups=mesh['panel'=2,'ang'=32,'rad'=4] {'ang'}, dimensions={0} | all-to-all | bytes 32768 | tf_op jit(solution)/shard_map/all_to_all | solution.py:423
  80.1 0.0 collective-permute-done.9.refs_3_
  80.1 1.6 %shard_map.116 = (f32[7,24,512]{2,1,0:T(8,128)S(1)}, f32[7,24,512]{2,1,0:T(8,128)S(1)}, f32[32,1,128]{2,1,0:T(1,128)S(1)}) custom-call(f32[1,512]{1,0:T(1,128)S(1)} %get-tuple-element.25.refs_0_, f32[7,24,512]{2,1,0:T(8,128)S(1)} %get-tuple-element.32.refs_1_, f32[7,24,512]{2,1,0:T(8,128)S(1)} %get-tuple-element.33.refs_2_, ...), custom_call_target="tpu_custom_call" | custom-call | tf_op jit(solution)/shard_map/pallas_call | solution.py:402
  81.7 0.8 collective-permute-start.12
  82.5 0.6 collective-permute-start.13
  83.1 1.2 %collective-permute-done.14 = f32[32,1,128]{2,1,0:T(1,128)S(1)} collective-permute-done((f32[32,1,128]{2,1,0:T(1,128)S(1)}, f32[32,1,128]{2,1,0:T(1,128)S(1)}, u32[]{:S(2)}, u32[]{:S(2)}) %collective-permute-start.14) | collective-permute-done | bytes 16416 | tf_op jit(solution)/shard_map/ppermute | solution.py:422
  84.3 12.7 %all_to_all.29.refs_5_ = f32[32,1,128]{2,1,0:T(1,128)S(1)} all-to-all(f32[32,1,128]{2,1,0:T(1,128)S(1)} %collective-permute-done.14), channel_id=1, replica_groups=mesh['panel'=2,'ang'=32,'rad'=4] {'ang'}, dimensions={0} | all-to-all | bytes 32768 | tf_op jit(solution)/shard_map/all_to_all | solution.py:423
  97.0 1.8 %shard_map.117 = (f32[1,2,16,512]{3,2,1,0:T(8,128)}, f32[1,3,2,16,512]{4,3,2,1,0:T(8,128)}, f32[1,3,2,16,512]{4,3,2,1,0:T(8,128)}) custom-call(f32[1,512]{1,0:T(1,128)S(1)} %get-tuple-element.25.refs_0_, f32[7,24,512]{2,1,0:T(8,128)S(1)} %get-tuple-element.32.refs_1_, f32[7,24,512]{2,1,0:T(8,128)S(1)} %get-tuple-element.33.refs_2_, ...), custom_call_target="tpu_custom_call" | custom-call | tf_op jit(solution)/shard_map/pallas_call | solution.py:402
  (9 shorter events, 0.0 us)
Async XLA Ops:
  2.1 23.4 %collective-permute-start.1 = (f32[8,8,512]{2,1,0:T(8,128)S(1)}, f32[8,8,512]{2,1,0:T(8,128)S(1)}, u32[]{:S(2)}, u32[]{:S(2)}) collective-permute-start(f32[8,8,512]{2,1,0:T(8,128)S(1)} %get-tuple-element.29), channel_id=1, source_target_pairs={{0,4},{4,0},{8,12},{12,8},{16,20},{20,16},{24,28},{28,24},{32,36},... | collective-permute-start | bytes 393224 | tf_op jit(solution)/shard_map/ppermute | solution.py:419
  4.4 21.1 %collective-permute-start.2 = (f32[8,8,512]{2,1,0:T(8,128)S(1)}, f32[8,8,512]{2,1,0:T(8,128)S(1)}, u32[]{:S(2)}, u32[]{:S(2)}) collective-permute-start(f32[8,8,512]{2,1,0:T(8,128)S(1)} %get-tuple-element.30), channel_id=1, source_target_pairs={{0,124},{4,8},{8,4},{12,16},{16,12},{20,24},{24,20},{28,32},{32,28... | collective-permute-start | bytes 393224 | tf_op jit(solution)/shard_map/ppermute | solution.py:419
  4.9 1.2 %collective-permute-start = (f32[32,1,128]{2,1,0:T(1,128)S(1)}, f32[32,1,128]{2,1,0:T(1,128)S(1)}, u32[]{:S(2)}, u32[]{:S(2)}) collective-permute-start(f32[32,1,128]{2,1,0:T(1,128)S(1)} %get-tuple-element.26), channel_id=1, source_target_pairs={{0,128},{128,0},{1,129},{129,1},{2,130},{130,2},{3,131},{131,3},{4... | collective-permute-start | bytes 49160 | tf_op jit(solution)/shard_map/ppermute | solution.py:422
  26.4 17.8 %collective-permute-start.3 = (f32[7,24,512]{2,1,0:T(8,128)S(1)}, f32[7,24,512]{2,1,0:T(8,128)S(1)}, u32[]{:S(2)}, u32[]{:S(2)}) collective-permute-start(f32[7,24,512]{2,1,0:T(8,128)S(1)} %get-tuple-element.32.refs_1_), channel_id=1, source_target_pairs={{0,1},{1,0},{2,3},{3,2},{4,5},{5,4},{6,7},{7,6},{8,9},{9,8},{10,11... | collective-permute-start | bytes 1032200 | tf_op jit(solution)/shard_map/ppermute | solution.py:419
  28.1 16.1 %collective-permute-start.4 = (f32[7,24,512]{2,1,0:T(8,128)S(1)}, f32[7,24,512]{2,1,0:T(8,128)S(1)}, u32[]{:S(2)}, u32[]{:S(2)}) collective-permute-start(f32[7,24,512]{2,1,0:T(8,128)S(1)} %get-tuple-element.33.refs_2_), channel_id=1, source_target_pairs={{0,3},{1,2},{2,1},{3,0},{4,7},{5,6},{6,5},{7,4},{8,11},{9,10},{10,... | collective-permute-start | bytes 1032200 | tf_op jit(solution)/shard_map/ppermute | solution.py:419
  30.3 1.2 %collective-permute-start.5 = (f32[32,1,128]{2,1,0:T(1,128)S(1)}, f32[32,1,128]{2,1,0:T(1,128)S(1)}, u32[]{:S(2)}, u32[]{:S(2)}) collective-permute-start(f32[32,1,128]{2,1,0:T(1,128)S(1)} %get-tuple-element.34), channel_id=1, source_target_pairs={{0,128},{128,0},{1,129},{129,1},{2,130},{130,2},{3,131},{131,3},{4... | collective-permute-start | bytes 49160 | tf_op jit(solution)/shard_map/ppermute | solution.py:422
  45.8 15.3 %collective-permute-start.6 = (f32[7,24,512]{2,1,0:T(8,128)S(1)}, f32[7,24,512]{2,1,0:T(8,128)S(1)}, u32[]{:S(2)}, u32[]{:S(2)}) collective-permute-start(f32[7,24,512]{2,1,0:T(8,128)S(1)} %get-tuple-element.38.refs_7_.refs_9_), channel_id=1, source_target_pairs={{0,1},{1,0},{2,3},{3,2},{4,5},{5,4},{6,7},{7,6},{8,9},{9,8},{10,11... | collective-permute-start | bytes 1032200 | tf_op jit(solution)/shard_map/ppermute | solution.py:419
  46.6 14.5 %collective-permute-start.7 = (f32[7,24,512]{2,1,0:T(8,128)S(1)}, f32[7,24,512]{2,1,0:T(8,128)S(1)}, u32[]{:S(2)}, u32[]{:S(2)}) collective-permute-start(f32[7,24,512]{2,1,0:T(8,128)S(1)} %get-tuple-element.39.refs_8_.refs_10_), channel_id=1, source_target_pairs={{0,3},{1,2},{2,1},{3,0},{4,7},{5,6},{6,5},{7,4},{8,11},{9,10},{10,... | collective-permute-start | bytes 1032200 | tf_op jit(solution)/shard_map/ppermute | solution.py:419
  47.2 1.2 %collective-permute-start.8 = (f32[32,1,128]{2,1,0:T(1,128)S(1)}, f32[32,1,128]{2,1,0:T(1,128)S(1)}, u32[]{:S(2)}, u32[]{:S(2)}) collective-permute-start(f32[32,1,128]{2,1,0:T(1,128)S(1)} %get-tuple-element.40), channel_id=1, source_target_pairs={{0,128},{128,0},{1,129},{129,1},{2,130},{130,2},{3,131},{131,3},{4... | collective-permute-start | bytes 49160 | tf_op jit(solution)/shard_map/ppermute | solution.py:422
  62.7 17.4 %collective-permute-start.9 = (f32[7,24,512]{2,1,0:T(8,128)S(1)}, f32[7,24,512]{2,1,0:T(8,128)S(1)}, u32[]{:S(2)}, u32[]{:S(2)}) collective-permute-start(f32[7,24,512]{2,1,0:T(8,128)S(1)} %get-tuple-element.41.refs_7_.refs_11_), channel_id=1, source_target_pairs={{0,1},{1,0},{2,3},{3,2},{4,5},{5,4},{6,7},{7,6},{8,9},{9,8},{10,11... | collective-permute-start | bytes 1032200 | tf_op jit(solution)/shard_map/ppermute | solution.py:419
  64.0 16.1 %collective-permute-start.10 = (f32[7,24,512]{2,1,0:T(8,128)S(1)}, f32[7,24,512]{2,1,0:T(8,128)S(1)}, u32[]{:S(2)}, u32[]{:S(2)}) collective-permute-start(f32[7,24,512]{2,1,0:T(8,128)S(1)} %get-tuple-element.42.refs_8_.refs_12_), channel_id=1, source_target_pairs={{0,3},{1,2},{2,1},{3,0},{4,7},{5,6},{6,5},{7,4},{8,11},{9,10},{10,... | collective-permute-start | bytes 1032200 | tf_op jit(solution)/shard_map/ppermute | solution.py:419
  66.2 1.2 %collective-permute-start.11 = (f32[32,1,128]{2,1,0:T(1,128)S(1)}, f32[32,1,128]{2,1,0:T(1,128)S(1)}, u32[]{:S(2)}, u32[]{:S(2)}) collective-permute-start(f32[32,1,128]{2,1,0:T(1,128)S(1)} %get-tuple-element.43), channel_id=1, source_target_pairs={{0,128},{128,0},{1,129},{129,1},{2,130},{130,2},{3,131},{131,3},{4... | collective-permute-start | bytes 49160 | tf_op jit(solution)/shard_map/ppermute | solution.py:422
  81.7 15.3 %collective-permute-start.12 = (f32[7,24,512]{2,1,0:T(8,128)S(1)}, f32[7,24,512]{2,1,0:T(8,128)S(1)}, u32[]{:S(2)}, u32[]{:S(2)}) collective-permute-start(f32[7,24,512]{2,1,0:T(8,128)S(1)} %get-tuple-element.44.refs_7_), channel_id=1, source_target_pairs={{0,1},{1,0},{2,3},{3,2},{4,5},{5,4},{6,7},{7,6},{8,9},{9,8},{10,11... | collective-permute-start | bytes 1032200 | tf_op jit(solution)/shard_map/ppermute | solution.py:419
  82.5 14.5 %collective-permute-start.13 = (f32[7,24,512]{2,1,0:T(8,128)S(1)}, f32[7,24,512]{2,1,0:T(8,128)S(1)}, u32[]{:S(2)}, u32[]{:S(2)}) collective-permute-start(f32[7,24,512]{2,1,0:T(8,128)S(1)} %get-tuple-element.45.refs_8_), channel_id=1, source_target_pairs={{0,3},{1,2},{2,1},{3,0},{4,7},{5,6},{6,5},{7,4},{8,11},{9,10},{10,... | collective-permute-start | bytes 1032200 | tf_op jit(solution)/shard_map/ppermute | solution.py:419
  83.1 1.2 %collective-permute-start.14 = (f32[32,1,128]{2,1,0:T(1,128)S(1)}, f32[32,1,128]{2,1,0:T(1,128)S(1)}, u32[]{:S(2)}, u32[]{:S(2)}) collective-permute-start(f32[32,1,128]{2,1,0:T(1,128)S(1)} %get-tuple-element.46), channel_id=1, source_target_pairs={{0,128},{128,0},{1,129},{129,1},{2,130},{130,2},{3,131},{131,3},{4... | collective-permute-start | bytes 49160 | tf_op jit(solution)/shard_map/ppermute | solution.py:422
